TPU v7x, 32 devices: a whole 2x2x4 slice. The times are simulated.
32 devices in a mesh: dp: 2 (over y), row: 4 (over z), col: 4 (over x, core).
Axes of the slice: x: 2, y: 2, z: 4, core: 2. Of those that a mesh axis runs over, the one named last changes fastest.
Arguments:
- tokens_in: bfloat16 [2, 4096, 1024], P(None, ('dp', 'row'), 'col'), may hold values from -6 to 6
- segments: int32 [2, 2, 2048], P(None, 'dp'), may hold values from 0 to 31, never falling along the last dimension, each value on 1 to 1024 neighbouring positions
- gain_attn: float32 [1024], P('col'), may hold values from 0.25 to 1.75
- gain_ffn: float32 [1024], P('col'), may hold values from 0.25 to 1.75
- w_heads: bfloat16 [1024, 160], P('col', 'row'), may hold values from -0.4375 to 0.4375
- w_ranks: bfloat16 [1024, 640], P('col', 'row'), may hold values from -0.1875 to 0.1875
- w_out: bfloat16 [1024, 1024], P('row', 'col'), may hold values from -0.75 to 0.75
- w_gate: bfloat16 [1024, 2816], P('col', 'row'), may hold values from -0.1875 to 0.1875
- w_up: bfloat16 [1024, 2816], P('col', 'row'), may hold values from -0.1875 to 0.1875
- w_down: bfloat16 [2816, 1024], P('row', 'col'), may hold values from -0.21875 to 0.21875
- cotangent: bfloat16 [2, 4096, 1024], P(None, ('dp', 'row'), 'col'), may hold values from -6 to 6
Outputs:
- output: bfloat16 [2, 4096, 1024], P(None, ('dp', 'row'), 'col')
- grad_input: float32 [2, 4096, 1024], P(None, ('dp', 'row'), 'col')
- grad_gain_attn: float32 [1024], P('col')
- grad_gain_ffn: float32 [1024], P('col')
- grad_w_heads: float32 [1024, 160], P('col', 'row')
- grad_w_ranks: float32 [1024, 640], P('col', 'row')
- grad_w_out: float32 [1024, 1024], P('row', 'col')
- grad_w_gate: float32 [1024, 2816], P('col', 'row')
- grad_w_up: float32 [1024, 2816], P('col', 'row')
- grad_w_down: float32 [2816, 1024], P('row', 'col')
Inputs may be any that keep to these rules, and one draw needn't show every extreme that they name: `segments`: document numbers count from 0 within each sequence of 2048 tokens, never fall, and a document holds 1 to 1024 tokens.
All inputs are finite; a program needn't handle non-finite values.
Results may differ from a plain program's by a relative error of at most 0.019.
The roundings to bfloat16 on the way count: a program that leaves them out, or rounds other values in their place, can miss the bound.
Values may be sent and summed in bfloat16 or wider, within the bound.
A program may use at most 128 MiB of HBM per device.

v0:
```python
import jax
import jax.numpy as jnp
from jax import lax
from jax.sharding import PartitionSpec as P

D = 1024
HD = 64
RQ = 6
RK = 2


norm_eps = 1e-06
rope_base = 10000.0
masked_score = -1e30
highest = lax.Precision.HIGHEST


def rotate(values, places, direction):
    half_size = values.shape[-1] // 2
    inverse = rope_base ** (-(jnp.arange(half_size, dtype=jnp.float32) * 2.0 / values.shape[-1]))
    angles = places.astype(jnp.float32)[:, None] * inverse[None, :]
    cosine = jnp.cos(angles)[:, None, :]
    sine_term = direction * jnp.sin(angles)[:, None, :]
    first_half = values[..., :half_size]
    second_half = values[..., half_size:]
    return jnp.concatenate(
        [
            first_half * cosine - second_half * sine_term,
            second_half * cosine + first_half * sine_term,
        ],
        axis=-1,
    )


def doc_places(segment_row):
    seq_len = segment_row.shape[0]
    index_all = jnp.arange(seq_len, dtype=jnp.int32)
    change = jnp.concatenate([jnp.ones((1,), jnp.bool_), segment_row[1:] != segment_row[:-1]])
    starts = lax.cummax(jnp.where(change, index_all, 0), axis=0)
    return index_all - starts


def row_gather(values):
    return lax.all_gather(values, "row", axis=0, tiled=True)


def col_gather(values):
    return lax.all_gather(values, "col", axis=0, tiled=True)


def col_reduce(term_fn, total_rows):
    return lax.psum_scatter(
        term_fn(jnp.int32(0), total_rows // lax.axis_size("col") * lax.axis_size("col")),
        "col",
        scatter_dimension=0,
        tiled=True,
    )


def row_reduce(term_fn, total_rows):
    return lax.psum_scatter(
        term_fn(jnp.int32(0), total_rows // lax.axis_size("row") * lax.axis_size("row")),
        "row",
        scatter_dimension=0,
        tiled=True,
    )


def col_total(values):
    return lax.psum(values, "col")


def sliced_product(left, right):

    def term_rows(offset, count):
        return jnp.dot(left, right, preferred_element_type=jnp.float32)

    return term_rows


def norm_forward(values, gain):
    squares = col_total(jnp.sum(values * values, axis=1))
    scaling = lax.rsqrt(squares / D + norm_eps)
    normed = values * scaling[:, None]
    return ((normed * gain).astype(jnp.bfloat16), normed, scaling)


def norm_backward(grad_in, normed, scaling, gain):
    gain_part = jnp.sum(grad_in * normed, axis=0)
    inner = grad_in * gain
    totals = col_total(jnp.sum(inner * normed, axis=1))
    return (scaling[:, None] * (inner - normed * (totals / D)[:, None]), gain_part)


def tile_mask(query_seg, query_idx, key_seg, key_idx, offset, tile_rows):
    seg_tile = lax.dynamic_slice_in_dim(key_seg, offset, tile_rows, 0)
    idx_tile = lax.dynamic_slice_in_dim(key_idx, offset, tile_rows, 0)
    return (query_seg[:, None] == seg_tile[None, :]) & (idx_tile[None, :] <= query_idx[:, None])


def tile_scores(queries, key_all, offset, tile_rows, scaling):
    key_tile = lax.dynamic_slice_in_dim(key_all, offset, tile_rows, 1)
    return (
        jnp.einsum("hqd,hkd->hqk", queries, key_tile, preferred_element_type=jnp.float32) * scaling
    )


def attend_forward(queries, key_all, value_all, query_seg, query_idx, key_seg, key_idx):
    head_count, row_count, head_size = queries.shape
    seq_len = key_all.shape[1]
    tile_rows = min(512, seq_len)
    scaling = head_size ** (-0.5)

    def stat_step(counter, carried):
        offset = counter * tile_rows
        allowed = tile_mask(query_seg, query_idx, key_seg, key_idx, offset, tile_rows)

        def stat_when_live(current):
            row_peak, row_total = current
            scores = jnp.where(
                allowed[None],
                tile_scores(queries, key_all, offset, tile_rows, scaling),
                masked_score,
            )
            new_peak = jnp.maximum(row_peak, jnp.max(scores, axis=-1))
            weights = jnp.where(allowed[None], jnp.exp(scores - new_peak[..., None]), 0.0)
            return (new_peak, row_total * jnp.exp(row_peak - new_peak) + jnp.sum(weights, axis=-1))

        return lax.cond(jnp.any(allowed), stat_when_live, lambda current: current, carried)

    initial = (
        jnp.full((head_count, row_count), masked_score, jnp.float32),
        jnp.zeros((head_count, row_count), jnp.float32),
    )
    row_peak, row_total = lax.fori_loop(0, seq_len // tile_rows, stat_step, initial)
    logsum = row_peak + jnp.log(row_total)

    def out_step(counter, summed):
        offset = counter * tile_rows
        allowed = tile_mask(query_seg, query_idx, key_seg, key_idx, offset, tile_rows)

        def out_when_live(current):
            scores = tile_scores(queries, key_all, offset, tile_rows, scaling)
            prob_tile = jnp.where(allowed[None], jnp.exp(scores - logsum[..., None]), 0.0).astype(
                jnp.bfloat16
            )
            value_tile = lax.dynamic_slice_in_dim(value_all, offset, tile_rows, 1)
            return current + jnp.einsum(
                "hqk,hkd->hqd", prob_tile, value_tile, preferred_element_type=jnp.float32
            )

        return lax.cond(jnp.any(allowed), out_when_live, lambda current: current, summed)

    attended = lax.fori_loop(
        0,
        seq_len // tile_rows,
        out_step,
        jnp.zeros((head_count, row_count, head_size), jnp.float32),
    )
    return (attended, logsum)


def attend_backward(
    queries, key_all, value_all, grad_out, logsum, query_seg, query_idx, key_seg, key_idx
):
    head_count, row_count, head_size = queries.shape
    seq_len = key_all.shape[1]
    tile_rows = min(512, seq_len)
    scaling = head_size ** (-0.5)

    def tile_terms(offset, allowed):
        scores = tile_scores(queries, key_all, offset, tile_rows, scaling)
        prob_tile = jnp.where(allowed[None], jnp.exp(scores - logsum[..., None]), 0.0)
        value_tile = lax.dynamic_slice_in_dim(value_all, offset, tile_rows, 1)
        dprob = jnp.einsum("hqd,hkd->hqk", grad_out, value_tile, preferred_element_type=jnp.float32)
        return (prob_tile, dprob)

    def delta_step(counter, summed):
        offset = counter * tile_rows
        allowed = tile_mask(query_seg, query_idx, key_seg, key_idx, offset, tile_rows)

        def delta_when_live(current):
            prob_tile, dprob = tile_terms(offset, allowed)
            return current + jnp.sum(prob_tile * dprob, axis=-1)

        return lax.cond(jnp.any(allowed), delta_when_live, lambda current: current, summed)

    delta = lax.fori_loop(
        0, seq_len // tile_rows, delta_step, jnp.zeros((head_count, row_count), jnp.float32)
    )

    def grad_step(counter, carried):
        offset = counter * tile_rows
        allowed = tile_mask(query_seg, query_idx, key_seg, key_idx, offset, tile_rows)

        def grad_when_live(current):
            grad_q, grad_k, grad_v = current
            prob_tile, dprob = tile_terms(offset, allowed)
            dscore = (prob_tile * (dprob - delta[..., None])).astype(jnp.bfloat16)
            key_tile = lax.dynamic_slice_in_dim(key_all, offset, tile_rows, 1)
            grad_q = (
                grad_q
                + jnp.einsum("hqk,hkd->hqd", dscore, key_tile, preferred_element_type=jnp.float32)
                * scaling
            )
            key_part = (
                jnp.einsum("hqk,hqd->hkd", dscore, queries, preferred_element_type=jnp.float32)
                * scaling
            )
            value_part = jnp.einsum(
                "hqk,hqd->hkd",
                prob_tile.astype(jnp.bfloat16),
                grad_out,
                preferred_element_type=jnp.float32,
            )
            grad_k = lax.dynamic_update_slice_in_dim(grad_k, key_part, offset, 1)
            grad_v = lax.dynamic_update_slice_in_dim(grad_v, value_part, offset, 1)
            return (grad_q, grad_k, grad_v)

        return lax.cond(jnp.any(allowed), grad_when_live, lambda current: current, carried)

    initial = (
        jnp.zeros((head_count, row_count, head_size), jnp.float32),
        jnp.zeros((head_count, seq_len, head_size), jnp.float32),
        jnp.zeros((head_count, seq_len, head_size), jnp.float32),
    )
    return lax.fori_loop(0, seq_len // tile_rows, grad_step, initial)


def local(
    tokens_in,
    segments,
    gain_attn,
    gain_ffn,
    w_heads,
    w_ranks,
    w_out,
    w_gate,
    w_up,
    w_down,
    cotangent,
):
    row_size = lax.axis_size("row")
    col_size = lax.axis_size("col")
    col_place = lax.axis_index("col")
    seq_len = tokens_in.shape[1] * row_size
    query_rows = seq_len // col_size
    fac_count = RQ + 2 * RK
    head_cols = w_heads.shape[1]
    head_local = head_cols // fac_count
    ffn_local = w_gate.shape[1]
    w_factor = jnp.concatenate([w_heads, w_ranks], axis=1)
    w_both = jnp.concatenate([w_gate, w_up], axis=1)

    def micro_step(carried, inputs):
        factor_acc, out_acc, both_acc, down_acc, gain_one_acc, gain_two_acc = carried
        tokens_mb, segment_mb, cot_mb = inputs
        residual = tokens_mb.astype(jnp.float32)
        segment_row = segment_mb[0]
        index_all = jnp.arange(seq_len, dtype=jnp.int32)
        own_start = col_place * query_rows
        query_seg = lax.dynamic_slice_in_dim(segment_row, own_start, query_rows, 0)
        query_idx = lax.dynamic_slice_in_dim(index_all, own_start, query_rows, 0)
        query_places = lax.dynamic_slice_in_dim(doc_places(segment_row), own_start, query_rows, 0)
        h_one, normed_one, scale_one = norm_forward(residual, gain_attn)
        h_one_all = row_gather(h_one)
        factors = col_reduce(sliced_product(h_one_all, w_factor), seq_len)
        head_part = factors[:, :head_cols].reshape(query_rows, head_local, fac_count)
        rank_all = lax.all_gather(factors[:, head_cols:], "row", axis=1, tiled=True).reshape(
            query_rows, fac_count, HD
        )
        a_q = head_part[..., :RQ]
        ak_low = head_part[..., RQ : RQ + RK].astype(jnp.bfloat16)
        av_low = head_part[..., RQ + RK :].astype(jnp.bfloat16)
        bq_rot = rotate(rank_all[:, :RQ], query_places, 1.0)
        bk_rot = rotate(rank_all[:, RQ : RQ + RK], query_places, 1.0).astype(jnp.bfloat16)
        bv_low = rank_all[:, RQ + RK :].astype(jnp.bfloat16)
        queries = (jnp.einsum("thr,tre->hte", a_q, bq_rot, precision=highest) / RQ).astype(
            jnp.bfloat16
        )
        head_send = jnp.concatenate([ak_low, av_low], axis=2).reshape(
            query_rows, head_local * 2 * RK
        )
        rank_send = jnp.concatenate([bk_rot, bv_low], axis=1).reshape(query_rows, 2 * RK * HD)
        key_heads, key_ranks = (
            lax.all_gather(head_send, "col", axis=0, tiled=True),
            lax.all_gather(rank_send, "col", axis=0, tiled=True),
        )
        key_heads = key_heads.reshape(seq_len, head_local, 2 * RK).astype(jnp.float32)
        key_ranks = key_ranks.reshape(seq_len, 2 * RK, HD).astype(jnp.float32)
        key_all = (
            jnp.einsum("thr,tre->hte", key_heads[..., :RK], key_ranks[:, :RK], precision=highest)
            / RK
        ).astype(jnp.bfloat16)
        value_all = (
            jnp.einsum("thr,tre->hte", key_heads[..., RK:], key_ranks[:, RK:], precision=highest)
            / RK
        ).astype(jnp.bfloat16)
        attended, logsum = attend_forward(
            queries, key_all, value_all, query_seg, query_idx, segment_row, index_all
        )
        heads_out = (
            attended.transpose(1, 0, 2).reshape(query_rows, head_local * HD).astype(jnp.bfloat16)
        )
        heads_all = col_gather(heads_out)
        mixed = residual + row_reduce(sliced_product(heads_all, w_out), seq_len)
        h_two, normed_two, scale_two = norm_forward(mixed, gain_ffn)
        h_two_all = row_gather(h_two)
        gate_up = col_reduce(sliced_product(h_two_all, w_both), seq_len)
        gate = gate_up[:, :ffn_local]
        up_vals = gate_up[:, ffn_local:]
        sigmoid_gate = jax.nn.sigmoid(gate)
        silu_gate = gate * sigmoid_gate
        hidden = (silu_gate * up_vals).astype(jnp.bfloat16)
        hidden_all = col_gather(hidden)
        ffn_out = row_reduce(sliced_product(hidden_all, w_down), seq_len)
        output_mb = (mixed + ffn_out).astype(jnp.bfloat16)
        cot_all = row_gather(cot_mb)
        grad_hidden = col_reduce(sliced_product(cot_all, w_down.T), seq_len)
        down_acc = down_acc + jnp.dot(hidden_all.T, cot_all, preferred_element_type=jnp.float32)
        grad_gate = grad_hidden * up_vals * sigmoid_gate * (1.0 + gate * (1.0 - sigmoid_gate))
        grad_up = grad_hidden * silu_gate
        grad_both = jnp.concatenate([grad_gate, grad_up], axis=1).astype(jnp.bfloat16)
        grad_both_all = col_gather(grad_both)
        grad_h_two = row_reduce(sliced_product(grad_both_all, w_both.T), seq_len)
        both_acc = both_acc + jnp.dot(
            h_two_all.T, grad_both_all, preferred_element_type=jnp.float32
        )
        grad_norm_two, gain_two_part = norm_backward(grad_h_two, normed_two, scale_two, gain_ffn)
        grad_mixed = cot_mb.astype(jnp.float32) + grad_norm_two
        grad_attn_all = row_gather(grad_mixed.astype(jnp.bfloat16))
        out_acc = out_acc + jnp.dot(heads_all.T, grad_attn_all, preferred_element_type=jnp.float32)
        grad_heads = col_reduce(sliced_product(grad_attn_all, w_out.T), seq_len)
        grad_heads = (
            grad_heads.astype(jnp.bfloat16).reshape(query_rows, head_local, HD).transpose(1, 0, 2)
        )
        grad_q, grad_k, grad_v = attend_backward(
            queries,
            key_all,
            value_all,
            grad_heads,
            logsum,
            query_seg,
            query_idx,
            segment_row,
            index_all,
        )
        grad_aq = jnp.einsum("hte,tre->thr", grad_q, bq_rot, precision=highest) / RQ
        grad_bq = jnp.einsum("thr,hte->tre", a_q, grad_q, precision=highest) / RQ
        grad_ak = jnp.einsum("hte,tre->thr", grad_k, key_ranks[:, :RK], precision=highest) / RK
        grad_bk = jnp.einsum("thr,hte->tre", key_heads[..., :RK], grad_k, precision=highest) / RK
        grad_av = jnp.einsum("hte,tre->thr", grad_v, key_ranks[:, RK:], precision=highest) / RK
        grad_bv = jnp.einsum("thr,hte->tre", key_heads[..., RK:], grad_v, precision=highest) / RK
        key_head_grads = jnp.concatenate([grad_ak, grad_av], axis=2).reshape(
            seq_len, head_local * 2 * RK
        )
        key_rank_grads = jnp.concatenate([grad_bk, grad_bv], axis=1).reshape(seq_len, 2 * RK * HD)
        own_heads, own_ranks = (
            lax.psum_scatter(
                key_head_grads.astype(jnp.bfloat16), "col", scatter_dimension=0, tiled=True
            ).astype(jnp.float32),
            lax.psum_scatter(
                key_rank_grads.astype(jnp.bfloat16), "col", scatter_dimension=0, tiled=True
            ).astype(jnp.float32),
        )
        own_heads = own_heads.reshape(query_rows, head_local, 2 * RK)
        own_ranks = own_ranks.reshape(query_rows, 2 * RK, HD)
        head_grads = jnp.concatenate([grad_aq, own_heads], axis=2).reshape(query_rows, head_cols)
        rank_grads_full = jnp.concatenate(
            [
                rotate(grad_bq, query_places, -1.0),
                rotate(own_ranks[:, :RK], query_places, -1.0),
                own_ranks[:, RK:],
            ],
            axis=1,
        ).reshape(query_rows, fac_count * HD)
        own_rank_grads = lax.psum_scatter(
            rank_grads_full.astype(jnp.bfloat16), "row", scatter_dimension=1, tiled=True
        ).astype(jnp.float32)
        grad_factors = jnp.concatenate([head_grads, own_rank_grads], axis=1).astype(jnp.bfloat16)
        grad_factors_all = col_gather(grad_factors)
        factor_acc = factor_acc + jnp.dot(
            h_one_all.T, grad_factors_all, preferred_element_type=jnp.float32
        )
        grad_h_one = row_reduce(sliced_product(grad_factors_all, w_factor.T), seq_len)
        grad_norm_one, gain_one_part = norm_backward(grad_h_one, normed_one, scale_one, gain_attn)
        grad_input_mb = grad_mixed + grad_norm_one
        updated = (
            factor_acc,
            out_acc,
            both_acc,
            down_acc,
            gain_one_acc + gain_one_part,
            gain_two_acc + gain_two_part,
        )
        return (updated, (output_mb, grad_input_mb))

    model_local = w_heads.shape[0]
    both_init = jnp.zeros((model_local, 2 * ffn_local), jnp.float32)
    down_init = jnp.zeros((ffn_local, model_local), jnp.float32)
    initial = (
        jnp.zeros(w_factor.shape, jnp.float32),
        jnp.zeros(w_out.shape, jnp.float32),
        both_init,
        down_init,
        jnp.zeros(gain_attn.shape, jnp.float32),
        jnp.zeros(gain_ffn.shape, jnp.float32),
    )
    finals, stacked = lax.scan(micro_step, initial, (tokens_in, segments, cotangent))
    factor_acc, out_acc, both_acc, down_acc, gain_one_acc, gain_two_acc = finals
    factor_sum, out_sum, both_sum, down_sum = (
        lax.psum(factor_acc.astype(jnp.bfloat16), "dp").astype(jnp.float32),
        lax.psum(out_acc.astype(jnp.bfloat16), "dp").astype(jnp.float32),
        lax.psum(both_acc.astype(jnp.bfloat16), "dp").astype(jnp.float32),
        lax.psum(down_acc.astype(jnp.bfloat16), "dp").astype(jnp.float32),
    )
    gain_one, gain_two = lax.psum((gain_one_acc, gain_two_acc), ("dp", "row"))
    return (
        stacked[0],
        stacked[1],
        gain_one,
        gain_two,
        factor_sum[:, :head_cols],
        factor_sum[:, head_cols:],
        out_sum,
        both_sum[:, :ffn_local],
        both_sum[:, ffn_local:],
        down_sum,
    )


def solution(mesh):
    placed = (
        P(None, ("dp", "row"), "col"),
        P(None, "dp", None),
        P("col"),
        P("col"),
        P("col", "row"),
        P("col", "row"),
        P("row", "col"),
        P("col", "row"),
        P("col", "row"),
        P("row", "col"),
        P(None, ("dp", "row"), "col"),
    )
    return jax.shard_map(
        local,
        mesh=mesh,
        in_specs=placed,
        out_specs=(
            P(None, ("dp", "row"), "col"),
            P(None, ("dp", "row"), "col"),
            P("col"),
            P("col"),
            P("col", "row"),
            P("col", "row"),
            P("row", "col"),
            P("col", "row"),
            P("col", "row"),
            P("row", "col"),
        ),
        check_vma=False,
    )
```

profile of v0, /device:TPU:0, one launch (start us, length us, event | category | flops | bytes accessed | tf_op | source)
XLA Modules:
  0.0 1919.7 jit_solution(9061966944448397454)
XLA Ops:
  13.5 1838.8 %while.148 = (s32[]{:T(128)}, f32[256,200]{0,1:T(8,128)}, f32[256,256]{1,0:T(8,128)}, f32[256,1408]{1,0:T(8,128)}, f32[704,256]{1,0:T(8,128)}, /*index=5*/f32[25...) while((s32[]{:T(128)}, f32[256,200]{0,1:T(8,128)}, ...), condition=%wide.region_47.48_spmd.clone, body=%wide.region_0.47_spmd.clone.sunk | while | flops 9566044160 | bytes 434714816 | solution.py:409
  24.3 28.4 %all-gather.14.cloned.1.call-done = bf16[2048,256]{1,0:T(8,128)(2,1)} async-done(((bf16[512,256]{1,0:T(8,128)(2,1)}), bf16[2048,256]{1,0:T(8,128)(2,1)}) %all-gather.14.cloned.1.call-update) | async-done | bytes 1048592 | tf_op jit(solution)/shard_map/while/body/eval_jaxpr/all_gather | solution.py:44
  55.6 28.2 %reduce-scatter.12.cloned.1.call-done = f32[512,200]{0,1:T(8,128)} async-done(((f32[2048,200]{0,1:T(8,128)}), f32[512,200]{0,1:T(8,128)}) %reduce-scatter.12.cloned.1.call-update) | async-done | bytes 409616 | tf_op jit(solution)/shard_map/while/body/eval_jaxpr/reduce_scatter | solution.py:52
  87.6 31.1 %all-gather.16.cloned.1.call-done = f32[512,640]{0,1:T(8,128)} async-done(((f32[512,160]{0,1:T(8,128)}), f32[512,640]{0,1:T(8,128)}) %all-gather.16.cloned.1.call-update) | async-done | bytes 1310736 | tf_op jit(solution)/shard_map/while/body/eval_jaxpr/all_gather | solution.py:269
  181.8 12.1 while.150
  194.8 24.0 %all-gather.22.cloned.1.call-done = bf16[2048,256]{0,1:T(8,128)(2,1)} async-done(((bf16[512,256]{0,1:T(8,128)(2,1)}), bf16[2048,256]{0,1:T(8,128)(2,1)}) %all-gather.22.cloned.1.call-update) | async-done | bytes 1048592 | tf_op jit(solution)/shard_map/while/body/eval_jaxpr/all_gather | solution.py:48
  222.8 43.2 %reduce-scatter.16.cloned.1.call-done = f32[512,256]{1,0:T(8,128)} async-done(((f32[2048,256]{1,0:T(8,128)}), f32[512,256]{1,0:T(8,128)}) %reduce-scatter.16.cloned.1.call-update) | async-done | bytes 524304 | tf_op jit(solution)/shard_map/while/body/eval_jaxpr/reduce_scatter | solution.py:61
  274.6 20.9 %all-gather.20.cloned.1.call-done = bf16[1,2048,256]{2,1,0:T(8,128)(2,1)} async-done(((bf16[1,512,256]{2,1,0:T(8,128)(2,1)}), bf16[1,2048,256]{2,1,0:T(8,128)(2,1)}) %all-gather.20.cloned.1.call-update) | async-done | bytes 1048592 | tf_op jit(solution)/shard_map/while/body/eval_jaxpr/all_gather | solution.py:44
  300.2 24.4 %all-gather.24.cloned.1.call-done = bf16[2048,256]{1,0:T(8,128)(2,1)} async-done(((bf16[512,256]{1,0:T(8,128)(2,1)}), bf16[2048,256]{1,0:T(8,128)(2,1)}) %all-gather.24.cloned.1.call-update) | async-done | bytes 1048592 | tf_op jit(solution)/shard_map/while/body/eval_jaxpr/all_gather | solution.py:44
  332.1 49.6 %reduce-scatter.14.cloned.1.call-done = f32[512,704]{0,1:T(8,128)} async-done(((f32[2048,704]{0,1:T(8,128)}), f32[512,704]{0,1:T(8,128)}) %reduce-scatter.14.cloned.1.call-update) | async-done | bytes 1441808 | tf_op jit(solution)/shard_map/while/body/eval_jaxpr/reduce_scatter | solution.py:52
  381.7 94.7 %reduce-scatter.18.cloned.1.call-done = f32[512,1408]{0,1:T(8,128)} async-done(((f32[2048,1408]{0,1:T(8,128)}), f32[512,1408]{0,1:T(8,128)}) %reduce-scatter.18.cloned.1.call-update) | async-done | bytes 2883600 | tf_op jit(solution)/shard_map/while/body/eval_jaxpr/reduce_scatter | solution.py:52
  481.8 43.5 %all-gather.26.cloned.1.call-done = bf16[2048,1408]{0,1:T(8,128)(2,1)} async-done(((bf16[512,1408]{0,1:T(8,128)(2,1)}), bf16[2048,1408]{0,1:T(8,128)(2,1)}) %all-gather.26.cloned.1.call-update) | async-done | bytes 5767184 | tf_op jit(solution)/shard_map/while/body/eval_jaxpr/all_gather | solution.py:48
  531.4 44.0 %reduce-scatter.20.cloned.1.call-done = f32[512,256]{1,0:T(8,128)} async-done(((f32[2048,256]{1,0:T(8,128)}), f32[512,256]{1,0:T(8,128)}) %reduce-scatter.20.cloned.1.call-update) | async-done | bytes 524304 | tf_op jit(solution)/shard_map/while/body/eval_jaxpr/reduce_scatter | solution.py:61
  585.7 26.9 %all-gather.28.cloned.1.call-done = bf16[2048,256]{1,0:T(8,128)(2,1)} async-done(((bf16[512,256]{1,0:T(8,128)(2,1)}), bf16[2048,256]{1,0:T(8,128)(2,1)}) %all-gather.28.cloned.1.call-update) | async-done | bytes 1048592 | tf_op jit(solution)/shard_map/while/body/eval_jaxpr/all_gather | solution.py:44
  615.7 31.0 %reduce-scatter.22.cloned.1.call-done = f32[512,256]{1,0:T(8,128)} async-done(((f32[2048,256]{1,0:T(8,128)}), f32[512,256]{1,0:T(8,128)}) %reduce-scatter.22.cloned.1.call-update) | async-done | bytes 524304 | tf_op jit(solution)/shard_map/while/body/eval_jaxpr/reduce_scatter | solution.py:52
  648.0 10.3 while.151
  661.5 14.9 while.152
  743.0 14.9 reduce-scatter.24.cloned.1.call-done
  760.8 26.2 %all-gather.30.cloned.1.call-done = bf16[2048,704]{0,1:T(8,128)(2,1)} async-done(((bf16[512,704]{0,1:T(8,128)(2,1)}), bf16[2048,704]{0,1:T(8,128)(2,1)}) %all-gather.30.cloned.1.call-update) | async-done | bytes 2883600 | tf_op jit(solution)/shard_map/while/body/eval_jaxpr/all_gather | solution.py:48
  798.7 10.2 reduce-scatter.28.cloned.1.call-done
  811.1 22.1 %reduce-scatter.26.cloned.1.call-done = bf16[512,160]{0,1:T(8,128)(2,1)} async-done(((bf16[512,640]{0,1:T(8,128)(2,1)}), bf16[512,160]{0,1:T(8,128)(2,1)}) %reduce-scatter.26.cloned.1.call-update) | async-done | bytes 163856 | tf_op jit(solution)/shard_map/while/body/eval_jaxpr/reduce_scatter | solution.py:377
  848.9 29.4 %reduce-scatter.32.cloned.1.call-done = f32[512,256]{1,0:T(8,128)} async-done(((f32[2048,256]{1,0:T(8,128)}), f32[512,256]{1,0:T(8,128)}) %reduce-scatter.32.cloned.1.call-update) | async-done | bytes 524304 | tf_op jit(solution)/shard_map/while/body/eval_jaxpr/reduce_scatter | solution.py:61
  887.9 35.9 %reduce-scatter.30.cloned.1.call-done = f32[512,256]{1,0:T(8,128)} async-done(((f32[2048,256]{1,0:T(8,128)}), f32[512,256]{1,0:T(8,128)}) %reduce-scatter.30.cloned.1.call-update) | async-done | bytes 524304 | tf_op jit(solution)/shard_map/while/body/eval_jaxpr/reduce_scatter | solution.py:61
  942.5 27.0 %all-gather.14.cloned.1.call-done = bf16[2048,256]{1,0:T(8,128)(2,1)} async-done(((bf16[512,256]{1,0:T(8,128)(2,1)}), bf16[2048,256]{1,0:T(8,128)(2,1)}) %all-gather.14.cloned.1.call-update) | async-done | bytes 1048592 | tf_op jit(solution)/shard_map/while/body/eval_jaxpr/all_gather | solution.py:44
  972.5 28.2 %reduce-scatter.12.cloned.1.call-done = f32[512,200]{0,1:T(8,128)} async-done(((f32[2048,200]{0,1:T(8,128)}), f32[512,200]{0,1:T(8,128)}) %reduce-scatter.12.cloned.1.call-update) | async-done | bytes 409616 | tf_op jit(solution)/shard_map/while/body/eval_jaxpr/reduce_scatter | solution.py:52
  1004.4 31.1 %all-gather.16.cloned.1.call-done = f32[512,640]{0,1:T(8,128)} async-done(((f32[512,160]{0,1:T(8,128)}), f32[512,640]{0,1:T(8,128)}) %all-gather.16.cloned.1.call-update) | async-done | bytes 1310736 | tf_op jit(solution)/shard_map/while/body/eval_jaxpr/all_gather | solution.py:269
  1087.3 10.1 while.149
  1098.7 12.1 while.150
  1111.7 24.0 %all-gather.22.cloned.1.call-done = bf16[2048,256]{0,1:T(8,128)(2,1)} async-done(((bf16[512,256]{0,1:T(8,128)(2,1)}), bf16[2048,256]{0,1:T(8,128)(2,1)}) %all-gather.22.cloned.1.call-update) | async-done | bytes 1048592 | tf_op jit(solution)/shard_map/while/body/eval_jaxpr/all_gather | solution.py:48
  1139.7 43.2 %reduce-scatter.16.cloned.1.call-done = f32[512,256]{1,0:T(8,128)} async-done(((f32[2048,256]{1,0:T(8,128)}), f32[512,256]{1,0:T(8,128)}) %reduce-scatter.16.cloned.1.call-update) | async-done | bytes 524304 | tf_op jit(solution)/shard_map/while/body/eval_jaxpr/reduce_scatter | solution.py:61
  1191.5 20.8 %all-gather.20.cloned.1.call-done = bf16[1,2048,256]{2,1,0:T(8,128)(2,1)} async-done(((bf16[1,512,256]{2,1,0:T(8,128)(2,1)}), bf16[1,2048,256]{2,1,0:T(8,128)(2,1)}) %all-gather.20.cloned.1.call-update) | async-done | bytes 1048592 | tf_op jit(solution)/shard_map/while/body/eval_jaxpr/all_gather | solution.py:44
  1216.9 24.4 %all-gather.24.cloned.1.call-done = bf16[2048,256]{1,0:T(8,128)(2,1)} async-done(((bf16[512,256]{1,0:T(8,128)(2,1)}), bf16[2048,256]{1,0:T(8,128)(2,1)}) %all-gather.24.cloned.1.call-update) | async-done | bytes 1048592 | tf_op jit(solution)/shard_map/while/body/eval_jaxpr/all_gather | solution.py:44
  1248.8 49.6 %reduce-scatter.14.cloned.1.call-done = f32[512,704]{0,1:T(8,128)} async-done(((f32[2048,704]{0,1:T(8,128)}), f32[512,704]{0,1:T(8,128)}) %reduce-scatter.14.cloned.1.call-update) | async-done | bytes 1441808 | tf_op jit(solution)/shard_map/while/body/eval_jaxpr/reduce_scatter | solution.py:52
  1298.4 94.7 %reduce-scatter.18.cloned.1.call-done = f32[512,1408]{0,1:T(8,128)} async-done(((f32[2048,1408]{0,1:T(8,128)}), f32[512,1408]{0,1:T(8,128)}) %reduce-scatter.18.cloned.1.call-update) | async-done | bytes 2883600 | tf_op jit(solution)/shard_map/while/body/eval_jaxpr/reduce_scatter | solution.py:52
  1398.5 43.5 %all-gather.26.cloned.1.call-done = bf16[2048,1408]{0,1:T(8,128)(2,1)} async-done(((bf16[512,1408]{0,1:T(8,128)(2,1)}), bf16[2048,1408]{0,1:T(8,128)(2,1)}) %all-gather.26.cloned.1.call-update) | async-done | bytes 5767184 | tf_op jit(solution)/shard_map/while/body/eval_jaxpr/all_gather | solution.py:48
  1448.1 44.0 %reduce-scatter.20.cloned.1.call-done = f32[512,256]{1,0:T(8,128)} async-done(((f32[2048,256]{1,0:T(8,128)}), f32[512,256]{1,0:T(8,128)}) %reduce-scatter.20.cloned.1.call-update) | async-done | bytes 524304 | tf_op jit(solution)/shard_map/while/body/eval_jaxpr/reduce_scatter | solution.py:61
  1502.4 26.9 %all-gather.28.cloned.1.call-done = bf16[2048,256]{1,0:T(8,128)(2,1)} async-done(((bf16[512,256]{1,0:T(8,128)(2,1)}), bf16[2048,256]{1,0:T(8,128)(2,1)}) %all-gather.28.cloned.1.call-update) | async-done | bytes 1048592 | tf_op jit(solution)/shard_map/while/body/eval_jaxpr/all_gather | solution.py:44
  1532.4 31.0 %reduce-scatter.22.cloned.1.call-done = f32[512,256]{1,0:T(8,128)} async-done(((f32[2048,256]{1,0:T(8,128)}), f32[512,256]{1,0:T(8,128)}) %reduce-scatter.22.cloned.1.call-update) | async-done | bytes 524304 | tf_op jit(solution)/shard_map/while/body/eval_jaxpr/reduce_scatter | solution.py:52
  1564.7 10.3 while.151
  1578.2 14.9 while.152
  1659.7 14.9 reduce-scatter.24.cloned.1.call-done
  1677.6 26.2 %all-gather.30.cloned.1.call-done = bf16[2048,704]{0,1:T(8,128)(2,1)} async-done(((bf16[512,704]{0,1:T(8,128)(2,1)}), bf16[2048,704]{0,1:T(8,128)(2,1)}) %all-gather.30.cloned.1.call-update) | async-done | bytes 2883600 | tf_op jit(solution)/shard_map/while/body/eval_jaxpr/all_gather | solution.py:48
  1715.4 10.2 reduce-scatter.28.cloned.1.call-done
  1727.8 22.3 %reduce-scatter.26.cloned.1.call-done = bf16[512,160]{0,1:T(8,128)(2,1)} async-done(((bf16[512,640]{0,1:T(8,128)(2,1)}), bf16[512,160]{0,1:T(8,128)(2,1)}) %reduce-scatter.26.cloned.1.call-update) | async-done | bytes 163856 | tf_op jit(solution)/shard_map/while/body/eval_jaxpr/reduce_scatter | solution.py:377
  1765.8 29.3 %reduce-scatter.32.cloned.1.call-done = f32[512,256]{1,0:T(8,128)} async-done(((f32[2048,256]{1,0:T(8,128)}), f32[512,256]{1,0:T(8,128)}) %reduce-scatter.32.cloned.1.call-update) | async-done | bytes 524304 | tf_op jit(solution)/shard_map/while/body/eval_jaxpr/reduce_scatter | solution.py:61
  1805.0 35.7 %reduce-scatter.30.cloned.1.call-done = f32[512,256]{1,0:T(8,128)} async-done(((f32[2048,256]{1,0:T(8,128)}), f32[512,256]{1,0:T(8,128)}) %reduce-scatter.30.cloned.1.call-update) | async-done | bytes 524304 | tf_op jit(solution)/shard_map/while/body/eval_jaxpr/reduce_scatter | solution.py:61
  1858.8 21.2 %all-reduce = (f32[256]{0:T(256)}, f32[256]{0:T(256)}) all-reduce(f32[256]{0:T(256)S(1)} %copy-done.49, f32[256]{0:T(256)S(1)} %copy-done.46), channel_id=1, replica_groups=mesh['dp'=2,'row'=4,'col'=4] {'dp','row'}, use_global_device_ids=true, to_apply=%region_48.49 | all-reduce | flops 512 | bytes 4096 | tf_op jit(solution)/shard_map/psum | solution.py:417
  1880.0 24.2 %all-reduce.4.cloned.1.call-done = (bf16[256,200]{0,1:T(8,128)(2,1)}, bf16[256,256]{1,0:T(8,128)(2,1)}, bf16[256,1408]{0,1:T(8,128)(2,1)}, bf16[704,256]{1,0:T(8,128)(2,1)}) async-done(((bf16[256,200]{0,1:T(8,128)(2,1)}, bf16[256,256]{1,0:T(8,128)(2,1)}, bf16[256,1408]{0,1:T(8,128)(2,1)}, bf16[704,256]{1,0:T(8,128)(2,1)}), (bf16[256,200]{0,1:T(8,128)(2,1)}, bf16[256,256]{1,0:T(8,128)(2,1)}, ...) | async-done | bytes 1314832 | tf_op jit(solution)/shard_map/psum | solution.py:412
  (698 shorter events, 615.1 us)
Async XLA Ops:
  13.5 39.1 %all-gather.14.cloned.1.call-start = ((), (), s32[]{:S(2)}) async-start(), calls=%async_computation.12 | async-start | bytes 1310720 | tf_op jit(solution)/shard_map/while/body/eval_jaxpr/all_gather | solution.py:44
  24.2 59.6 %reduce-scatter.12.cloned.1.call-start = ((), (), s32[]{:S(2)}) async-start(), calls=%async_computation.13 | async-start | bytes 2048000 | tf_op jit(solution)/shard_map/while/body/eval_jaxpr/reduce_scatter | solution.py:52
  55.6 63.1 %all-gather.16.cloned.1.call-start = ((), (), s32[]{:S(2)}) async-start(), calls=%async_computation.14 | async-start | bytes 1638400 | tf_op jit(solution)/shard_map/while/body/eval_jaxpr/all_gather | solution.py:269
  85.6 65.0 %all-gather.18.cloned.1.call-start = ((), (), s32[]{:S(2)}) async-start(), calls=%async_computation.15 | async-start | bytes 1310720 | tf_op jit(solution)/shard_map/while/body/eval_jaxpr/all_gather | solution.py:287
  121.5 97.4 %all-gather.22.cloned.1.call-start = ((), (), s32[]{:S(2)}) async-start(), calls=%async_computation.18 | async-start | bytes 1310720 | tf_op jit(solution)/shard_map/while/body/eval_jaxpr/all_gather | solution.py:48
  194.8 71.2 %reduce-scatter.16.cloned.1.call-start = ((), (), s32[]{:S(2)}) async-start(), calls=%async_computation.19 | async-start | bytes 2621440 | tf_op jit(solution)/shard_map/while/body/eval_jaxpr/reduce_scatter | solution.py:61
  222.0 73.6 %copy-start.26 = (bf16[704,256]{1,0:T(8,128)(2,1)S(1)}, bf16[704,256]{1,0:T(8,128)(2,1)}, u32[]{:S(2)}) copy-start(bf16[704,256]{1,0:T(8,128)(2,1)} %get-tuple-element.2583) | copy-start | bytes 1081348 | tf_op jit(solution)/shard_map/while
  222.0 73.5 %all-gather.20.cloned.1.call-start = ((), (), s32[]{:S(2)}) async-start(), calls=%async_computation.16 | async-start | bytes 1310720 | tf_op jit(solution)/shard_map/while/body/eval_jaxpr/all_gather | solution.py:44
  222.8 101.8 %all-gather.24.cloned.1.call-start = ((), (), s32[]{:S(2)}) async-start(), calls=%async_computation.20 | async-start | bytes 1310720 | tf_op jit(solution)/shard_map/while/body/eval_jaxpr/all_gather | solution.py:44
  273.7 309.9 %copy-start.32 = (f32[512]{0:T(512)}, f32[512]{0:T(512)S(1)}, u32[]{:S(2)}) copy-start(f32[512]{0:T(512)S(1)} %add_rsqrt_fusion.5) | copy-start | bytes 6148 | tf_op jit(solution)/shard_map/while
  274.6 107.2 %reduce-scatter.14.cloned.1.call-start = ((), (), s32[]{:S(2)}) async-start(), calls=%async_computation.17 | async-start | bytes 7208960 | tf_op jit(solution)/shard_map/while/body/eval_jaxpr/reduce_scatter | solution.py:52
  300.2 176.2 %reduce-scatter.18.cloned.1.call-start = ((), (), s32[]{:S(2)}) async-start(), calls=%async_computation.21 | async-start | bytes 14417920 | tf_op jit(solution)/shard_map/while/body/eval_jaxpr/reduce_scatter | solution.py:52
  332.0 193.2 %all-gather.26.cloned.1.call-start = ((), (), s32[]{:S(2)}) async-start(), calls=%async_computation.22 | async-start | bytes 7208960 | tf_op jit(solution)/shard_map/while/body/eval_jaxpr/all_gather | solution.py:48
  481.7 93.6 %reduce-scatter.20.cloned.1.call-start = ((), (), s32[]{:S(2)}) async-start(), calls=%async_computation.23 | async-start | bytes 2621440 | tf_op jit(solution)/shard_map/while/body/eval_jaxpr/reduce_scatter | solution.py:61
  531.3 81.3 %copy-start.23 = (bf16[256,256]{1,0:T(8,128)(2,1)S(1)}, bf16[256,256]{1,0:T(8,128)(2,1)}, u32[]{:S(2)}) copy-start(bf16[256,256]{1,0:T(8,128)(2,1)} %get-tuple-element.2582) | copy-start | bytes 393220 | tf_op jit(solution)/shard_map/while
  531.3 81.2 %all-gather.28.cloned.1.call-start = ((), (), s32[]{:S(2)}) async-start(), calls=%async_computation.24 | async-start | bytes 1310720 | tf_op jit(solution)/shard_map/while/body/eval_jaxpr/all_gather | solution.py:44
  585.6 61.1 %reduce-scatter.22.cloned.1.call-start = ((), (), s32[]{:S(2)}) async-start(), calls=%async_computation.25 | async-start | bytes 2621440 | tf_op jit(solution)/shard_map/while/body/eval_jaxpr/reduce_scatter | solution.py:52
  615.6 142.3 %reduce-scatter.24.cloned.1.call-start = ((), (), s32[]{:S(2)}) async-start(), calls=%async_computation.26 | async-start | bytes 1310720 | tf_op jit(solution)/shard_map/while/body/eval_jaxpr/reduce_scatter | solution.py:362
  711.8 75.2 %all-gather.30.cloned.1.call-start = ((), (), s32[]{:S(2)}) async-start(), calls=%async_computation.29 | async-start | bytes 3604480 | tf_op jit(solution)/shard_map/while/body/eval_jaxpr/all_gather | solution.py:48
  712.4 96.5 %reduce-scatter.28.cloned.1.call-start = ((), (), s32[]{:S(2)}) async-start(), calls=%async_computation.28 | async-start | bytes 81920 | tf_op jit(solution)/shard_map/while/body/eval_jaxpr/reduce_scatter | solution.py:359
  742.9 90.3 %reduce-scatter.26.cloned.1.call-start = ((), (), s32[]{:S(2)}) async-start(), calls=%async_computation.27 | async-start | bytes 819200 | tf_op jit(solution)/shard_map/while/body/eval_jaxpr/reduce_scatter | solution.py:377
  760.8 117.5 %reduce-scatter.32.cloned.1.call-start = ((), (), s32[]{:S(2)}) async-start(), calls=%async_computation.31 | async-start | bytes 2621440 | tf_op jit(solution)/shard_map/while/body/eval_jaxpr/reduce_scatter | solution.py:61
  791.3 132.5 %reduce-scatter.30.cloned.1.call-start = ((), (), s32[]{:S(2)}) async-start(), calls=%async_computation.30 | async-start | bytes 2621440 | tf_op jit(solution)/shard_map/while/body/eval_jaxpr/reduce_scatter | solution.py:61
  934.2 35.3 %all-gather.14.cloned.1.call-start = ((), (), s32[]{:S(2)}) async-start(), calls=%async_computation.12 | async-start | bytes 1310720 | tf_op jit(solution)/shard_map/while/body/eval_jaxpr/all_gather | solution.py:44
  942.4 58.2 %reduce-scatter.12.cloned.1.call-start = ((), (), s32[]{:S(2)}) async-start(), calls=%async_computation.13 | async-start | bytes 2048000 | tf_op jit(solution)/shard_map/while/body/eval_jaxpr/reduce_scatter | solution.py:52
  972.4 63.1 %all-gather.16.cloned.1.call-start = ((), (), s32[]{:S(2)}) async-start(), calls=%async_computation.14 | async-start | bytes 1638400 | tf_op jit(solution)/shard_map/while/body/eval_jaxpr/all_gather | solution.py:269
  1002.4 65.0 %all-gather.18.cloned.1.call-start = ((), (), s32[]{:S(2)}) async-start(), calls=%async_computation.15 | async-start | bytes 1310720 | tf_op jit(solution)/shard_map/while/body/eval_jaxpr/all_gather | solution.py:287
  1038.3 97.4 %all-gather.22.cloned.1.call-start = ((), (), s32[]{:S(2)}) async-start(), calls=%async_computation.18 | async-start | bytes 1310720 | tf_op jit(solution)/shard_map/while/body/eval_jaxpr/all_gather | solution.py:48
  1111.6 71.2 %reduce-scatter.16.cloned.1.call-start = ((), (), s32[]{:S(2)}) async-start(), calls=%async_computation.19 | async-start | bytes 2621440 | tf_op jit(solution)/shard_map/while/body/eval_jaxpr/reduce_scatter | solution.py:61
  1138.8 51.7 %copy-start.40 = (f32[256]{0:T(256)S(1)}, f32[256]{0:T(256)}, u32[]{:S(2)}) copy-start(f32[256]{0:T(256)} %get-tuple-element.2584) | copy-start | bytes 3076 | tf_op jit(solution)/shard_map/while
  1138.8 73.4 %copy-start.26 = (bf16[704,256]{1,0:T(8,128)(2,1)S(1)}, bf16[704,256]{1,0:T(8,128)(2,1)}, u32[]{:S(2)}) copy-start(bf16[704,256]{1,0:T(8,128)(2,1)} %get-tuple-element.2583) | copy-start | bytes 1081348 | tf_op jit(solution)/shard_map/while
  1138.8 73.4 %all-gather.20.cloned.1.call-start = ((), (), s32[]{:S(2)}) async-start(), calls=%async_computation.16 | async-start | bytes 1310720 | tf_op jit(solution)/shard_map/while/body/eval_jaxpr/all_gather | solution.py:44
  1139.7 101.7 %all-gather.24.cloned.1.call-start = ((), (), s32[]{:S(2)}) async-start(), calls=%async_computation.20 | async-start | bytes 1310720 | tf_op jit(solution)/shard_map/while/body/eval_jaxpr/all_gather | solution.py:44
  1190.5 309.8 %copy-start.32 = (f32[512]{0:T(512)}, f32[512]{0:T(512)S(1)}, u32[]{:S(2)}) copy-start(f32[512]{0:T(512)S(1)} %add_rsqrt_fusion.5) | copy-start | bytes 6148 | tf_op jit(solution)/shard_map/while
  1191.4 107.0 %reduce-scatter.14.cloned.1.call-start = ((), (), s32[]{:S(2)}) async-start(), calls=%async_computation.17 | async-start | bytes 7208960 | tf_op jit(solution)/shard_map/while/body/eval_jaxpr/reduce_scatter | solution.py:52
  1216.9 176.2 %reduce-scatter.18.cloned.1.call-start = ((), (), s32[]{:S(2)}) async-start(), calls=%async_computation.21 | async-start | bytes 14417920 | tf_op jit(solution)/shard_map/while/body/eval_jaxpr/reduce_scatter | solution.py:52
  1248.7 193.2 %all-gather.26.cloned.1.call-start = ((), (), s32[]{:S(2)}) async-start(), calls=%async_computation.22 | async-start | bytes 7208960 | tf_op jit(solution)/shard_map/while/body/eval_jaxpr/all_gather | solution.py:48
  1398.4 93.7 %reduce-scatter.20.cloned.1.call-start = ((), (), s32[]{:S(2)}) async-start(), calls=%async_computation.23 | async-start | bytes 2621440 | tf_op jit(solution)/shard_map/while/body/eval_jaxpr/reduce_scatter | solution.py:61
  1448.0 81.3 %copy-start.23 = (bf16[256,256]{1,0:T(8,128)(2,1)S(1)}, bf16[256,256]{1,0:T(8,128)(2,1)}, u32[]{:S(2)}) copy-start(bf16[256,256]{1,0:T(8,128)(2,1)} %get-tuple-element.2582) | copy-start | bytes 393220 | tf_op jit(solution)/shard_map/while
  1448.0 81.3 %all-gather.28.cloned.1.call-start = ((), (), s32[]{:S(2)}) async-start(), calls=%async_computation.24 | async-start | bytes 1310720 | tf_op jit(solution)/shard_map/while/body/eval_jaxpr/all_gather | solution.py:44
  1502.3 61.1 %reduce-scatter.22.cloned.1.call-start = ((), (), s32[]{:S(2)}) async-start(), calls=%async_computation.25 | async-start | bytes 2621440 | tf_op jit(solution)/shard_map/while/body/eval_jaxpr/reduce_scatter | solution.py:52
  1532.4 142.3 %reduce-scatter.24.cloned.1.call-start = ((), (), s32[]{:S(2)}) async-start(), calls=%async_computation.26 | async-start | bytes 1310720 | tf_op jit(solution)/shard_map/while/body/eval_jaxpr/reduce_scatter | solution.py:362
  1628.6 75.2 %all-gather.30.cloned.1.call-start = ((), (), s32[]{:S(2)}) async-start(), calls=%async_computation.29 | async-start | bytes 3604480 | tf_op jit(solution)/shard_map/while/body/eval_jaxpr/all_gather | solution.py:48
  1629.2 96.5 %reduce-scatter.28.cloned.1.call-start = ((), (), s32[]{:S(2)}) async-start(), calls=%async_computation.28 | async-start | bytes 81920 | tf_op jit(solution)/shard_map/while/body/eval_jaxpr/reduce_scatter | solution.py:359
  1659.7 90.5 %reduce-scatter.26.cloned.1.call-start = ((), (), s32[]{:S(2)}) async-start(), calls=%async_computation.27 | async-start | bytes 819200 | tf_op jit(solution)/shard_map/while/body/eval_jaxpr/reduce_scatter | solution.py:377
  1677.5 117.5 %reduce-scatter.32.cloned.1.call-start = ((), (), s32[]{:S(2)}) async-start(), calls=%async_computation.31 | async-start | bytes 2621440 | tf_op jit(solution)/shard_map/while/body/eval_jaxpr/reduce_scatter | solution.py:61
  1708.0 132.7 %reduce-scatter.30.cloned.1.call-start = ((), (), s32[]{:S(2)}) async-start(), calls=%async_computation.30 | async-start | bytes 2621440 | tf_op jit(solution)/shard_map/while/body/eval_jaxpr/reduce_scatter | solution.py:61
  1852.4 51.9 %all-reduce.4.cloned.1.call-start = ((), (), s32[]{:S(2)}) async-start(), calls=%async_computation.11 | async-start | bytes 2629632 | tf_op jit(solution)/shard_map/psum | solution.py:412
  (90 other events, 1773.5 us)
Sparse Core Ops, SparseCore 0:
  24.3 28.2 all-gather.13
  55.7 28.0 reduce-scatter.11
  85.9 32.7 all-gather.15
  121.6 15.7 all-gather.17
  194.9 23.8 all-gather.21
  222.1 43.8 reduce-scatter.15
  268.2 27.2 all-gather.19
  297.2 27.4 all-gather.23
  327.3 54.3 reduce-scatter.13
  384.2 92.1 reduce-scatter.17
  481.8 43.3 all-gather.25
  531.4 43.8 reduce-scatter.19
  585.7 26.7 all-gather.27
  615.8 30.9 reduce-scatter.21
  712.0 45.8 reduce-scatter.23
  760.0 27.0 all-gather.29
  789.4 19.4 reduce-scatter.27
  811.1 22.1 reduce-scatter.25
  835.5 42.7 reduce-scatter.31
  880.6 43.1 reduce-scatter.29
  942.6 26.8 all-gather.13
  972.5 28.0 reduce-scatter.11
  1002.8 32.7 all-gather.15
  1038.4 15.7 all-gather.17
  1111.8 23.8 all-gather.21
  1139.0 43.8 reduce-scatter.15
  1184.9 27.2 all-gather.19
  1213.9 27.4 all-gather.23
  1244.0 54.3 reduce-scatter.13
  1300.9 92.1 reduce-scatter.17
  1398.5 43.3 all-gather.25
  1448.1 43.8 reduce-scatter.19
  1502.4 26.7 all-gather.27
  1532.5 30.9 reduce-scatter.21
  1628.7 45.9 reduce-scatter.23
  1676.7 27.0 all-gather.29
  1706.2 19.4 reduce-scatter.27
  1727.9 22.1 reduce-scatter.25
  1752.3 42.6 reduce-scatter.31
  1797.5 43.1 reduce-scatter.29
Sparse Core Ops, SparseCore 1:
  1858.9 45.3 all-reduce.3
where the time goes:
time: 1930 us; the launch traced here: 1920 us
  waiting for transfers between devices  1280 us (66%)
  matrix products  243 us (13%)
  local copies, waits for them, and re-layouts  132 us (7%)
  other arithmetic  116 us (6%)
  blocking collectives  102 us (5%)
  loops' own time  27.5 us (1%)
    reduce_scatter x8, waiting for transfers between devices, col_reduce(): lax.psum_scatter(term_fn(jnp.int32(0), total_rows // lax.axis_size('col')...  407 us
    reduce_scatter x8, waiting for transfers between devices, row_reduce(): lax.psum_scatter(term_fn(jnp.int32(0), total_rows // lax.axis_size('row')...  305 us
    all_gather x8, waiting for transfers between devices, row_gather(): return lax.all_gather(values, 'row', axis=0, tiled=True)  200 us
    all_gather x6, waiting for transfers between devices, col_gather(): return lax.all_gather(values, 'col', axis=0, tiled=True)  187 us
    dot_general x16, matrix products, term_rows(): return jnp.dot(left, right, preferred_element_type=jnp.float32)  68.4 us
    all_gather x2, waiting for transfers between devices, micro_step(): lax.all_gather(factors[:, head_cols:], 'row', axis=1, tiled=True)  62.3 us
    psum x8, blocking collectives, col_total(): return lax.psum(values, 'col')  52.4 us
    reduce_scatter x2, waiting for transfers between devices, micro_step(): lax.psum_scatter(rank_grads_full.astype(jnp.bfloat16), 'row', scatter_dim...  44.5 us
  transfers between devices with their start and end apart: 41, of which 39 were waited for; matrix products, arithmetic and copies ran while one was open for 10% of the time, Pallas kernels for 0%

commit v1 on v0

v1 whole, which is shorter than its diff:
```python
import functools

import jax
import jax.numpy as jnp
from jax import lax
from jax.experimental import pallas as pl
from jax.experimental.pallas import tpu as pltpu
from jax.sharding import PartitionSpec as P

D = 1024
H = 16
HD = 64
RQ = 6
RK = 2
FAC = 10
MAX_DOC = 1024

EPS = 1e-06
ROPE = 10000.0
NEG = -1e30
BF = jnp.bfloat16
F32 = jnp.float32
LANES = 128
PAIRS = H // 2
FAC_ORDER = (6, 7, 8, 9, 0, 1, 2, 3, 4, 5)
FAC_BACK = (4, 5, 6, 7, 8, 9, 0, 1, 2, 3)
VMEM = pl.BlockSpec(memory_space=pltpu.VMEM)


def nn(a, b):
    return jnp.dot(a, b, preferred_element_type=F32)


def nt(a, b):
    return lax.dot_general(a, b, (((1,), (1,)), ((), ())), preferred_element_type=F32)


def tn(a, b):
    return lax.dot_general(a, b, (((0,), (0,)), ((), ())), preferred_element_type=F32)


def two_pass(a, b):
    high = a.astype(BF)
    low = (a - high.astype(F32)).astype(BF)
    return nn(high, b) + nn(low, b)


def lane_iota(shape):
    return lax.broadcasted_iota(jnp.int32, shape, len(shape) - 1)


def spread(rows, first, width):
    row = lax.broadcasted_iota(jnp.int32, (rows, width), 0)
    head = lax.broadcasted_iota(jnp.int32, (rows, width), 1) // HD
    return (row == head + first).astype(F32).astype(BF)


def collect(rows, width, first):
    head = lax.broadcasted_iota(jnp.int32, (rows, width), 0) // HD
    lane = lax.broadcasted_iota(jnp.int32, (rows, width), 1)
    return (lane == head + first).astype(F32).astype(BF)


def swap_halves(tile):
    lane = lane_iota(tile.shape)
    ahead = pltpu.roll(tile, LANES - HD // 2, 1)
    behind = pltpu.roll(tile, HD // 2, 1)
    return jnp.where(lane % HD < HD // 2, ahead, behind)


def double_left(tile):
    return jnp.where(lane_iota(tile.shape) < HD, tile, pltpu.roll(tile, HD, 1))


def double_right(tile):
    return jnp.where(lane_iota(tile.shape) < HD, pltpu.roll(tile, HD, 1), tile)


def params(**more):
    return pltpu.CompilerParams(vmem_limit_bytes=60 << 20, **more)


def call(body, outs, scratch=(), cost=None):
    return pl.pallas_call(
        body,
        out_shape=outs,
        scratch_shapes=scratch,
        compiler_params=params(),
        cost_estimate=cost,
    )


def cost_of(flops, moved):
    return pl.CostEstimate(flops=int(flops), bytes_accessed=int(moved), transcendentals=0)


def front_body(x_ref, gain_ref, w_ref, turn_ref, h_ref, hf_ref, bq_ref, kf_ref, q_ref):
    parts = x_ref.shape[0]
    feat = x_ref.shape[2]
    xs = [x_ref[c].astype(F32) for c in range(parts)]
    total = sum(jnp.sum(v * v, axis=1, keepdims=True) for v in xs)
    scale = lax.rsqrt(total / D + EPS)
    for c in range(parts):
        lanes = slice(c * feat, (c + 1) * feat)
        h_ref[:, lanes] = (xs[c] * scale * gain_ref[:, lanes]).astype(BF)
    both = nn(h_ref[...], w_ref[...])
    heads = both[:, FAC * HD :]
    hf_ref[...] = heads
    cosine = turn_ref[:, :LANES]
    sine = turn_ref[:, LANES:]
    for tile in range(FAC * HD // LANES):
        lanes = slice(tile * LANES, (tile + 1) * LANES)
        part = both[:, lanes]
        if tile < 4:
            part = part * cosine + swap_halves(part) * sine
        if tile < 3:
            bq_ref[:, lanes] = part
        else:
            kf_ref[:, (tile - 3) * LANES : (tile - 2) * LANES] = part.astype(BF)
    kf_ref[:, 2 * LANES :] = heads[:, : 2 * RK * H].astype(BF)
    high = heads.astype(BF)
    low = (heads - high.astype(F32)).astype(BF)
    ranks = []
    for r in range(RQ):
        tile = bq_ref[:, (r // 2) * LANES : (r // 2 + 1) * LANES]
        ranks.append(double_left(tile) if r % 2 == 0 else double_right(tile))
    width = 2 * LANES
    for p in range(D // width):
        lanes = slice(p * width, (p + 1) * width)
        acc = None
        for r in range(RQ):
            pick = spread(H * FAC, (2 * RK + r) * H + p * (width // HD), width)
            term = (nn(high, pick) + nn(low, pick)) * jnp.concatenate([ranks[r]] * 2, axis=1)
            acc = term if acc is None else acc + term
        q_ref[:, lanes] = (acc / RQ).astype(BF)


def front(x_parts, gain, w_rh, turn):
    rows = x_parts.shape[1]
    return call(
        front_body,
        (
            jax.ShapeDtypeStruct((rows, D), BF),
            jax.ShapeDtypeStruct((rows, H * FAC), F32),
            jax.ShapeDtypeStruct((rows, RQ * HD), F32),
            jax.ShapeDtypeStruct((rows, 2 * LANES + 2 * RK * H), BF),
            jax.ShapeDtypeStruct((rows, D), BF),
        ),
        cost=cost_of(2 * rows * D * 800 * 3, 6 << 20),
    )(x_parts, gain, w_rh, turn)


def mask_bias(seg_ref, keys, rows):
    seg_row = seg_ref[...].astype(F32)
    wide = jnp.broadcast_to(seg_row, (LANES, keys))
    column = wide.T
    column = jnp.concatenate([column] * (rows // LANES), axis=1)
    key_idx = lax.broadcasted_iota(jnp.int32, (keys, rows), 0)
    query_idx = lax.broadcasted_iota(jnp.int32, (keys, rows), 1) + (keys - rows)
    same = column == seg_row[:, keys - rows :]
    return jnp.where(same & (key_idx <= query_idx), 0.0, NEG)


def attend_body(q_ref, kf_ref, seg_ref, o_ref, lse_ref, k_ref, v_ref, bias_ref, dup_ref):
    rows = q_ref.shape[0]
    keys = kf_ref.shape[0]
    bias_ref[...] = mask_bias(seg_ref, keys, rows)
    for s in range(2 * RK):
        tile = kf_ref[:, (s // 2) * LANES : (s // 2 + 1) * LANES].astype(F32)
        dup_ref[s] = double_left(tile) if s % 2 == 0 else double_right(tile)

    def pair(p, carried):
        lanes = pl.ds(pl.multiple_of(p * LANES, LANES), LANES)
        weights = kf_ref[:, 2 * LANES :]
        made = []
        for kind in range(2):
            acc = None
            for s in range(RK):
                pick = spread(2 * RK * H, (kind * RK + s) * H + 2 * p, LANES)
                term = nn(weights, pick) * dup_ref[kind * RK + s]
                acc = term if acc is None else acc + term
            made.append((acc / RK).astype(BF))
        k_tile, v_tile = made
        k_ref[:, lanes] = k_tile
        v_ref[:, lanes] = v_tile
        v_turned = v_tile.astype(F32).T.astype(BF)
        q_turned = (q_ref[:, lanes].astype(F32) * HD**-0.5).T
        half = lax.broadcasted_iota(jnp.int32, q_turned.shape, 0) // HD
        outs = []
        for side in range(2):
            q_side = jnp.where(half == side, q_turned, 0.0).astype(BF)
            scores = nn(k_tile, q_side) + bias_ref[...]
            peak = jnp.max(scores, axis=0, keepdims=True)
            weight = jnp.exp(scores - peak)
            total = jnp.sum(weight, axis=0, keepdims=True)
            probs = (weight * (1.0 / total)).astype(BF)
            outs.append(nn(v_turned[side * HD : (side + 1) * HD], probs))
            lse_ref[2 * p + side] = jnp.broadcast_to(peak + jnp.log(total), (8, rows))
        o_ref[:, lanes] = jnp.concatenate(outs, axis=0).T.astype(BF)
        return carried

    lax.fori_loop(0, PAIRS, pair, 0)


def attend(q, kf_window, seg_window):
    rows = q.shape[0]
    keys = kf_window.shape[0]
    return call(
        attend_body,
        (
            jax.ShapeDtypeStruct((rows, D), BF),
            jax.ShapeDtypeStruct((H, 8, rows), F32),
            jax.ShapeDtypeStruct((keys, D), BF),
            jax.ShapeDtypeStruct((keys, D), BF),
        ),
        scratch=(pltpu.VMEM((keys, rows), F32), pltpu.VMEM((2 * RK, keys, LANES), F32)),
        cost=cost_of(2 * rows * keys * D * 16, 16 << 20),
    )(q, kf_window, seg_window)


def attend_back_body(
    q_ref, k_ref, v_ref, do_ref, lse_ref, kf_ref, seg_ref, dq_ref, dkf_ref, bias_ref, dup_ref, sum_ref, fac_ref
):
    rows = q_ref.shape[0]
    keys = kf_ref.shape[0]
    bias_ref[...] = mask_bias(seg_ref, keys, rows)
    for s in range(2 * RK):
        tile = kf_ref[:, (s // 2) * LANES : (s // 2 + 1) * LANES].astype(F32)
        dup_ref[s] = double_left(tile) if s % 2 == 0 else double_right(tile)
    sum_ref[...] = jnp.zeros_like(sum_ref)
    fac_ref[...] = jnp.zeros_like(fac_ref)

    def pair(p, carried):
        lanes = pl.ds(pl.multiple_of(p * LANES, LANES), LANES)
        k_tile = k_ref[:, lanes]
        v_tile = v_ref[:, lanes]
        k_turned = k_tile.astype(F32).T.astype(BF)
        q_tile = q_ref[:, lanes].astype(F32) * HD**-0.5
        do_tile = do_ref[:, lanes].astype(F32)
        q_turned = q_tile.T
        do_turned = do_tile.T
        half = lax.broadcasted_iota(jnp.int32, q_turned.shape, 0) // HD
        lane_half = lax.broadcasted_iota(jnp.int32, q_tile.shape, 1) // HD
        d_k = None
        d_v = None
        d_q = []
        for side in range(2):
            q_side = jnp.where(half == side, q_turned, 0.0).astype(BF)
            do_side = jnp.where(half == side, do_turned, 0.0).astype(BF)
            scores = nn(k_tile, q_side) + bias_ref[...]
            probs = jnp.exp(scores - lse_ref[2 * p + side][:1])
            d_prob = nn(v_tile, do_side)
            delta = jnp.sum(probs * d_prob, axis=0, keepdims=True)
            d_score = (probs * (d_prob - delta)).astype(BF)
            d_q.append(nn(k_turned[side * HD : (side + 1) * HD], d_score))
            q_back = jnp.where(lane_half == side, q_tile, 0.0).astype(BF)
            do_back = jnp.where(lane_half == side, do_tile, 0.0).astype(BF)
            part_k = nn(d_score, q_back)
            part_v = nn(probs.astype(BF), do_back)
            d_k = part_k if d_k is None else d_k + part_k
            d_v = part_v if d_v is None else d_v + part_v
        dq_ref[:, lanes] = jnp.concatenate(d_q, axis=0).T * HD**-0.5
        weights = kf_ref[:, 2 * LANES :]
        for kind, grad in ((0, d_k), (1, d_v)):
            for s in range(RK):
                slot = kind * RK + s
                pick = spread(2 * RK * H, slot * H + 2 * p, LANES)
                sum_ref[slot] += nn(weights, pick) * grad
                fac_ref[...] += two_pass(grad * dup_ref[slot], collect(LANES, 2 * RK * H, slot * H + 2 * p))
        return carried

    lax.fori_loop(0, PAIRS, pair, 0)
    for tile in range(2):
        first = sum_ref[2 * tile]
        second = sum_ref[2 * tile + 1]
        first = first + pltpu.roll(first, HD, 1)
        second = second + pltpu.roll(second, HD, 1)
        merged = jnp.where(lane_iota(first.shape) < HD, first, second)
        dkf_ref[:, tile * LANES : (tile + 1) * LANES] = (merged / RK).astype(BF)
    dkf_ref[:, 2 * LANES :] = (fac_ref[...] / RK).astype(BF)


def attend_back(q, k, v, d_heads, lse, kf_window, seg_window):
    rows = q.shape[0]
    keys = kf_window.shape[0]
    return call(
        attend_back_body,
        (
            jax.ShapeDtypeStruct((rows, D), F32),
            jax.ShapeDtypeStruct(kf_window.shape, BF),
        ),
        scratch=(
            pltpu.VMEM((keys, rows), F32),
            pltpu.VMEM((2 * RK, keys, LANES), F32),
            pltpu.VMEM((2 * RK, keys, LANES), F32),
            pltpu.VMEM((keys, 2 * RK * H), F32),
        ),
        cost=cost_of(2 * rows * keys * D * 40, 16 << 20),
    )(q, k, v, d_heads, lse, kf_window, seg_window)


def middle_body(
    x_ref, cot_ref, heads_ref, w_out_ref, gain_ref, w_ref,
    out_ref, d_mixed_ref, d_heads_ref, g_out_ref, g_gain_ref, g_ref,
    mixed_ref, h_ref, scale_ref, sum_ref, back_ref, cot_all_ref,
):
    step = pl.program_id(0)
    steps = pl.num_programs(0)
    parts, _, feat = x_ref.shape
    rows_of = w_out_ref.shape[0]
    head_rows = w_out_ref.shape[2]
    hidden_size = w_ref.shape[2] // 3

    def lanes_of(c):
        return slice(c * feat, (c + 1) * feat)

    @pl.when(step == 0)
    def _():
        total = None
        for c in range(parts):
            acc = x_ref[c].astype(F32)
            for r in range(rows_of):
                acc = acc + nn(heads_ref[:, r * head_rows : (r + 1) * head_rows], w_out_ref[r, c])
            mixed_ref[:, lanes_of(c)] = acc
            part = jnp.sum(acc * acc, axis=1, keepdims=True)
            total = part if total is None else total + part
            cot_all_ref[:, lanes_of(c)] = cot_ref[c]
        scale = lax.rsqrt(total / D + EPS)
        scale_ref[...] = jnp.broadcast_to(scale, scale_ref.shape)
        h_ref[...] = (mixed_ref[...] * scale * gain_ref[...]).astype(BF)
        sum_ref[...] = jnp.zeros_like(sum_ref)
        back_ref[...] = jnp.zeros_like(back_ref)

    gate = None
    up = None
    d_hidden = None
    for c in range(parts):
        h_part = h_ref[:, lanes_of(c)]
        term_g = nt(h_part, w_ref[0, c, :hidden_size])
        term_u = nt(h_part, w_ref[0, c, hidden_size : 2 * hidden_size])
        term_d = nt(cot_ref[c], w_ref[0, c, 2 * hidden_size :])
        gate = term_g if gate is None else gate + term_g
        up = term_u if up is None else up + term_u
        d_hidden = term_d if d_hidden is None else d_hidden + term_d
    sig = 1.0 / (1.0 + jnp.exp(-gate))
    silu = gate * sig
    hidden = (silu * up).astype(BF)
    d_gate = (d_hidden * up * sig * (1.0 + gate * (1.0 - sig))).astype(BF)
    d_up = (d_hidden * silu).astype(BF)
    for c in range(parts):
        sum_ref[:, lanes_of(c)] += nn(hidden, w_ref[0, c, 2 * hidden_size :])
        back_ref[:, lanes_of(c)] += nn(d_gate, w_ref[0, c, :hidden_size]) + nn(
            d_up, w_ref[0, c, hidden_size : 2 * hidden_size]
        )
    for place, (left, right) in enumerate(((d_gate, h_ref), (d_up, h_ref), (hidden, cot_all_ref))):
        grad = tn(left, right[...])
        for c in range(parts):
            g_ref[0, c, place * hidden_size : (place + 1) * hidden_size] = grad[:, lanes_of(c)].astype(BF)

    @pl.when(step == steps - 1)
    def _():
        scale = scale_ref[:, :1]
        mixed = mixed_ref[...]
        out_ref[...] = (mixed + sum_ref[...]).astype(BF)
        normed = mixed * scale
        d_h = back_ref[...]
        g_gain_ref[...] = jnp.sum(d_h * normed, axis=0, keepdims=True)
        inner = d_h * gain_ref[...]
        dot = jnp.sum(inner * normed, axis=1, keepdims=True) / D
        d_mixed = cot_all_ref[...].astype(F32) + scale * (inner - normed * dot)
        d_mixed_ref[...] = d_mixed
        low = d_mixed.astype(BF)
        grad = tn(heads_ref[...], low)
        for r in range(rows_of):
            acc = None
            for c in range(parts):
                term = nt(low[:, lanes_of(c)], w_out_ref[r, c])
                acc = term if acc is None else acc + term
                g_out_ref[r, c] = grad[r * head_rows : (r + 1) * head_rows, lanes_of(c)].astype(BF)
            d_heads_ref[:, r * head_rows : (r + 1) * head_rows] = acc.astype(BF)


def middle(x_parts, cot_parts, heads, w_out, gain, w_ffn):
    parts, rows, feat = x_parts.shape
    steps = w_ffn.shape[0]
    block = (1,) + w_ffn.shape[1:]

    def whole(shape):
        return pl.BlockSpec(shape, lambda r: (0,) * len(shape))

    outs = (
        jax.ShapeDtypeStruct((rows, D), BF),
        jax.ShapeDtypeStruct((rows, D), F32),
        jax.ShapeDtypeStruct((rows, D), BF),
        jax.ShapeDtypeStruct(w_out.shape, BF),
        jax.ShapeDtypeStruct((1, D), F32),
        jax.ShapeDtypeStruct(w_ffn.shape, BF),
    )
    return pl.pallas_call(
        middle_body,
        grid=(steps,),
        out_shape=outs,
        in_specs=[whole(a.shape) for a in (x_parts, cot_parts, heads, w_out, gain)]
        + [pl.BlockSpec(block, lambda r: (r, 0, 0, 0))],
        out_specs=[whole(a.shape) for a in outs[:-1]] + [pl.BlockSpec(block, lambda r: (r, 0, 0, 0))],
        scratch_shapes=(
            pltpu.VMEM((rows, D), F32),
            pltpu.VMEM((rows, D), BF),
            pltpu.VMEM((rows, LANES), F32),
            pltpu.VMEM((rows, D), F32),
            pltpu.VMEM((rows, D), F32),
            pltpu.VMEM((rows, D), BF),
        ),
        compiler_params=params(dimension_semantics=("arbitrary",)),
        cost_estimate=cost_of(2 * rows * 3 * 3 * D * 2816, 40 << 20),
    )(x_parts, cot_parts, heads, w_out, gain, w_ffn)


def back_body(
    dq_ref, dkf_ref, hf_ref, bq_ref, turn_ref, w_ref, h_ref, x_ref, gain_ref, d_mixed_ref,
    gi_ref, g_gain_ref, g_ref, d_ref,
):
    parts, rows, feat = x_ref.shape
    heads = hf_ref[...]
    high = heads.astype(BF)
    low = (heads - high.astype(F32)).astype(BF)
    dq = dq_ref[...] * (1.0 / RQ)
    cosine = turn_ref[:, :LANES]
    sine = turn_ref[:, LANES:]
    d_fac = jnp.zeros((rows, H * FAC), F32)
    folded = []
    for r in range(RQ):
        tile = bq_ref[:, (r // 2) * LANES : (r // 2 + 1) * LANES]
        rank = double_left(tile) if r % 2 == 0 else double_right(tile)
        first = (2 * RK + r) * H
        product = dq * jnp.concatenate([rank] * PAIRS, axis=1)
        d_fac = d_fac + two_pass(product, collect(D, H * FAC, first))
        pick = spread(H * FAC, first, D)
        terms = (nn(high, pick) + nn(low, pick)) * dq
        acc = terms[:, :LANES]
        for p in range(1, PAIRS):
            acc = acc + terms[:, p * LANES : (p + 1) * LANES]
        folded.append(acc + pltpu.roll(acc, HD, 1))
    lane = lane_iota(folded[0].shape)

    def turn_back(part):
        return part * cosine - swap_halves(part) * sine

    for tile in range(3):
        merged = jnp.where(lane < HD, folded[2 * tile], folded[2 * tile + 1])
        d_ref[:, tile * LANES : (tile + 1) * LANES] = turn_back(merged).astype(BF)
    d_ref[:, 3 * LANES : 4 * LANES] = turn_back(dkf_ref[:, :LANES].astype(F32)).astype(BF)
    d_ref[:, 4 * LANES : 5 * LANES] = dkf_ref[:, LANES : 2 * LANES].astype(BF)
    keep = 2 * RK * H
    key_fac = jnp.concatenate(
        [dkf_ref[:, 2 * LANES :].astype(F32), jnp.zeros((rows, H * FAC - keep), F32)], axis=1
    )
    d_ref[:, 5 * LANES :] = jnp.where(lane_iota(d_fac.shape) < keep, key_fac, d_fac).astype(BF)
    d_all = d_ref[...]
    d_h = nt(d_all, w_ref[...])
    g_ref[...] = tn(d_all, h_ref[...]).astype(BF)
    xs = [x_ref[c].astype(F32) for c in range(parts)]
    total = sum(jnp.sum(v * v, axis=1, keepdims=True) for v in xs)
    scale = lax.rsqrt(total / D + EPS)
    dot = None
    for c in range(parts):
        lanes = slice(c * feat, (c + 1) * feat)
        normed = xs[c] * scale
        grad = d_h[:, lanes]
        g_gain_ref[:, lanes] = jnp.sum(grad * normed, axis=0, keepdims=True)
        part = jnp.sum(grad * gain_ref[:, lanes] * normed, axis=1, keepdims=True)
        dot = part if dot is None else dot + part
    for c in range(parts):
        lanes = slice(c * feat, (c + 1) * feat)
        normed = xs[c] * scale
        gi_ref[c] = d_mixed_ref[:, lanes] + scale * (
            d_h[:, lanes] * gain_ref[:, lanes] - normed * (dot / D)
        )


def back(dq, dkf, hf, bq, turn, w_rh, h, x_parts, gain, d_mixed):
    rows = dq.shape[0]
    return call(
        back_body,
        (
            jax.ShapeDtypeStruct(x_parts.shape, F32),
            jax.ShapeDtypeStruct((1, D), F32),
            jax.ShapeDtypeStruct((w_rh.shape[1], D), BF),
        ),
        scratch=(pltpu.VMEM((rows, w_rh.shape[1]), BF),),
        cost=cost_of(2 * rows * D * 800 * 6, 12 << 20),
    )(dq, dkf, hf, bq, turn, w_rh, h, x_parts, gain, d_mixed)


def local(
    tokens_in, segments, gain_attn, gain_ffn, w_heads, w_ranks, w_out, w_gate, w_up, w_down, cotangent
):
    n_row = lax.axis_size("row")
    n_col = lax.axis_size("col")
    row = lax.axis_index("row")
    col = lax.axis_index("col")
    micro, row_tokens, feat = tokens_in.shape
    subs = n_col // micro
    rows = row_tokens // subs
    length = row_tokens * n_row
    head_local = w_heads.shape[1] // FAC
    rank_local = w_ranks.shape[1]
    ffn_local = w_gate.shape[1]
    out_local = w_out.shape[0]
    block = row * subs + col % subs
    past = min(-(-(MAX_DOC - 1) // rows), n_row * subs - 1)
    keys = (past + 1) * rows

    heads_t = jnp.transpose(w_heads.reshape(feat, head_local, FAC), (2, 1, 0))
    heads_t = heads_t[jnp.array(FAC_ORDER)].reshape(FAC * head_local, feat)
    attn_local = jnp.concatenate([w_ranks.T, heads_t, w_out], axis=0)
    ffn_block = jnp.concatenate([w_gate.T, w_up.T, w_down], axis=0)
    attn_all = lax.all_gather(attn_local, ("row", "col"), axis=0)
    ffn_all = lax.all_gather(ffn_block, ("row", "col"), axis=0)
    ffn_all = ffn_all.reshape(n_row, n_col, 3 * ffn_local, feat)
    attn_all = attn_all.reshape(n_row, n_col, attn_local.shape[0], feat)
    ranks_full = jnp.transpose(attn_all[:, :, :rank_local], (1, 3, 0, 2)).reshape(D, n_row * rank_local)
    heads_full = attn_all[:, :, rank_local : rank_local + FAC * head_local]
    heads_full = heads_full.reshape(n_row, n_col, FAC, head_local, feat)
    heads_full = jnp.transpose(heads_full, (1, 4, 2, 0, 3)).reshape(D, FAC * H)
    w_rh = jnp.concatenate([ranks_full, heads_full], axis=1)
    w_out_all = attn_all[:, :, rank_local + FAC * head_local :]
    gain_one = lax.all_gather(gain_attn, "col", axis=0, tiled=True).reshape(1, D)
    gain_two = lax.all_gather(gain_ffn, "col", axis=0, tiled=True).reshape(1, D)

    def own_tokens(values):
        return lax.all_to_all(values.reshape(n_col, rows, feat), "col", 0, 0, tiled=True)

    x_parts = own_tokens(tokens_in)
    cot_parts = own_tokens(cotangent)

    seg_row = lax.dynamic_index_in_dim(segments, col // subs, 0, keepdims=False)
    padded = jnp.concatenate([jnp.full((1, past * rows), -1, jnp.int32), seg_row], axis=1)
    seg_window = lax.dynamic_slice_in_dim(padded, block * rows, keys, 1)
    own_seg = seg_window[0, past * rows :]
    key_idx = jnp.arange(keys, dtype=jnp.int32)
    query_idx = jnp.arange(rows, dtype=jnp.int32) + past * rows
    before = (own_seg[:, None] == seg_window) & (key_idx[None, :] < query_idx[:, None])
    places = jnp.sum(before.astype(jnp.int32), axis=1)
    inverse = ROPE ** (-(jnp.arange(HD // 2, dtype=F32) * 2.0 / HD))
    angles = places.astype(F32)[:, None] * inverse[None, :]
    cosine = jnp.cos(angles)
    sine = jnp.sin(angles)
    turn = jnp.concatenate([cosine] * 4 + [-sine, sine, -sine, sine], axis=1)

    h_one, head_fac, bq_rot, key_fac, queries = front(x_parts, gain_one, w_rh, turn)

    groups = [[m * subs + s for s in range(subs)] for m in range(micro)]
    gathered = lax.all_gather(key_fac, "row", axis=0)
    gathered = lax.all_gather(gathered, "col", axis=1, axis_index_groups=groups)
    gathered = gathered.reshape(length, key_fac.shape[1])
    padded = jnp.concatenate([jnp.zeros((past * rows, key_fac.shape[1]), BF), gathered], axis=0)
    kf_window = lax.dynamic_slice_in_dim(padded, block * rows, keys, 0)

    heads_out, lse, key_all, value_all = attend(queries, kf_window, seg_window)
    out_own, d_mixed, d_heads, g_out, g_gain_two, g_ffn = middle(
        x_parts, cot_parts, heads_out, w_out_all, gain_two, ffn_all
    )
    d_q, d_kf = attend_back(queries, key_all, value_all, d_heads, lse, kf_window, seg_window)

    spread_kf = lax.dynamic_update_slice_in_dim(jnp.zeros_like(padded), d_kf, block * rows, 0)[past * rows :]
    spread_kf = spread_kf.reshape(n_row, subs, rows, -1)
    own_kf = lax.psum_scatter(spread_kf, "row", scatter_dimension=0, tiled=False)
    own_kf = lax.psum_scatter(own_kf, "col", scatter_dimension=0, tiled=False, axis_index_groups=groups)

    gi_parts, g_gain_one, g_rh = back(
        d_q, own_kf, head_fac, bq_rot, turn, w_rh, h_one, x_parts, gain_one, d_mixed
    )

    out_parts = jnp.transpose(out_own.reshape(rows, n_col, feat), (1, 0, 2))
    output = lax.all_to_all(out_parts, "col", 0, 0, tiled=True).reshape(tokens_in.shape)
    grad_input = lax.all_to_all(gi_parts, "col", 0, 0, tiled=True).reshape(tokens_in.shape)

    g_ranks = g_rh[: FAC * HD].reshape(n_row, rank_local, n_col, feat)
    g_heads = g_rh[FAC * HD :].reshape(FAC, n_row, head_local, n_col, feat)
    g_ranks = jnp.transpose(g_ranks, (0, 2, 1, 3))
    g_heads = jnp.transpose(g_heads, (1, 3, 0, 2, 4)).reshape(n_row, n_col, FAC * head_local, feat)
    g_attn = jnp.concatenate([g_ranks, g_heads, g_out], axis=2)

    def total(values):
        values = values.reshape((n_row * n_col,) + values.shape[2:])
        part = lax.psum_scatter(values, ("row", "col"), scatter_dimension=0, tiled=False)
        return lax.psum(part, "dp").astype(F32)

    g_ffn = total(g_ffn)
    g_attn = total(g_attn)
    gains = jnp.concatenate([g_gain_one, g_gain_two], axis=0)
    gains = lax.psum(gains, ("dp", "row", "col"))
    gains = lax.dynamic_slice_in_dim(gains, col * feat, feat, 1)
    own_heads = g_attn[rank_local : rank_local + FAC * head_local].reshape(FAC, head_local, feat)
    own_heads = jnp.transpose(own_heads[jnp.array(FAC_BACK)], (2, 1, 0)).reshape(w_heads.shape)
    return (
        output,
        grad_input,
        gains[0],
        gains[1],
        own_heads,
        g_attn[:rank_local].T,
        g_attn[rank_local + FAC * head_local :],
        g_ffn[:ffn_local].T,
        g_ffn[ffn_local : 2 * ffn_local].T,
        g_ffn[2 * ffn_local :],
    )


def solution(mesh):
    tokens = P(None, ("dp", "row"), "col")
    both = P("col", "row")
    turned = P("row", "col")
    gain = P("col")
    return jax.shard_map(
        local,
        mesh=mesh,
        in_specs=(tokens, P(None, "dp", None), gain, gain, both, both, turned, both, both, turned, tokens),
        out_specs=(tokens, tokens, gain, gain, both, both, turned, both, both, turned),
        check_vma=False,
    )
```

time: 1930 us -> 661 us (0.34)
  waiting for transfers between devices: 1280 us -> 397 us
  matrix products: 243 us -> 0 us
  other arithmetic: 116 us -> 10.5 us
  local copies, waits for them, and re-layouts: 132 us -> 29.7 us
  Pallas kernels: 0 us -> 100 us
  loops' own time: 27.5 us -> 0 us
    reduce_scatter x22 -> x4, waiting for transfers between devices: 806 us -> 301 us  [the longest x2 257 us: total(): lax.psum_scatter(values, ('row', 'col'), scatter_dimension=0, tiled=False)]
    all_gather x18 -> x3, waiting for transfers between devices: 449 us -> 95.4 us  [the longest x1 58.8 us: local(): ffn_all = lax.all_gather(ffn_block, ('row', 'col'), axis=0)]
    dot_general x60 -> x0, matrix products: 243 us -> none  [the longest x16 68.4 us: term_rows(): return jnp.dot(left, right, preferred_element_type=jnp.float32)]
    pallas_call x0 -> x5, Pallas kernels: none -> 100 us  [the longest x1 35.5 us: attend_back(): call(attend_back_body, (jax.ShapeDtypeStruct((rows, D), F32), jax.ShapeDt...]
    while x207 -> x0, local copies, waits for them, and re-layouts: 68.2 us -> none  [the longest x12 34.4 us: attend_backward(): return lax.fori_loop(0, seq_len // tile_rows, grad_step, initial)]
    reduce_or x32 -> x0, other arithmetic: 31.8 us -> none  [the longest x8 8.16 us: stat_step(): jnp.any(allowed)]
    another operation x41 -> x0, loops' own time: 27.5 us -> none  [the longest x2 6.76 us: attend_forward(): lax.fori_loop(0, seq_len // tile_rows, stat_step, initial)]
    psum x9 -> x1, blocking collectives: 73.6 us -> 46.8 us  [local(): gains = lax.psum(gains, ('dp', 'row', 'col'))]
  transfers between devices with their start and end apart: 41 -> 11, of which waited for: 39 -> 6; matrix products, arithmetic and copies ran while one was open for 10% -> 3% of each run, Pallas kernels for 0% -> 4%
where the time goes in v1:
time: 661 us; the launch traced here: 660 us
  waiting for transfers between devices  397 us (60%)
  Pallas kernels  100 us (15%)
  blocking collectives  95.6 us (14%)
  local copies, waits for them, and re-layouts  29.7 us (4%)
  between operations  14.5 us (2%)
  starting transfers between devices  11.5 us (2%)
  other arithmetic  10.5 us (2%)
    reduce_scatter x2, waiting for transfers between devices, total(): lax.psum_scatter(values, ('row', 'col'), scatter_dimension=0, tiled=False)  257 us
    all_gather x1, waiting for transfers between devices, local(): ffn_all = lax.all_gather(ffn_block, ('row', 'col'), axis=0)  58.8 us
    psum x1, blocking collectives, local(): gains = lax.psum(gains, ('dp', 'row', 'col'))  46.8 us
    all_gather x1, waiting for transfers between devices, local(): attn_all = lax.all_gather(attn_local, ('row', 'col'), axis=0)  36.6 us
    pallas_call x1, Pallas kernels, attend_back(): call(attend_back_body, (jax.ShapeDtypeStruct((rows, D), F32), jax.ShapeDt...  35.5 us
    reduce_scatter x1, waiting for transfers between devices, local(): lax.psum_scatter(spread_kf, 'row', scatter_dimension=0, tiled=False)  35.4 us
    pallas_call x1, Pallas kernels, middle(): pl.pallas_call(middle_body, grid=(steps,), out_shape=outs, in_specs=[whol...  25.7 us
    pallas_call x1, Pallas kernels, attend(): call(attend_body, (jax.ShapeDtypeStruct((rows, D), BF), jax.ShapeDtypeStr...  24.2 us
  transfers between devices with their start and end apart: 11, of which 6 were waited for; matrix products, arithmetic and copies ran while one was open for 3% of the time, Pallas kernels for 4%

profile of v1, /device:TPU:0, one launch (start us, length us, event | category | flops | bytes accessed | tf_op | source)
XLA Modules:
  0.0 659.8 jit_solution(1197072308084120100)
XLA Ops:
  7.2 0.7 reshape.106
  8.0 0.7 pad_clamp_fusion.1
  9.3 1.7 pad_maximum_fusion.3
  11.0 4.2 all-to-all-start
  16.8 1.0 concatenate.34.turn_ref
  17.8 8.1 %all-gather.4 = f32[4,1,256]{2,1,0:T(1,128)} all-gather(f32[1,1,256]{2,1,0:T(1,128)S(1)} %bitcast.91), channel_id=1, replica_groups=mesh['dp'=2,'row'=4,'col'=4] {'col'}, dimensions={0}, use_global_device_ids=true | all-gather | bytes 5120 | tf_op jit(solution)/shard_map/all_gather | solution.py:528
  25.9 36.6 %all-gather.10.cloned.1.call-done = bf16[7296,256]{1,0:T(8,128)(2,1)} async-done(((bf16[456,256]{1,0:T(8,128)(2,1)}), bf16[7296,256]{1,0:T(8,128)(2,1)}) %all-gather.10.cloned.1.call-update) | async-done | bytes 3735568 | tf_op jit(solution)/shard_map/all_gather | solution.py:518
  62.5 1.7 slice.65
  64.2 1.4 slice_bitcast_fusion
  65.6 1.3 copy.74
  67.0 1.3 reshape.153
  68.3 1.1 reshape.110
  69.8 1.4 pad_maximum_fusion.1.w_ref
  71.2 5.3 shard_map.204
  76.5 19.3 %all-gather.1 = bf16[1024,320]{1,0:T(8,128)(2,1)} all-gather(bf16[256,320]{1,0:T(8,128)(2,1)} %get-tuple-element.31), channel_id=3, replica_groups=mesh['dp'=2,'row'=4,'col'=4] {'row'}, dimensions={0}, use_global_device_ids=true | all-gather | bytes 819200 | tf_op jit(solution)/shard_map/all_gather | solution.py:554
  96.0 1.1 pad_maximum_fusion.2
  97.1 3.5 all-to-all-start.1
  100.6 10.0 %all-gather.5 = f32[4,1,256]{2,1,0:T(1,128)} all-gather(f32[1,1,256]{2,1,0:T(1,128)S(1)} %bitcast.92), channel_id=1, replica_groups=mesh['dp'=2,'row'=4,'col'=4] {'col'}, dimensions={0}, use_global_device_ids=true | all-gather | bytes 5120 | tf_op jit(solution)/shard_map/all_gather | solution.py:529
  110.7 3.1 slice.66.w_out_ref
  113.8 2.2 pad_dynamic-slice_fusion.kf_ref
  116.0 24.2 %shard_map.205 = (bf16[256,1024]{1,0:T(8,128)(2,1)}, f32[16,8,256]{2,1,0:T(8,128)}, bf16[1280,1024]{1,0:T(8,128)(2,1)}, bf16[1280,1024]{1,0:T(8,128)(2,1)}) custom-call(bf16[256,1024]{1,0:T(8,128)(2,1)} %get-tuple-element.30.q_ref, bf16[1280,320]{1,0:T(8,128)(2,1)} %pad_dynamic-slice_fusion.kf_ref, s32[1,1280]{1,0:T(1,128)} %get-tuple-element.53.seg_ref), custom_call_target="tpu_custom_call" | custom-call | flops 10737418240 | bytes 16777216 | tf_op jit(solution)/shard_map/pallas_call | solution.py:208
  140.3 58.8 %all-gather.14.cloned.1.call-done = bf16[33792,256]{1,0:T(8,128)(2,1)} async-done(((bf16[2112,256]{1,0:T(8,128)(2,1)}), bf16[33792,256]{1,0:T(8,128)(2,1)}) %all-gather.14.cloned.1.call-update) | async-done | bytes 17301520 | tf_op jit(solution)/shard_map/all_gather | solution.py:519
  199.0 25.7 %shard_map.206 = (bf16[256,1024]{1,0:T(8,128)(2,1)}, f32[256,1024]{1,0:T(8,128)}, bf16[256,1024]{1,0:T(8,128)(2,1)}, bf16[4,4,256,256]{3,2,1,0:T(8,128)(2,1)}, f...) custom-call(bf16[4,256,256]{2,1,0:T(8,128)(2,1)} %all-to-all-done.x_ref, bf16[4,256,256]{2,1,0:T(8,128)(2,1)} %copy-done.6, ...), custom_call_target="tpu_custom_call" | custom-call | flops 13287555072 | bytes 41943040 | tf_op jit(solution)/shard_map/pallas_call | solution.py:399
  224.8 35.5 %shard_map.207 = (f32[256,1024]{1,0:T(8,128)}, bf16[1280,320]{1,0:T(8,128)(2,1)}) custom-call(bf16[256,1024]{1,0:T(8,128)(2,1)} %get-tuple-element.30.q_ref, bf16[1280,1024]{1,0:T(8,128)(2,1)} %get-tuple-element.34.k_ref, bf16[1280,1024]{1,0:T(8,128)(2,1)} %get-tuple-element.35.v_ref, bf16[256,1024]{1,0:T(8,128)(2,1)} %get-tuple-element.36.do_ref, ...), custom_call_target="tpu_custom_call" | custom-call | flops 26843545600 | bytes 16777216 | tf_op jit(solution)/shard_map/pallas_call | solution.py:286
  260.5 1.0 copy-done.4
  261.7 1.3 slice.67
  263.1 35.4 %reduce-scatter.5.cloned.1.call-done = bf16[1,2,256,320]{3,2,1,0:T(8,128)(2,1)} async-done(((bf16[4,2,256,320]{3,2,1,0:T(8,128)(2,1)}), bf16[1,2,256,320]{3,2,1,0:T(8,128)(2,1)}) %reduce-scatter.5.cloned.1.call-update) | async-done | bytes 327696 | tf_op jit(solution)/shard_map/reduce_scatter | solution.py:568
  298.6 8.8 %reduce-scatter.7.cloned.1.call-done = bf16[1,256,320]{2,1,0:T(8,128)(2,1)} async-done(((bf16[2,256,320]{2,1,0:T(8,128)(2,1)}), bf16[1,256,320]{2,1,0:T(8,128)(2,1)}) %reduce-scatter.7.cloned.1.call-update) | async-done | bytes 163856 | tf_op jit(solution)/shard_map/reduce_scatter | solution.py:569
  307.4 9.7 %shard_map.208 = (f32[4,256,256]{2,1,0:T(8,128)}, f32[1,1024]{1,0:T(1,128)}, bf16[800,1024]{1,0:T(8,128)(2,1)}) custom-call(f32[256,1024]{1,0:T(8,128)} %get-tuple-element.38.dq_ref, bf16[256,320]{1,0:T(8,128)(2,1)} %bitcast.96, f32[256,160]{1,0:T(8,128)} %get-tuple-element.40.hf_ref, f32[256,384]{1,0:T(8,128)} %get-tuple-element.41.bq_ref, ...), custom_call_target="tpu_custom_call" | custom-call | flops 2516582400 | bytes 12582912 | tf_op jit(solution)/shard_map/pallas_call | solution.py:483
  317.1 1.4 slice.52
  318.5 1.0 slice.53
  319.5 1.0 reshape.119
  321.2 3.2 pad_maximum_fusion
  324.5 0.7 reduce-scatter.11.cloned.1.call-update
  325.2 70.3 %reduce-scatter.9.cloned.1.call-done = bf16[1,456,256]{2,1,0:T(8,128)(2,1)} async-done(((bf16[16,456,256]{2,1,0:T(8,128)(2,1)}), bf16[1,456,256]{2,1,0:T(8,128)(2,1)}) %reduce-scatter.9.cloned.1.call-update) | async-done | bytes 233488 | tf_op jit(solution)/shard_map/reduce_scatter | solution.py:587
  395.5 186.8 %reduce-scatter.11.cloned.1.call-done = bf16[1,2112,256]{2,1,0:T(8,128)(2,1)} async-done(((bf16[16,2112,256]{2,1,0:T(8,128)(2,1)}), bf16[1,2112,256]{2,1,0:T(8,128)(2,1)}) %reduce-scatter.11.cloned.1.call-update) | async-done | bytes 1081360 | tf_op jit(solution)/shard_map/reduce_scatter | solution.py:587
  582.4 11.4 %all_to_all.20 = bf16[4,256,256]{2,1,0:T(8,128)(2,1)S(1)} all-to-all(bf16[4,256,256]{2,1,0:T(8,128)(2,1)S(1)} %bitcast.72), channel_id=1, replica_groups=mesh['dp'=2,'row'=4,'col'=4] {'col'}, dimensions={0} | all-to-all | bytes 1048576 | tf_op jit(solution)/shard_map/all_to_all | solution.py:576
  593.8 3.5 all-to-all-start.3
  597.4 46.8 %psum.21 = f32[2,1024]{1,0:T(2,128)S(1)} all-reduce(f32[2,1024]{1,0:T(2,128)S(1)} %pad_maximum_fusion.4), channel_id=1, replica_groups=mesh['dp'=2,'row'=4,'col'=4] {'dp','row','col'}, use_global_device_ids=true, to_apply=%region_3.4 | all-reduce | flops 2048 | bytes 16384 | tf_op jit(solution)/shard_map/psum | solution.py:593
  644.2 0.6 fusion.3
  644.9 1.5 convert_element_type.19
  646.4 0.9 slice.73
  647.3 0.7 slice.70
  648.1 1.2 slice_bitcast_fusion.1
  649.3 0.7 slice_bitcast_fusion.3
  650.6 0.6 reshape.122
  651.2 0.8 copy.87
  652.0 1.0 copy.88
  (77 shorter events, 4.9 us)
Async XLA Ops:
  7.2 8.0 %copy-start = (s32[2,1,2048]{2,1,0:T(1,128)S(1)}, s32[2,1,2048]{2,1,0:T(1,128)}, u32[]{:S(2)}) copy-start(s32[2,1,2048]{2,1,0:T(1,128)} %param.14) | copy-start | bytes 49156
  7.2 10.6 %copy-start.12 = (f32[256]{0:T(256)S(1)}, f32[256]{0:T(256)}, u32[]{:S(2)}) copy-start(f32[256]{0:T(256)} %param.15) | copy-start | bytes 3076
  7.2 55.3 %all-gather.10.cloned.1.call-start = ((), (), s32[]{:S(2)}) async-start(), calls=%async_computation.12 | async-start | bytes 3969024 | tf_op jit(solution)/shard_map/all_gather | solution.py:518
  11.0 60.3 %all-to-all-start = ((bf16[4,256,256]{2,1,0:T(8,128)(2,1)}), bf16[4,256,256]{2,1,0:T(8,128)(2,1)}, u32[]{:S(2)}, u32[]{:S(2)}) async-start(bf16[4,256,256]{2,1,0:T(8,128)(2,1)} %bitcast.78), calls=%async_computation | async-start | bytes 1048576 | tf_op jit(solution)/shard_map/all_to_all | solution.py:532
  15.2 98.6 %all-gather.12.cloned.1.call-start = ((), (), s32[]{:S(2)}) async-start(), calls=%async_computation.13 | async-start | bytes 2359296 | tf_op jit(solution)/shard_map/all_gather | solution.py:555
  71.2 24.7 %copy-start.7 = (bf16[704,256]{1,0:T(8,128)(2,1)S(1)}, bf16[704,256]{1,0:T(8,128)(2,1)}, u32[]{:S(2)}) copy-start(bf16[704,256]{1,0:T(8,128)(2,1)} %param.22) | copy-start | bytes 1081348
  71.2 24.8 %copy-start.8 = (bf16[256,704]{0,1:T(8,128)(2,1)S(1)}, bf16[256,704]{0,1:T(8,128)(2,1)}, u32[]{:S(2)}) copy-start(bf16[256,704]{0,1:T(8,128)(2,1)} %param.21) | copy-start | bytes 1081348
  71.2 24.8 %copy-start.9 = (bf16[256,704]{0,1:T(8,128)(2,1)S(1)}, bf16[256,704]{0,1:T(8,128)(2,1)}, u32[]{:S(2)}) copy-start(bf16[256,704]{0,1:T(8,128)(2,1)} %param.20) | copy-start | bytes 1081348
  95.9 103.1 %all-gather.14.cloned.1.call-start = ((), (), s32[]{:S(2)}) async-start(), calls=%async_computation.14 | async-start | bytes 18382848 | tf_op jit(solution)/shard_map/all_gather | solution.py:519
  96.0 4.6 copy-start.13
  97.1 43.2 %all-to-all-start.1 = ((bf16[4,256,256]{2,1,0:T(8,128)(2,1)}), bf16[4,256,256]{2,1,0:T(8,128)(2,1)S(1)}, u32[]{:S(2)}, u32[]{:S(2)}) async-start(bf16[4,256,256]{2,1,0:T(8,128)(2,1)} %bitcast.1), calls=%async_computation.1 | async-start | bytes 1048576 | tf_op jit(solution)/shard_map/all_to_all | solution.py:532
  100.6 198.0 %reduce-scatter.5.cloned.1.call-start = ((), (), s32[]{:S(2)}) async-start(), calls=%async_computation.8 | async-start | bytes 1966080 | tf_op jit(solution)/shard_map/reduce_scatter | solution.py:568
  140.3 58.8 %copy-start.6 = (bf16[4,256,256]{2,1,0:T(8,128)(2,1)}, bf16[4,256,256]{2,1,0:T(8,128)(2,1)S(1)}, u32[]{:S(2)}) copy-start(bf16[4,256,256]{2,1,0:T(8,128)(2,1)S(1)} %all-to-all-done.1.cot_ref) | copy-start | bytes 1572868
  260.3 1.2 copy-start.4
  263.1 44.3 %reduce-scatter.7.cloned.1.call-start = ((), (), s32[]{:S(2)}) async-start(), calls=%async_computation.9 | async-start | bytes 589824 | tf_op jit(solution)/shard_map/reduce_scatter | solution.py:569
  298.6 97.0 %reduce-scatter.9.cloned.1.call-start = ((), (), s32[]{:S(2)}) async-start(), calls=%async_computation.10 | async-start | bytes 3969024 | tf_op jit(solution)/shard_map/reduce_scatter | solution.py:587
  324.4 257.9 %reduce-scatter.11.cloned.1.call-start = ((), (), s32[]{:S(2)}) async-start(), calls=%async_computation.11 | async-start | bytes 18382848 | tf_op jit(solution)/shard_map/reduce_scatter | solution.py:587
  324.4 257.9 %copy-start.5 = (bf16[256,1024]{1,0:T(8,128)(2,1)S(1)}, bf16[256,1024]{1,0:T(8,128)(2,1)}, u32[]{:S(2)}) copy-start(bf16[256,1024]{1,0:T(8,128)(2,1)} %get-tuple-element.33) | copy-start | bytes 1572868
  325.2 319.7 %all-reduce.5.cloned.1.call-start = ((), (), s32[]{:S(2)}) async-start(), calls=%async_computation.15 | async-start | bytes 2629632 | tf_op jit(solution)/shard_map/psum | solution.py:588
  582.3 15.0 %copy-start.14 = (s32[10]{0:T(128)S(1)}, s32[10]{0:T(128)}, u32[]{:S(2)}) copy-start(s32[10]{0:T(128)} %constant.77) | copy-start | bytes 124
  582.4 15.0 %copy-start.10 = (f32[1,1024]{1,0:T(1,128)S(1)}, f32[1,1024]{1,0:T(1,128)}, u32[]{:S(2)}) copy-start(f32[1,1024]{1,0:T(1,128)} %get-tuple-element.46) | copy-start | bytes 12292
  582.4 15.0 %copy-start.11 = (f32[1,1024]{1,0:T(1,128)S(1)}, f32[1,1024]{1,0:T(1,128)}, u32[]{:S(2)}) copy-start(f32[1,1024]{1,0:T(1,128)} %get-tuple-element.45) | copy-start | bytes 12292
  593.8 51.0 %all-to-all-start.3 = ((f32[4,256,256]{2,1,0:T(8,128)}), f32[4,256,256]{2,1,0:T(8,128)S(1)}, u32[]{:S(2)}, u32[]{:S(2)}) async-start(f32[4,256,256]{2,1,0:T(8,128)} %get-tuple-element.44), calls=%async_computation.5 | async-start | bytes 2097152 | tf_op jit(solution)/shard_map/all_to_all | solution.py:577
  644.8 1.6 copy-start.2
  644.8 2.5 copy-start.3
  648.1 4.9 copy-start.1
Sparse Core Ops, SparseCore 0:
  11.1 51.3 all-gather.9
  96.0 8.5 all-gather.11
  106.3 92.7 all-gather.13
  263.2 35.2 reduce-scatter.4
  300.6 6.7 reduce-scatter.6
  324.5 70.9 reduce-scatter.8
  399.7 182.6 reduce-scatter.10
  584.6 45.5 all-reduce.4

commit v2 on v1

--- a/solution.py
+++ b/solution.py
@@ -299,121 +299,533 @@
     )(q, k, v, d_heads, lse, kf_window, seg_window)
 
 
-def middle_body(
-    x_ref, cot_ref, heads_ref, w_out_ref, gain_ref, w_ref,
-    out_ref, d_mixed_ref, d_heads_ref, g_out_ref, g_gain_ref, g_ref,
-    mixed_ref, h_ref, scale_ref, sum_ref, back_ref, cot_all_ref,
+MESH = pl.DeviceIdType.MESH
+ANY = pl.BlockSpec(memory_space=pl.ANY)
+
+
+class Mover:
+    def __init__(self, send_sem, recv_sem):
+        self.send_sem = send_sem
+        self.recv_sem = recv_sem
+        self.used = 0
+
+    def copy(self, source, target, **place):
+        index = self.used
+        self.used += 1
+        return pltpu.make_async_remote_copy(
+            src_ref=source,
+            dst_ref=target,
+            send_sem=self.send_sem.at[index],
+            recv_sem=self.recv_sem.at[index],
+            device_id=place,
+            device_id_type=MESH,
+        )
+
+
+def greet(partners):
+    barrier = pltpu.get_barrier_semaphore()
+    count = 0
+    for present, place in partners:
+        if present is None:
+            pl.semaphore_signal(barrier, inc=1, device_id=place, device_id_type=MESH)
+            count = count + 1
+        else:
+
+            @pl.when(present)
+            def _():
+                pl.semaphore_signal(barrier, inc=1, device_id=place, device_id_type=MESH)
+
+            count = count + present.astype(jnp.int32)
+    pl.semaphore_wait(barrier, count)
+
+
+def neighbours():
+    col = lax.axis_index("col")
+    core = col + 1 - 2 * lax.rem(col, 2)
+    across = lax.rem(col + 2, 4)
+    return col, core, across
+
+
+def comm_params(ident):
+    return params(collective_id=ident, has_side_effects=True)
+
+
+GATHER_CHUNKS = 4
+
+
+def col_gather_body(x_ref, out_ref, send_sem, recv_sem, local_sem):
+    col, core, across = neighbours()
+    greet([(None, {"col": core}), (None, {"col": across})])
+    mover = Mover(send_sem, recv_sem)
+    size = x_ref.shape[0] // GATHER_CHUNKS
+    rows = [pl.ds(k * size, size) for k in range(GATHER_CHUNKS)]
+    far = [mover.copy(x_ref.at[r], out_ref.at[col, r], col=across) for r in rows]
+    for c in far:
+        c.start()
+    near = mover.copy(x_ref, out_ref.at[col], col=core)
+    near.start()
+    own = pltpu.make_async_copy(x_ref, out_ref.at[col], local_sem)
+    own.start()
+    passed = []
+    for k, r in enumerate(rows):
+        far[k].wait_recv()
+        c = mover.copy(out_ref.at[across, r], out_ref.at[across, r], col=core)
+        c.start()
+        passed.append(c)
+    for c in far:
+        c.wait_send()
+    near.wait()
+    own.wait()
+    for c in passed:
+        c.wait()
+
+
+def col_gather(x, ident):
+    count = 2 * GATHER_CHUNKS + 1
+    return pl.pallas_call(
+        col_gather_body,
+        out_shape=jax.ShapeDtypeStruct((4,) + x.shape, x.dtype),
+        in_specs=[ANY],
+        out_specs=ANY,
+        scratch_shapes=[
+            pltpu.SemaphoreType.DMA((count,)),
+            pltpu.SemaphoreType.DMA((count,)),
+            pltpu.SemaphoreType.DMA,
+        ],
+        compiler_params=comm_params(ident),
+        cost_estimate=cost_of(0, 3 << 20),
+    )(x)
+
+
+REDUCE_CHUNKS = 4
+
+
+def col_reduce_body(
+    dh_ref, out_ref, dh_sum_ref, out_sum_ref, near_ref, far_ref, pair_ref, send_sem, recv_sem
 ):
-    step = pl.program_id(0)
-    steps = pl.num_programs(0)
+    col, core, across = neighbours()
+    cross = lax.rem(core + 2, 4)
+    greet([(None, {"col": core}), (None, {"col": across})])
+    mover = Mover(send_sem, recv_sem)
+    size = dh_ref.shape[1] // REDUCE_CHUNKS
+    near = []
+    for index, source in enumerate((dh_ref, out_ref)):
+        pieces = []
+        for k in range(REDUCE_CHUNKS):
+            rows = pl.ds(k * size, size)
+            c = mover.copy(source.at[cross, rows], near_ref.at[index, 1, rows], col=core)
+            c.start()
+            pieces.append(c)
+        mine = mover.copy(source.at[core], near_ref.at[index, 0], col=core)
+        mine.start()
+        near.append((pieces, mine))
+    far = []
+    for index, source in enumerate((dh_ref, out_ref)):
+        for k in range(REDUCE_CHUNKS):
+            rows = pl.ds(k * size, size)
+            near[index][0][k].wait_recv()
+            pair_ref[index, rows] = (
+                source[across, rows].astype(F32) + near_ref[index, 1, rows].astype(F32)
+            ).astype(BF)
+            c = mover.copy(pair_ref.at[index, rows], far_ref.at[index, rows], col=across)
+            c.start()
+            far.append(c)
+    for index, (source, target) in enumerate(((dh_ref, dh_sum_ref), (out_ref, out_sum_ref))):
+        near[index][1].wait_recv()
+        for k in range(REDUCE_CHUNKS):
+            rows = pl.ds(k * size, size)
+            far[index * REDUCE_CHUNKS + k].wait_recv()
+            target[rows] = (
+                source[col, rows].astype(F32)
+                + near_ref[index, 0, rows].astype(F32)
+                + far_ref[index, rows].astype(F32)
+            )
+    for pieces, mine in near:
+        for c in pieces:
+            c.wait_send()
+        mine.wait_send()
+    for c in far:
+        c.wait_send()
+
+
+def col_reduce(dh_parts, out_parts):
+    rows = dh_parts.shape[1]
+    count = 2 * (2 * REDUCE_CHUNKS + 1)
+    total = jax.ShapeDtypeStruct((rows, D), F32)
+    return pl.pallas_call(
+        col_reduce_body,
+        out_shape=(total, total),
+        in_specs=[VMEM, VMEM],
+        out_specs=(VMEM, VMEM),
+        scratch_shapes=[
+            pltpu.VMEM((2, 2, rows, D), BF),
+            pltpu.VMEM((2, rows, D), BF),
+            pltpu.VMEM((2, rows, D), BF),
+            pltpu.SemaphoreType.DMA((count,)),
+            pltpu.SemaphoreType.DMA((count,)),
+        ],
+        compiler_params=comm_params(2),
+        cost_estimate=cost_of(0, 6 << 20),
+    )(dh_parts, out_parts)
+
+
+def row_partners(row, n_row, core):
+    return [
+        (None, {"col": core}),
+        (row + 1 < n_row, {"row": row + 1}),
+        (row + 2 < n_row, {"row": row + 2}),
+        (row >= 1, {"row": row - 1}),
+        (row >= 2, {"row": row - 2}),
+    ]
+
+
+def window_body(n_row, x_ref, zero_ref, win_ref, send_sem, recv_sem, local_sem):
+    row = lax.axis_index("row")
+    col, core, _ = neighbours()
+    side = lax.rem(col, 2)
+    greet(row_partners(row, n_row, core))
+    mover = Mover(send_sem, recv_sem)
+    one = mover.copy(x_ref, win_ref.at[2], row=row + 1)
+    two = mover.copy(x_ref, win_ref.at[0], row=row + 2)
+    near = mover.copy(x_ref, win_ref.at[3], col=core)
+    pass_one = mover.copy(win_ref.at[2], win_ref.at[1 + 2 * side], col=core)
+    pass_two = mover.copy(win_ref.at[0], win_ref.at[1], col=core)
+    has_one = row >= 1
+    has_two = row >= 2
+
+    @pl.when(row + 1 < n_row)
+    def _():
+        one.start()
+
+    @pl.when(row + 2 < n_row)
+    def _():
+        two.start()
+
+    @pl.when(side == 0)
+    def _():
+        near.start()
+
+    own = pltpu.make_async_copy(x_ref, win_ref.at[4], local_sem.at[0])
+    own.start()
+
+    def fill(slot):
+        return pltpu.make_async_copy(zero_ref, win_ref.at[slot], local_sem.at[slot + 1])
+
+    for absent, slots in (
+        (jnp.logical_not(has_two), (0,)),
+        (jnp.logical_and(jnp.logical_not(has_two), side == 0), (1,)),
+        (jnp.logical_and(jnp.logical_not(has_one), side == 1), (1,)),
+        (jnp.logical_not(has_one), (2,)),
+        (jnp.logical_and(jnp.logical_not(has_one), side == 0), (3,)),
+    ):
+
+        @pl.when(absent)
+        def _():
+            for slot in slots:
+                c = fill(slot)
+                c.start()
+                c.wait()
+
+    @pl.when(has_one)
+    def _():
+        one.wait_recv()
+        pass_one.start()
+
+    @pl.when(has_two)
+    def _():
+        two.wait_recv()
+
+    sends_two = jnp.logical_and(has_two, side == 1)
+    takes_two = jnp.logical_and(has_two, side == 0)
+
+    @pl.when(sends_two)
+    def _():
+        pass_two.start()
+
+    @pl.when(has_one)
+    def _():
+        pass_one.wait_recv()
+        pass_one.wait_send()
+
+    @pl.when(takes_two)
+    def _():
+        pass_two.wait_recv()
+
+    @pl.when(sends_two)
+    def _():
+        pass_two.wait_send()
+
+    @pl.when(side == 1)
+    def _():
+        near.wait_recv()
+
+    @pl.when(side == 0)
+    def _():
+        near.wait_send()
+
+    @pl.when(row + 1 < n_row)
+    def _():
+        one.wait_send()
+
+    @pl.when(row + 2 < n_row)
+    def _():
+        two.wait_send()
+
+    own.wait()
+
+
+def window(x, n_row):
+    zero = jnp.zeros(x.shape, x.dtype)
+    return pl.pallas_call(
+        functools.partial(window_body, n_row),
+        out_shape=jax.ShapeDtypeStruct((5,) + x.shape, x.dtype),
+        in_specs=[ANY, ANY],
+        out_specs=ANY,
+        scratch_shapes=[
+            pltpu.SemaphoreType.DMA((5,)),
+            pltpu.SemaphoreType.DMA((5,)),
+            pltpu.SemaphoreType.DMA((6,)),
+        ],
+        compiler_params=comm_params(3),
+        cost_estimate=cost_of(0, 1 << 20),
+    )(x, zero)
+
+
+def window_back_body(n_row, win_ref, sum_ref, near_ref, send_ref, far_ref, send_sem, recv_sem):
+    row = lax.axis_index("row")
+    col, core, _ = neighbours()
+    side = lax.rem(col, 2)
+    greet(row_partners(row, n_row, core))
+    mover = Mover(send_sem, recv_sem)
+    first = mover.copy(win_ref.at[1], near_ref.at[0], col=core)
+    second = mover.copy(win_ref.at[3], near_ref.at[1], col=core)
+    first.start()
+    second.start()
+    one = mover.copy(send_ref.at[0], far_ref.at[0], row=row - 1)
+    two = mover.copy(send_ref.at[1], far_ref.at[1], row=row - 2)
+    first.wait_recv()
+    second.wait_recv()
+    zero = jnp.zeros(near_ref.shape[1:], F32)
+    low = near_ref[0].astype(F32)
+    high = near_ref[1].astype(F32)
+    left = side == 0
+    send_ref[0] = (win_ref[2].astype(F32) + jnp.where(left, low, high)).astype(BF)
+    send_ref[1] = (win_ref[0].astype(F32) + jnp.where(left, zero, low)).astype(BF)
+
+    @pl.when(row >= 1)
+    def _():
+        one.start()
+
+    @pl.when(row >= 2)
+    def _():
+        two.start()
+
+    sum_ref[...] = win_ref[4].astype(F32) + jnp.where(left, high, zero)
+
+    @pl.when(row + 1 < n_row)
+    def _():
+        one.wait_recv()
+        sum_ref[...] += far_ref[0].astype(F32)
+
+    @pl.when(row + 2 < n_row)
+    def _():
+        two.wait_recv()
+        sum_ref[...] += far_ref[1].astype(F32)
+
+    first.wait_send()
+    second.wait_send()
+
+    @pl.when(row >= 1)
+    def _():
+        one.wait_send()
+
+    @pl.when(row >= 2)
+    def _():
+        two.wait_send()
+
+
+def window_back(win, n_row):
+    shape = win.shape[1:]
+    return pl.pallas_call(
+        functools.partial(window_back_body, n_row),
+        out_shape=jax.ShapeDtypeStruct(shape, F32),
+        in_specs=[VMEM],
+        out_specs=VMEM,
+        scratch_shapes=[
+            pltpu.VMEM((2,) + shape, BF),
+            pltpu.VMEM((2,) + shape, BF),
+            pltpu.VMEM((2,) + shape, BF),
+            pltpu.SemaphoreType.DMA((4,)),
+            pltpu.SemaphoreType.DMA((4,)),
+        ],
+        compiler_params=comm_params(4),
+        cost_estimate=cost_of(0, 1 << 20),
+    )(win)
+
+
+def mixing_body(x_ref, heads_ref, w_out_ref, gain_ref, mixed_ref, h_ref):
     parts, _, feat = x_ref.shape
     rows_of = w_out_ref.shape[0]
     head_rows = w_out_ref.shape[2]
-    hidden_size = w_ref.shape[2] // 3
-
-    def lanes_of(c):
-        return slice(c * feat, (c + 1) * feat)
-
-    @pl.when(step == 0)
-    def _():
-        total = None
+    total = None
+    for c in range(parts):
+        lanes = slice(c * feat, (c + 1) * feat)
+        acc = x_ref[c].astype(F32)
+        for r in range(rows_of):
+            acc = acc + nn(heads_ref[:, r * head_rows : (r + 1) * head_rows], w_out_ref[r, c])
+        mixed_ref[:, lanes] = acc
+        part = jnp.sum(acc * acc, axis=1, keepdims=True)
+        total = part if total is None else total + part
+    scale = lax.rsqrt(total / D + EPS)
+    h_ref[...] = (mixed_ref[...] * scale * gain_ref[...]).astype(BF)
+
+
+def mixing(x_parts, heads, w_out, gain):
+    rows = heads.shape[0]
+    return call(
+        mixing_body,
+        (jax.ShapeDtypeStruct((rows, D), F32), jax.ShapeDtypeStruct((rows, D), BF)),
+        cost=cost_of(2 * rows * D * D, 5 << 20),
+    )(x_parts, heads, w_out, gain)
+
+
+def ffn_body(pieces, split, *refs):
+    h_ref, cot_ref = refs[:2]
+    w_refs = refs[2 : 2 + pieces]
+    outs = refs[2 + pieces :]
+    out_ref, back_ref = outs[:2]
+    if split:
+        keep_ref, send_ref, down_ref = outs[2:5]
+        w_ref, dg_ref, du_ref, hid_ref, sems = outs[5:]
+    else:
+        g_ref = outs[2]
+        w_ref, dg_ref, du_ref, hid_ref, sems = outs[3:]
+    parts, rows, _ = h_ref.shape
+    copies = []
+    if split:
+        dp = lax.axis_index("dp")
+        units = w_refs[0].shape[1]
+        wide = D // 2
+        copies.append(pltpu.make_async_copy(w_refs[0], w_ref.at[:, pl.ds(0, units)], sems.at[0]))
+        for k in range(1, pieces):
+            slot = 1 + (k - 1) % 3
+            first = dp if k <= 3 else 1 - dp
+            lanes = pl.ds(pl.multiple_of(first * wide, wide), wide)
+            copies.append(
+                pltpu.make_async_copy(
+                    w_refs[k], w_ref.at[:, pl.ds(slot * units, units), lanes], sems.at[k]
+                )
+            )
+    else:
+        copies.append(pltpu.make_async_copy(w_refs[0], w_ref, sems.at[0]))
+    for c in copies:
+        c.start()
+    for c in copies:
+        c.wait()
+
+    def block(t, carried):
+        gate = nt(h_ref[t], w_ref[0])
+        up = nt(h_ref[t], w_ref[1])
+        d_hidden = nt(cot_ref[t], w_ref[2])
+        sig = 1.0 / (1.0 + jnp.exp(-gate))
+        silu = gate * sig
+        hidden = (silu * up).astype(BF)
+        d_gate = (d_hidden * up * sig * (1.0 + gate * (1.0 - sig))).astype(BF)
+        d_up = (d_hidden * silu).astype(BF)
+        place = pl.ds(pl.multiple_of(t * rows, rows), rows)
+        hid_ref[place] = hidden
+        dg_ref[place] = d_gate
+        du_ref[place] = d_up
+        out_ref[t] = nn(hidden, w_ref[2]).astype(BF)
+        back_ref[t] = (nn(d_gate, w_ref[0]) + nn(d_up, w_ref[1])).astype(BF)
+        return carried
+
+    lax.fori_loop(0, parts, block, 0)
+    h_all = h_ref[...].reshape(parts * rows, D)
+    cot_all = cot_ref[...].reshape(parts * rows, D)
+    for place, (left, right) in enumerate(((dg_ref, h_all), (du_ref, h_all), (hid_ref, cot_all))):
+        grad = tn(left[...], right)
+        if not split:
+            g_ref[place] = grad.astype(BF)
+        elif place == 2:
+            for k in range(down_ref.shape[0]):
+                down_ref[k] = grad[k * units : (k + 1) * units].astype(BF)
+        else:
+            low = grad[:, :wide].astype(BF)
+            high = grad[:, wide:].astype(BF)
+            keep_ref[place] = jnp.where(dp == 0, low, high)
+            send_ref[place] = jnp.where(dp == 0, high, low)
+
+
+def ffn(h_all, cot_all, pieces, units, split):
+    parts, rows, _ = h_all.shape
+    tokens = parts * rows
+    outs = [jax.ShapeDtypeStruct((parts, rows, D), BF)] * 2
+    if split:
+        outs += [jax.ShapeDtypeStruct((2, units, D // 2), BF)] * 2
+        outs += [jax.ShapeDtypeStruct((4, units // 4, D), BF)]
+    else:
+        outs += [jax.ShapeDtypeStruct((3, units, D), BF)]
+    return pl.pallas_call(
+        functools.partial(ffn_body, len(pieces), split),
+        out_shape=tuple(outs),
+        in_specs=[VMEM, VMEM] + [ANY] * len(pieces),
+        scratch_shapes=[
+            pltpu.VMEM((3, units, D), BF),
+            pltpu.VMEM((tokens, units), BF),
+            pltpu.VMEM((tokens, units), BF),
+            pltpu.VMEM((tokens, units), BF),
+            pltpu.SemaphoreType.DMA((len(pieces),)),
+        ],
+        compiler_params=params(),
+        cost_estimate=cost_of(2 * tokens * 9 * D * units, 20 << 20),
+    )(h_all, cot_all, *pieces)
+
+
+def unmix_body(
+    mixed_ref, cot_ref, dh_ref, out_sum_ref, heads_ref, w_out_ref, gain_ref,
+    out_ref, d_mixed_ref, d_heads_ref, g_out_ref, g_gain_ref,
+):
+    parts, _, feat = cot_ref.shape
+    rows_of = w_out_ref.shape[0]
+    head_rows = w_out_ref.shape[2]
+    mixed = mixed_ref[...]
+    scale = lax.rsqrt(jnp.sum(mixed * mixed, axis=1, keepdims=True) / D + EPS)
+    normed = mixed * scale
+    d_h = dh_ref[...]
+    g_gain_ref[...] = jnp.sum(d_h * normed, axis=0, keepdims=True)
+    inner = d_h * gain_ref[...]
+    dot = jnp.sum(inner * normed, axis=1, keepdims=True) / D
+    cot = jnp.concatenate([cot_ref[c] for c in range(parts)], axis=1).astype(F32)
+    d_mixed = cot + scale * (inner - normed * dot)
+    d_mixed_ref[...] = d_mixed
+    low = d_mixed.astype(BF)
+    grad = tn(heads_ref[...], low)
+    for c in range(parts):
+        out_ref[c] = (mixed[:, c * feat : (c + 1) * feat] + out_sum_ref[:, c * feat : (c + 1) * feat]).astype(BF)
+    for r in range(rows_of):
+        acc = None
         for c in range(parts):
-            acc = x_ref[c].astype(F32)
-            for r in range(rows_of):
-                acc = acc + nn(heads_ref[:, r * head_rows : (r + 1) * head_rows], w_out_ref[r, c])
-            mixed_ref[:, lanes_of(c)] = acc
-            part = jnp.sum(acc * acc, axis=1, keepdims=True)
-            total = part if total is None else total + part
-            cot_all_ref[:, lanes_of(c)] = cot_ref[c]
-        scale = lax.rsqrt(total / D + EPS)
-        scale_ref[...] = jnp.broadcast_to(scale, scale_ref.shape)
-        h_ref[...] = (mixed_ref[...] * scale * gain_ref[...]).astype(BF)
-        sum_ref[...] = jnp.zeros_like(sum_ref)
-        back_ref[...] = jnp.zeros_like(back_ref)
-
-    gate = None
-    up = None
-    d_hidden = None
-    for c in range(parts):
-        h_part = h_ref[:, lanes_of(c)]
-        term_g = nt(h_part, w_ref[0, c, :hidden_size])
-        term_u = nt(h_part, w_ref[0, c, hidden_size : 2 * hidden_size])
-        term_d = nt(cot_ref[c], w_ref[0, c, 2 * hidden_size :])
-        gate = term_g if gate is None else gate + term_g
-        up = term_u if up is None else up + term_u
-        d_hidden = term_d if d_hidden is None else d_hidden + term_d
-    sig = 1.0 / (1.0 + jnp.exp(-gate))
-    silu = gate * sig
-    hidden = (silu * up).astype(BF)
-    d_gate = (d_hidden * up * sig * (1.0 + gate * (1.0 - sig))).astype(BF)
-    d_up = (d_hidden * silu).astype(BF)
-    for c in range(parts):
-        sum_ref[:, lanes_of(c)] += nn(hidden, w_ref[0, c, 2 * hidden_size :])
-        back_ref[:, lanes_of(c)] += nn(d_gate, w_ref[0, c, :hidden_size]) + nn(
-            d_up, w_ref[0, c, hidden_size : 2 * hidden_size]
-        )
-    for place, (left, right) in enumerate(((d_gate, h_ref), (d_up, h_ref), (hidden, cot_all_ref))):
-        grad = tn(left, right[...])
-        for c in range(parts):
-            g_ref[0, c, place * hidden_size : (place + 1) * hidden_size] = grad[:, lanes_of(c)].astype(BF)
-
-    @pl.when(step == steps - 1)
-    def _():
-        scale = scale_ref[:, :1]
-        mixed = mixed_ref[...]
-        out_ref[...] = (mixed + sum_ref[...]).astype(BF)
-        normed = mixed * scale
-        d_h = back_ref[...]
-        g_gain_ref[...] = jnp.sum(d_h * normed, axis=0, keepdims=True)
-        inner = d_h * gain_ref[...]
-        dot = jnp.sum(inner * normed, axis=1, keepdims=True) / D
-        d_mixed = cot_all_ref[...].astype(F32) + scale * (inner - normed * dot)
-        d_mixed_ref[...] = d_mixed
-        low = d_mixed.astype(BF)
-        grad = tn(heads_ref[...], low)
-        for r in range(rows_of):
-            acc = None
-            for c in range(parts):
-                term = nt(low[:, lanes_of(c)], w_out_ref[r, c])
-                acc = term if acc is None else acc + term
-                g_out_ref[r, c] = grad[r * head_rows : (r + 1) * head_rows, lanes_of(c)].astype(BF)
-            d_heads_ref[:, r * head_rows : (r + 1) * head_rows] = acc.astype(BF)
-
-
-def middle(x_parts, cot_parts, heads, w_out, gain, w_ffn):
-    parts, rows, feat = x_parts.shape
-    steps = w_ffn.shape[0]
-    block = (1,) + w_ffn.shape[1:]
-
-    def whole(shape):
-        return pl.BlockSpec(shape, lambda r: (0,) * len(shape))
-
-    outs = (
-        jax.ShapeDtypeStruct((rows, D), BF),
-        jax.ShapeDtypeStruct((rows, D), F32),
-        jax.ShapeDtypeStruct((rows, D), BF),
-        jax.ShapeDtypeStruct(w_out.shape, BF),
-        jax.ShapeDtypeStruct((1, D), F32),
-        jax.ShapeDtypeStruct(w_ffn.shape, BF),
-    )
-    return pl.pallas_call(
-        middle_body,
-        grid=(steps,),
-        out_shape=outs,
-        in_specs=[whole(a.shape) for a in (x_parts, cot_parts, heads, w_out, gain)]
-        + [pl.BlockSpec(block, lambda r: (r, 0, 0, 0))],
-        out_specs=[whole(a.shape) for a in outs[:-1]] + [pl.BlockSpec(block, lambda r: (r, 0, 0, 0))],
-        scratch_shapes=(
-            pltpu.VMEM((rows, D), F32),
-            pltpu.VMEM((rows, D), BF),
-            pltpu.VMEM((rows, LANES), F32),
-            pltpu.VMEM((rows, D), F32),
-            pltpu.VMEM((rows, D), F32),
-            pltpu.VMEM((rows, D), BF),
+            lanes = slice(c * feat, (c + 1) * feat)
+            term = nt(low[:, lanes], w_out_ref[r, c])
+            acc = term if acc is None else acc + term
+            g_out_ref[r, c] = grad[r * head_rows : (r + 1) * head_rows, lanes].astype(BF)
+        d_heads_ref[:, r * head_rows : (r + 1) * head_rows] = acc.astype(BF)
+
+
+def unmix(mixed, cot_parts, dh, out_sum, heads, w_out, gain):
+    rows = heads.shape[0]
+    return call(
+        unmix_body,
+        (
+            jax.ShapeDtypeStruct(cot_parts.shape, BF),
+            jax.ShapeDtypeStruct((rows, D), F32),
+            jax.ShapeDtypeStruct((rows, D), BF),
+            jax.ShapeDtypeStruct(w_out.shape, BF),
+            jax.ShapeDtypeStruct((1, D), F32),
         ),
-        compiler_params=params(dimension_semantics=("arbitrary",)),
-        cost_estimate=cost_of(2 * rows * 3 * 3 * D * 2816, 40 << 20),
-    )(x_parts, cot_parts, heads, w_out, gain, w_ffn)
+        cost=cost_of(4 * rows * D * D, 10 << 20),
+    )(mixed, cot_parts, dh, out_sum, heads, w_out, gain)
 
 
 def back_body(
@@ -511,13 +923,12 @@
     past = min(-(-(MAX_DOC - 1) // rows), n_row * subs - 1)
     keys = (past + 1) * rows
 
+    fast = n_col == 4 and n_row == 4 and lax.axis_size("dp") == 2 and micro == 2 and past == 4
+
     heads_t = jnp.transpose(w_heads.reshape(feat, head_local, FAC), (2, 1, 0))
     heads_t = heads_t[jnp.array(FAC_ORDER)].reshape(FAC * head_local, feat)
     attn_local = jnp.concatenate([w_ranks.T, heads_t, w_out], axis=0)
-    ffn_block = jnp.concatenate([w_gate.T, w_up.T, w_down], axis=0)
     attn_all = lax.all_gather(attn_local, ("row", "col"), axis=0)
-    ffn_all = lax.all_gather(ffn_block, ("row", "col"), axis=0)
-    ffn_all = ffn_all.reshape(n_row, n_col, 3 * ffn_local, feat)
     attn_all = attn_all.reshape(n_row, n_col, attn_local.shape[0], feat)
     ranks_full = jnp.transpose(attn_all[:, :, :rank_local], (1, 3, 0, 2)).reshape(D, n_row * rank_local)
     heads_full = attn_all[:, :, rank_local : rank_local + FAC * head_local]
@@ -528,11 +939,32 @@
     gain_one = lax.all_gather(gain_attn, "col", axis=0, tiled=True).reshape(1, D)
     gain_two = lax.all_gather(gain_ffn, "col", axis=0, tiled=True).reshape(1, D)
 
+    part = ffn_local // n_col
+    units = part * n_row
+    w_ffn = jnp.stack([w_gate.T, w_up.T, w_down]).reshape(3, n_col, part, feat)
+    w_ffn = lax.all_to_all(jnp.transpose(w_ffn, (1, 0, 2, 3)), "col", 0, 0, tiled=True)
+    w_ffn = jnp.transpose(w_ffn, (1, 2, 0, 3)).reshape(3, part, D)
+
+    def row_swap(values, k):
+        return lax.ppermute(values, "row", [(r, r ^ k) for r in range(n_row)])
+
+    def dp_swap(values):
+        return lax.ppermute(values, "dp", [(0, 1), (1, 0)])
+
+    if fast:
+        dp = lax.axis_index("dp")
+        half = lax.dynamic_slice_in_dim(w_ffn, dp * (D // 2), D // 2, 2)
+        first = [row_swap(half, k) for k in range(1, n_row)]
+        pieces = [w_ffn] + first + [dp_swap(v) for v in first]
+    else:
+        pieces = [jnp.transpose(lax.all_gather(w_ffn, "row", axis=0), (1, 0, 2, 3)).reshape(3, units, D)]
+
     def own_tokens(values):
         return lax.all_to_all(values.reshape(n_col, rows, feat), "col", 0, 0, tiled=True)
 
     x_parts = own_tokens(tokens_in)
     cot_parts = own_tokens(cotangent)
+    cot_own = jnp.transpose(cot_parts, (1, 0, 2)).reshape(rows, D)
 
     seg_row = lax.dynamic_index_in_dim(segments, col // subs, 0, keepdims=False)
     padded = jnp.concatenate([jnp.full((1, past * rows), -1, jnp.int32), seg_row], axis=1)
@@ -551,48 +983,102 @@
     h_one, head_fac, bq_rot, key_fac, queries = front(x_parts, gain_one, w_rh, turn)
 
     groups = [[m * subs + s for s in range(subs)] for m in range(micro)]
-    gathered = lax.all_gather(key_fac, "row", axis=0)
-    gathered = lax.all_gather(gathered, "col", axis=1, axis_index_groups=groups)
-    gathered = gathered.reshape(length, key_fac.shape[1])
-    padded = jnp.concatenate([jnp.zeros((past * rows, key_fac.shape[1]), BF), gathered], axis=0)
-    kf_window = lax.dynamic_slice_in_dim(padded, block * rows, keys, 0)
+    if fast:
+        kf_window = window(key_fac, n_row).reshape(keys, -1)
+    else:
+        gathered = lax.all_gather(key_fac, "row", axis=0)
+        gathered = lax.all_gather(gathered, "col", axis=1, axis_index_groups=groups)
+        gathered = gathered.reshape(length, key_fac.shape[1])
+        padded_kf = jnp.concatenate([jnp.zeros((past * rows, key_fac.shape[1]), BF), gathered], axis=0)
+        kf_window = lax.dynamic_slice_in_dim(padded_kf, block * rows, keys, 0)
 
     heads_out, lse, key_all, value_all = attend(queries, kf_window, seg_window)
-    out_own, d_mixed, d_heads, g_out, g_gain_two, g_ffn = middle(
-        x_parts, cot_parts, heads_out, w_out_all, gain_two, ffn_all
+    mixed, h_two = mixing(x_parts, heads_out, w_out_all, gain_two)
+
+    if fast:
+        cot_all = col_gather(cot_own, 5)
+        h_all = col_gather(h_two, 1)
+    else:
+        cot_all = lax.all_gather(cot_own, "col", axis=0)
+        h_all = lax.all_gather(h_two, "col", axis=0)
+    out_part, dh_part, *g_parts = ffn(h_all, cot_all, pieces, units, fast)
+    if fast:
+        dh_sum, out_sum = col_reduce(dh_part, out_part)
+    else:
+        dh_sum = lax.psum_scatter(dh_part, "col", scatter_dimension=0, tiled=False).astype(F32)
+        out_sum = lax.psum_scatter(out_part, "col", scatter_dimension=0, tiled=False).astype(F32)
+    out_parts, d_mixed, d_heads, g_out, g_gain_two = unmix(
+        mixed, cot_parts, dh_sum, out_sum, heads_out, w_out_all, gain_two
     )
     d_q, d_kf = attend_back(queries, key_all, value_all, d_heads, lse, kf_window, seg_window)
 
-    spread_kf = lax.dynamic_update_slice_in_dim(jnp.zeros_like(padded), d_kf, block * rows, 0)[past * rows :]
-    spread_kf = spread_kf.reshape(n_row, subs, rows, -1)
-    own_kf = lax.psum_scatter(spread_kf, "row", scatter_dimension=0, tiled=False)
-    own_kf = lax.psum_scatter(own_kf, "col", scatter_dimension=0, tiled=False, axis_index_groups=groups)
+    if fast:
+        own_kf = window_back(d_kf.reshape(past + 1, rows, -1), n_row)
+    else:
+        spread_kf = jnp.zeros((past * rows + length, d_kf.shape[1]), BF)
+        spread_kf = lax.dynamic_update_slice_in_dim(spread_kf, d_kf, block * rows, 0)[past * rows :]
+        spread_kf = spread_kf.reshape(n_row, subs, rows, -1)
+        own_kf = lax.psum_scatter(spread_kf, "row", scatter_dimension=0, tiled=False)
+        own_kf = lax.psum_scatter(own_kf, "col", scatter_dimension=0, tiled=False, axis_index_groups=groups)
 
     gi_parts, g_gain_one, g_rh = back(
         d_q, own_kf, head_fac, bq_rot, turn, w_rh, h_one, x_parts, gain_one, d_mixed
     )
 
-    out_parts = jnp.transpose(out_own.reshape(rows, n_col, feat), (1, 0, 2))
     output = lax.all_to_all(out_parts, "col", 0, 0, tiled=True).reshape(tokens_in.shape)
     grad_input = lax.all_to_all(gi_parts, "col", 0, 0, tiled=True).reshape(tokens_in.shape)
+
+    def add(*values):
+        total = values[0].astype(F32)
+        for v in values[1:]:
+            total = total + v.astype(F32)
+        return total.astype(BF)
+
+    if fast:
+        keep, send, down = g_parts
+        both = add(keep, dp_swap(send)).reshape(2, n_row, part, D // 2)
+        low = add(down[0], *[row_swap(down[k], k) for k in range(1, n_row)])
+        both = add(both[:, 0], *[row_swap(both[:, k], k) for k in range(1, n_row)])
+        other = dp_swap(both)
+        both = jnp.where(dp == 0, jnp.concatenate([both, other], 2), jnp.concatenate([other, both], 2))
+        low = add(low, dp_swap(low))
+        g_ffn = jnp.concatenate([both, low[None]], axis=0)
+    else:
+        g_ffn = g_parts[0].reshape(3, n_row, part, D)
+        g_ffn = lax.psum_scatter(g_ffn, "row", scatter_dimension=1, tiled=False)
+        g_ffn = lax.psum(g_ffn, "dp")
+    g_ffn = jnp.transpose(g_ffn.reshape(3, part, n_col, feat), (2, 0, 1, 3))
+    g_ffn = lax.all_to_all(g_ffn, "col", 0, 0, tiled=True)
+    g_ffn = jnp.transpose(g_ffn, (1, 0, 2, 3)).reshape(3, ffn_local, feat).astype(F32)
 
     g_ranks = g_rh[: FAC * HD].reshape(n_row, rank_local, n_col, feat)
     g_heads = g_rh[FAC * HD :].reshape(FAC, n_row, head_local, n_col, feat)
     g_ranks = jnp.transpose(g_ranks, (0, 2, 1, 3))
     g_heads = jnp.transpose(g_heads, (1, 3, 0, 2, 4)).reshape(n_row, n_col, FAC * head_local, feat)
-    g_attn = jnp.concatenate([g_ranks, g_heads, g_out], axis=2)
+    g_rh = jnp.concatenate([g_ranks, g_heads], axis=2)
 
     def total(values):
+        if fast:
+            place = [
+                lax.dynamic_index_in_dim(values.reshape(n_row, 2, 2, *values.shape[2:]), (col + k) % 2, 2, False)
+                for k in range(2)
+            ]
+            values = add(place[0], lax.ppermute(place[1], "col", [(c, c ^ 1) for c in range(4)]))
+            place = [lax.dynamic_index_in_dim(values, (col // 2 + k) % 2, 1, False) for k in range(2)]
+            values = add(place[0], lax.ppermute(place[1], "col", [(c, c ^ 2) for c in range(4)]))
+            place = [lax.dynamic_index_in_dim(values, row ^ k, 0, False) for k in range(n_row)]
+            values = add(place[0], *[row_swap(place[k], k) for k in range(1, n_row)])
+            return add(values, dp_swap(values)).astype(F32)
         values = values.reshape((n_row * n_col,) + values.shape[2:])
         part = lax.psum_scatter(values, ("row", "col"), scatter_dimension=0, tiled=False)
         return lax.psum(part, "dp").astype(F32)
 
-    g_ffn = total(g_ffn)
-    g_attn = total(g_attn)
+    g_out = total(g_out)
+    g_rh = total(g_rh)
     gains = jnp.concatenate([g_gain_one, g_gain_two], axis=0)
     gains = lax.psum(gains, ("dp", "row", "col"))
     gains = lax.dynamic_slice_in_dim(gains, col * feat, feat, 1)
-    own_heads = g_attn[rank_local : rank_local + FAC * head_local].reshape(FAC, head_local, feat)
+    own_heads = g_rh[rank_local:].reshape(FAC, head_local, feat)
     own_heads = jnp.transpose(own_heads[jnp.array(FAC_BACK)], (2, 1, 0)).reshape(w_heads.shape)
     return (
         output,
@@ -600,11 +1086,11 @@
         gains[0],
         gains[1],
         own_heads,
-        g_attn[:rank_local].T,
-        g_attn[rank_local + FAC * head_local :],
-        g_ffn[:ffn_local].T,
-        g_ffn[ffn_local : 2 * ffn_local].T,
-        g_ffn[2 * ffn_local :],
+        g_rh[:rank_local].T,
+        g_out,
+        g_ffn[0].T,
+        g_ffn[1].T,
+        g_ffn[2],
     )
 
 

time: 661 us -> 514 us (0.78)
  waiting for transfers between devices: 397 us -> 68.7 us
  Pallas kernels: 100 us -> 236 us
  starting transfers between devices: 11.5 us -> 69.7 us
  blocking collectives: 95.6 us -> 55.2 us
  other arithmetic: 10.5 us -> 26.5 us
    reduce_scatter x4 -> x0, waiting for transfers between devices: 301 us -> none  [the longest x2 257 us: total(): lax.psum_scatter(values, ('row', 'col'), scatter_dimension=0, tiled=False)]
    pallas_call x1 -> x8, Pallas kernels: 25.7 us -> 161 us  [the longest x1 45.8 us: window(): pl.pallas_call(functools.partial(window_body, n_row), out_shape=jax.Shape...]
    all_gather x2 -> x0, waiting for transfers between devices: 58.8 us -> none  [the longest x1 58.8 us: local(): ffn_all = lax.all_gather(ffn_block, ('row', 'col'), axis=0)]
    ppermute x0 -> x27, waiting for transfers between devices: none -> 47.1 us  [the longest x15 22.2 us: row_swap(): return lax.ppermute(values, 'row', [(r, r ^ k) for r in range(n_row)])]
    ppermute x0 -> x27, starting transfers between devices: none -> 46.3 us  [the longest x8 23.7 us: dp_swap(): return lax.ppermute(values, 'dp', [(0, 1), (1, 0)])]
    all_gather x1, waiting for transfers between devices: 36.6 us -> 0.01 us  [local(): attn_all = lax.all_gather(attn_local, ('row', 'col'), axis=0)]
    all_to_all x0 -> x3, waiting for transfers between devices: none -> 21.6 us  [the longest x1 16.7 us: local(): lax.all_to_all(jnp.transpose(w_ffn, (1, 0, 2, 3)), 'col', 0, 0, tiled=True)]
    all_gather x1 -> x0, blocking collectives: 19.3 us -> none  [local(): gathered = lax.all_gather(key_fac, 'row', axis=0)]
  transfers between devices with their start and end apart: 11 -> 34, of which waited for: 6 -> 10; matrix products, arithmetic and copies ran while one was open for 3% -> 9% of each run, Pallas kernels for 4% -> 23%
where the time goes in v2:
time: 514 us; the launch traced here: 507 us
  Pallas kernels  236 us (46%)
  starting transfers between devices  69.7 us (14%)
  waiting for transfers between devices  68.7 us (13%)
  blocking collectives  55.2 us (11%)
  local copies, waits for them, and re-layouts  35.6 us (7%)
  other arithmetic  26.5 us (5%)
  between operations  14.9 us (3%)
    pallas_call x1, Pallas kernels, window(): pl.pallas_call(functools.partial(window_body, n_row), out_shape=jax.Shape...  45.8 us
    psum x1, blocking collectives, local(): gains = lax.psum(gains, ('dp', 'row', 'col'))  44.3 us
    pallas_call x2, Pallas kernels, col_gather(): pl.pallas_call(col_gather_body, out_shape=jax.ShapeDtypeStruct((4,) + x.s...  39.4 us
    pallas_call x1, Pallas kernels, attend_back(): call(attend_back_body, (jax.ShapeDtypeStruct((rows, D), F32), jax.ShapeDt...  35.3 us
    pallas_call x1, Pallas kernels, col_reduce(): pl.pallas_call(col_reduce_body, out_shape=(total, total), in_specs=[VMEM,...  29.4 us
    pallas_call x1, Pallas kernels, attend(): call(attend_body, (jax.ShapeDtypeStruct((rows, D), BF), jax.ShapeDtypeStr...  24.4 us
    ppermute x8, starting transfers between devices, dp_swap(): return lax.ppermute(values, 'dp', [(0, 1), (1, 0)])  23.7 us
    ppermute x15, waiting for transfers between devices, row_swap(): return lax.ppermute(values, 'row', [(r, r ^ k) for r in range(n_row)])  22.2 us
  transfers between devices with their start and end apart: 34, of which 10 were waited for; matrix products, arithmetic and copies ran while one was open for 9% of the time, Pallas kernels for 23%

profile of v2, /device:TPU:0, one launch (start us, length us, event | category | flops | bytes accessed | tf_op | source)
XLA Modules:
  0.0 506.5 jit_solution(987656695393846029)
XLA Ops:
  9.3 1.7 pad_maximum_fusion.1
  10.9 2.4 maximum_bitcast_fusion
  13.3 4.2 all-to-all-start.2
  18.1 16.7 %all-to-all-done.2 = bf16[4,3,176,256]{3,2,1,0:T(8,128)(2,1)S(1)} async-done(((bf16[4,3,176,256]{3,2,1,0:T(8,128)(2,1)}), bf16[4,3,176,256]{3,2,1,0:T(8,128)(2,1)S(1)}, u32[]{:S(2)}, u32[]{:S(2)}) %all-to-all-start.2) | async-done | bytes 1081376 | tf_op jit(solution)/shard_map/all_to_all | solution.py:945
  34.8 3.5 all-to-all-start.1
  39.5 2.4 collective-permute-start
  41.9 2.6 collective-permute-start.1
  46.4 5.2 %all-gather.1 = f32[4,1,256]{2,1,0:T(1,128)} all-gather(f32[1,1,256]{2,1,0:T(1,128)S(1)} %bitcast.175), channel_id=1, replica_groups=mesh['dp'=2,'row'=4,'col'=4] {'col'}, dimensions={0}, use_global_device_ids=true | all-gather | bytes 5120 | tf_op jit(solution)/shard_map/all_gather | solution.py:939
  51.6 5.6 %all-gather.2 = f32[4,1,256]{2,1,0:T(1,128)} all-gather(f32[1,1,256]{2,1,0:T(1,128)S(1)} %bitcast.176), channel_id=1, replica_groups=mesh['dp'=2,'row'=4,'col'=4] {'col'}, dimensions={0}, use_global_device_ids=true | all-gather | bytes 5120 | tf_op jit(solution)/shard_map/all_gather | solution.py:940
  57.3 4.1 all-to-all-start
  62.6 20.7 %shard_map.209.refs_1_ = bf16[4,256,1024]{2,1,0:T(8,128)(2,1)} custom-call(bf16[256,1024]{1,0:T(8,128)(2,1)} %copy.149.x_ref), custom_call_target="tpu_custom_call" | custom-call | bytes 3145728 | tf_op jit(solution)/shard_map/pallas_call | solution.py:385
  83.4 1.8 collective-permute-start.3
  85.2 10.1 %collective-permute-done.1.refs_4_ = bf16[3,176,512]{2,1,0:T(8,128)(2,1)} collective-permute-done((bf16[3,176,512]{2,1,0:T(8,128)(2,1)S(1)}, bf16[3,176,512]{2,1,0:T(8,128)(2,1)}, u32[]{:S(2)}, u32[]{:S(2)}) %collective-permute-start.1) | collective-permute-done | bytes 540704 | tf_op jit(solution)/shard_map/ppermute | solution.py:949
  103.8 2.5 pad_maximum_fusion.w_ref
  106.2 5.2 %shard_map.204 = (bf16[256,1024]{1,0:T(8,128)(2,1)}, f32[256,160]{1,0:T(8,128)}, f32[256,384]{1,0:T(8,128)}, bf16[256,320]{1,0:T(8,128)(2,1)}, bf16[256,1024]{1,0:T(8,128)(2,1)}) custom-call(bf16[4,256,256]{2,1,0:T(8,128)(2,1)} %all-to-all-done.x_ref, f32[1,1024]{1,0:T(1,128)} %bitcast.172, bf16[1024,800]{1,0:T(8,128)(2,1)} %pad_maximum_fusion.w_ref, ...), custom_call_target="tpu_custom_call" | custom-call | flops 1258291200 | bytes 6291456 | tf_op jit(solution)/shard_map/pallas_call | solution.py:140
  112.2 45.8 %shard_map.205 = bf16[5,256,320]{2,1,0:T(8,128)(2,1)} custom-call(bf16[256,320]{1,0:T(8,128)(2,1)} %get-tuple-element.39.x_ref, bf16[256,320]{1,0:T(8,128)(2,1)} %broadcast_in_dim.7.zero_ref), custom_call_target="tpu_custom_call" | custom-call | bytes 1048576 | tf_op jit(solution)/shard_map/pallas_call | solution.py:579
  158.0 24.4 %shard_map.206 = (bf16[256,1024]{1,0:T(8,128)(2,1)}, f32[16,8,256]{2,1,0:T(8,128)}, bf16[1280,1024]{1,0:T(8,128)(2,1)}, bf16[1280,1024]{1,0:T(8,128)(2,1)}) custom-call(bf16[256,1024]{1,0:T(8,128)(2,1)} %get-tuple-element.38.q_ref, bf16[1280,320]{1,0:T(8,128)(2,1)} %bitcast.158, s32[1,1280]{1,0:T(1,128)} %get-tuple-element.67.seg_ref), custom_call_target="tpu_custom_call" | custom-call | flops 10737418240 | bytes 16777216 | tf_op jit(solution)/shard_map/pallas_call | solution.py:208
  183.9 3.8 shard_map.207
  187.7 18.6 %shard_map.208.refs_0_ = bf16[4,256,1024]{2,1,0:T(8,128)(2,1)} custom-call(bf16[256,1024]{1,0:T(8,128)(2,1)} %get-tuple-element.42.x_ref), custom_call_target="tpu_custom_call" | custom-call | bytes 3145728 | tf_op jit(solution)/shard_map/pallas_call | solution.py:385
  206.3 21.1 %shard_map.210 = (bf16[4,256,1024]{2,1,0:T(8,128)(2,1)}, bf16[4,256,1024]{2,1,0:T(8,128)(2,1)}, bf16[2,704,512]{2,1,0:T(8,128)(2,1)}, bf16[2,704,512]{2,1,0:T(8,128)(2,1)}, bf16[4,176,1024]{2,1,0:T(8,128)(2,1)}) custom-call(bf16[4,256,1024]{2,1,0:T(8,128)(2,1)} %shard_map.208.refs_0_, bf16[4,256,1024]{2,1,0:T(8,128)(2,1)} %shard_map.209.refs_1_, ...), custom_call_target="tpu_custom_call" | custom-call | flops 13287555072 | bytes 20971520 | tf_op jit(solution)/shard_map/pallas_call | solution.py:769
  227.5 29.4 %shard_map.211 = (f32[256,1024]{1,0:T(8,128)}, f32[256,1024]{1,0:T(8,128)}) custom-call(bf16[4,256,1024]{2,1,0:T(8,128)(2,1)} %get-tuple-element.43.dh_ref, bf16[4,256,1024]{2,1,0:T(8,128)(2,1)} %get-tuple-element.44.out_ref), custom_call_target="tpu_custom_call" | custom-call | bytes 6291456 | tf_op jit(solution)/shard_map/pallas_call | solution.py:455
  256.9 5.6 %shard_map.212 = (bf16[4,256,256]{2,1,0:T(8,128)(2,1)}, f32[256,1024]{1,0:T(8,128)}, bf16[256,1024]{1,0:T(8,128)(2,1)}, bf16[4,4,256,256]{3,2,1,0:T(8,128)(2,1)}, f32[1,1024]{1,0:T(1,128)}) custom-call(f32[256,1024]{1,0:T(8,128)} %get-tuple-element.41.mixed_ref, bf16[4,256,256]{2,1,0:T(8,128)(2,1)} %copy-done.2, f32[256,1024]{1,0:T(8,128)} %get-tuple-element.45.dh_ref, ...), custom_call_target="tpu_custom_call" | custom-call | flops 1073741824 | bytes 10485760 | tf_op jit(solution)/shard_map/pallas_call | solution.py:818
  262.5 35.3 %shard_map.213 = (f32[256,1024]{1,0:T(8,128)}, bf16[1280,320]{1,0:T(8,128)(2,1)}) custom-call(bf16[256,1024]{1,0:T(8,128)(2,1)} %get-tuple-element.38.q_ref, bf16[1280,1024]{1,0:T(8,128)(2,1)} %get-tuple-element.48.k_ref, bf16[1280,1024]{1,0:T(8,128)(2,1)} %get-tuple-element.49.v_ref, bf16[256,1024]{1,0:T(8,128)(2,1)} %get-tuple-element.50.do_ref, ...), custom_call_target="tpu_custom_call" | custom-call | flops 26843545600 | bytes 16777216 | tf_op jit(solution)/shard_map/pallas_call | solution.py:286
  297.8 16.3 %shard_map.214.dkf_ref = f32[256,320]{1,0:T(8,128)} custom-call(bf16[5,256,320]{2,1,0:T(8,128)(2,1)} %bitcast.160), custom_call_target="tpu_custom_call" | custom-call | bytes 1048576 | tf_op jit(solution)/shard_map/pallas_call | solution.py:649
  314.1 9.6 %shard_map.215 = (f32[4,256,256]{2,1,0:T(8,128)}, f32[1,1024]{1,0:T(1,128)}, bf16[800,1024]{1,0:T(8,128)(2,1)}) custom-call(f32[256,1024]{1,0:T(8,128)} %get-tuple-element.52.dq_ref, f32[256,320]{1,0:T(8,128)} %shard_map.214.dkf_ref, f32[256,160]{1,0:T(8,128)} %get-tuple-element.54.hf_ref, f32[256,384]{1,0:T(8,128)} %get-tuple-element.55.bq_ref, ...), custom_call_target="tpu_custom_call" | custom-call | flops 2516582400 | bytes 12582912 | tf_op jit(solution)/shard_map/pallas_call | solution.py:895
  332.6 4.4 collective-permute-start.23
  337.0 3.5 all-to-all-start.3
  340.6 44.3 %psum.7 = f32[2,1024]{1,0:T(2,128)S(1)} all-reduce(f32[2,1024]{1,0:T(2,128)S(1)} %pad_maximum_fusion.2), channel_id=1, replica_groups=mesh['dp'=2,'row'=4,'col'=4] {'dp','row','col'}, use_global_device_ids=true, to_apply=%region_1.2 | all-reduce | flops 2048 | bytes 16384 | tf_op jit(solution)/shard_map/psum | solution.py:1079
  385.5 2.3 collective-permute-start.18
  387.8 2.3 fusion.11
  390.1 4.5 all-to-all-start.4
  396.1 2.1 collective-permute-start.7
  400.5 17.8 %collective-permute-done.7 = bf16[4,200,256]{2,1,0:T(8,128)(2,1)S(1)} collective-permute-done((bf16[4,200,256]{2,1,0:T(8,128)(2,1)S(1)}, bf16[4,200,256]{2,1,0:T(8,128)(2,1)S(1)}, u32[]{:S(2)}, u32[]{:S(2)}) %collective-permute-start.7) | collective-permute-done | bytes 409632 | tf_op jit(solution)/shard_map/ppermute | solution.py:1068
  418.5 1.6 collective-permute-start.10
  420.6 2.3 collective-permute-start.8
  422.9 1.8 add_convert_fusion
  431.0 1.9 add_convert_fusion.1
  432.9 2.0 concatenate.54
  435.9 13.6 %collective-permute-start.11 = (bf16[200,256]{1,0:T(8,128)(2,1)S(1)}, bf16[200,256]{1,0:T(8,128)(2,1)}, u32[]{:S(2)}, u32[]{:S(2)}) collective-permute-start(bf16[200,256]{1,0:T(8,128)(2,1)S(1)} %fusion.20), channel_id=1, source_target_pairs={{0,16},{16,0},{1,17},{17,1},{2,18},{18,2},{3,19},{19,3},{4,20},{20... | collective-permute-start | bytes 307208 | tf_op jit(solution)/shard_map/ppermute | solution.py:952
  449.6 10.6 %collective-permute-done.20 = bf16[2,176,512]{2,1,0:T(8,128)(2,1)} collective-permute-done((bf16[2,176,512]{2,1,0:T(8,128)(2,1)}, bf16[2,176,512]{2,1,0:T(8,128)(2,1)}, u32[]{:S(2)}, u32[]{:S(2)}) %collective-permute-start.20) | collective-permute-done | bytes 360480 | tf_op jit(solution)/shard_map/ppermute | solution.py:949
  461.5 2.1 collective-permute-start.22
  467.0 2.9 collective-permute-start.14
  470.0 2.1 collective-permute-done.22
  476.5 3.5 all-to-all-start.5
  483.2 1.8 collective-permute-start.17
  485.7 3.4 collective-permute-done.17
  489.9 4.9 all-to-all-done.5
  497.2 2.3 copy.181
  (142 shorter events, 55.0 us)
Async XLA Ops:
  7.2 10.3 %copy-start = (s32[2,1,2048]{2,1,0:T(1,128)S(1)}, s32[2,1,2048]{2,1,0:T(1,128)}, u32[]{:S(2)}) copy-start(s32[2,1,2048]{2,1,0:T(1,128)} %param.14) | copy-start | bytes 49156
  7.2 90.2 %all-gather.5.cloned.1.call-start = ((), (), s32[]{:S(2)}) async-start(), calls=%async_computation.6 | async-start | bytes 3969024 | tf_op jit(solution)/shard_map/all_gather | solution.py:931
  13.3 21.5 %all-to-all-start.2 = ((bf16[4,3,176,256]{3,2,1,0:T(8,128)(2,1)}), bf16[4,3,176,256]{3,2,1,0:T(8,128)(2,1)S(1)}, u32[]{:S(2)}, u32[]{:S(2)}) async-start(bf16[4,3,176,256]{3,2,1,0:T(8,128)(2,1)} %maximum_bitcast_fusion), calls=%async_computation.2 | async-start | bytes 2162688 | tf_op jit(solution)/shard_map/all_to_all | solution.py:945
  34.8 22.4 %all-to-all-start.1 = ((bf16[4,256,256]{2,1,0:T(8,128)(2,1)}), bf16[4,256,256]{2,1,0:T(8,128)(2,1)S(1)}, u32[]{:S(2)}, u32[]{:S(2)}) async-start(bf16[4,256,256]{2,1,0:T(8,128)(2,1)} %bitcast.13), calls=%async_computation.1 | async-start | bytes 1048576 | tf_op jit(solution)/shard_map/all_to_all | solution.py:963
  38.5 1.0 copy-start.4
  38.5 8.0 %copy-start.11 = (f32[256]{0:T(256)S(1)}, f32[256]{0:T(256)}, u32[]{:S(2)}) copy-start(f32[256]{0:T(256)} %param.15) | copy-start | bytes 3076
  38.5 13.2 %copy-start.12 = (f32[256]{0:T(256)S(1)}, f32[256]{0:T(256)}, u32[]{:S(2)}) copy-start(f32[256]{0:T(256)} %param.16) | copy-start | bytes 3076
  39.5 43.9 %collective-permute-start = (bf16[3,176,512]{2,1,0:T(8,128)(2,1)S(1)}, bf16[3,176,512]{2,1,0:T(8,128)(2,1)}, u32[]{:S(2)}, u32[]{:S(2)}) collective-permute-start(bf16[3,176,512]{2,1,0:T(8,128)(2,1)S(1)} %constant_dynamic-slice_fusion.3), channel_id=1, source_target_pairs={{0,4},{4,0},{8,12},{12,8},{1,5},{5,1},{9,13},{13,9},{2,6},{6,2},{1... | collective-permute-start | bytes 1622024 | tf_op jit(solution)/shard_map/ppermute | solution.py:949
  41.9 53.5 %collective-permute-start.1 = (bf16[3,176,512]{2,1,0:T(8,128)(2,1)S(1)}, bf16[3,176,512]{2,1,0:T(8,128)(2,1)}, u32[]{:S(2)}, u32[]{:S(2)}) collective-permute-start(bf16[3,176,512]{2,1,0:T(8,128)(2,1)S(1)} %constant_dynamic-slice_fusion.3), channel_id=1, source_target_pairs={{0,8},{4,12},{8,0},{12,4},{1,9},{5,13},{9,1},{13,5},{2,10},{6,14},... | collective-permute-start | bytes 1622024 | tf_op jit(solution)/shard_map/ppermute | solution.py:949
  44.5 52.4 %collective-permute-start.2 = (bf16[3,176,512]{2,1,0:T(8,128)(2,1)S(1)}, bf16[3,176,512]{2,1,0:T(8,128)(2,1)}, u32[]{:S(2)}, u32[]{:S(2)}) collective-permute-start(bf16[3,176,512]{2,1,0:T(8,128)(2,1)S(1)} %constant_dynamic-slice_fusion.3), channel_id=1, source_target_pairs={{0,12},{4,8},{8,4},{12,0},{1,13},{5,9},{9,5},{13,1},{2,14},{6,10},... | collective-permute-start | bytes 1622024 | tf_op jit(solution)/shard_map/ppermute | solution.py:949
  57.3 5.4 %copy-start.2 = (bf16[4,256,256]{2,1,0:T(8,128)(2,1)}, bf16[4,256,256]{2,1,0:T(8,128)(2,1)S(1)}, u32[]{:S(2)}) copy-start(bf16[4,256,256]{2,1,0:T(8,128)(2,1)S(1)} %all-to-all-done.1.cot_ref) | copy-start | bytes 1572868
  57.3 49.0 %all-to-all-start = ((bf16[4,256,256]{2,1,0:T(8,128)(2,1)}), bf16[4,256,256]{2,1,0:T(8,128)(2,1)}, u32[]{:S(2)}, u32[]{:S(2)}) async-start(bf16[4,256,256]{2,1,0:T(8,128)(2,1)} %bitcast), calls=%async_computation | async-start | bytes 1048576 | tf_op jit(solution)/shard_map/all_to_all | solution.py:963
  83.4 122.9 %collective-permute-start.3 = (bf16[3,176,512]{2,1,0:T(8,128)(2,1)}, bf16[3,176,512]{2,1,0:T(8,128)(2,1)}, u32[]{:S(2)}, u32[]{:S(2)}) collective-permute-start(bf16[3,176,512]{2,1,0:T(8,128)(2,1)} %collective-permute-done.refs_3_), channel_id=1, source_target_pairs={{0,16},{16,0},{1,17},{17,1},{2,18},{18,2},{3,19},{19,3},{4,20},{20... | collective-permute-start | bytes 1622024 | tf_op jit(solution)/shard_map/ppermute | solution.py:952
  95.4 111.0 %collective-permute-start.4 = (bf16[3,176,512]{2,1,0:T(8,128)(2,1)}, bf16[3,176,512]{2,1,0:T(8,128)(2,1)}, u32[]{:S(2)}, u32[]{:S(2)}) collective-permute-start(bf16[3,176,512]{2,1,0:T(8,128)(2,1)} %collective-permute-done.1.refs_4_), channel_id=1, source_target_pairs={{0,16},{16,0},{1,17},{17,1},{2,18},{18,2},{3,19},{19,3},{4,20},{20... | collective-permute-start | bytes 1622024 | tf_op jit(solution)/shard_map/ppermute | solution.py:952
  96.8 109.5 %collective-permute-start.5 = (bf16[3,176,512]{2,1,0:T(8,128)(2,1)}, bf16[3,176,512]{2,1,0:T(8,128)(2,1)}, u32[]{:S(2)}, u32[]{:S(2)}) collective-permute-start(bf16[3,176,512]{2,1,0:T(8,128)(2,1)} %collective-permute-done.2.refs_5_), channel_id=1, source_target_pairs={{0,16},{16,0},{1,17},{17,1},{2,18},{18,2},{3,19},{19,3},{4,20},{20... | collective-permute-start | bytes 1622024 | tf_op jit(solution)/shard_map/ppermute | solution.py:952
  157.9 24.4 %copy-start.3 = (bf16[7296,256]{1,0:T(8,128)(2,1)S(1)}, bf16[7296,256]{1,0:T(8,128)(2,1)}, u32[]{:S(2)}) copy-start(bf16[7296,256]{1,0:T(8,128)(2,1)} %all-gather.5.cloned.1.call-done) | copy-start | bytes 11206660
  327.8 1.9 copy-start.5
  328.9 65.8 %collective-permute-start.6 = (bf16[4,2,200,256]{3,2,1,0:T(8,128)(2,1)}, bf16[4,2,200,256]{3,2,1,0:T(8,128)(2,1)}, u32[]{:S(2)}, u32[]{:S(2)}) collective-permute-start(bf16[4,2,200,256]{3,2,1,0:T(8,128)(2,1)} %fusion.5), channel_id=1, source_target_pairs={{0,1},{1,0},{2,3},{3,2},{4,5},{5,4},{6,7},{7,6},{8,9},{9,8},{10,11... | collective-permute-start | bytes 2457608 | tf_op jit(solution)/shard_map/ppermute | solution.py:1066
  329.9 1.7 copy-start.7
  330.9 6.1 %copy-start.13 = (s32[10]{0:T(128)S(1)}, s32[10]{0:T(128)}, u32[]{:S(2)}) copy-start(s32[10]{0:T(128)} %constant.160) | copy-start | bytes 124
  330.9 67.2 %collective-permute-start.12 = (bf16[4,2,256,256]{3,2,0,1:T(8,128)(2,1)}, bf16[4,2,256,256]{3,2,0,1:T(8,128)(2,1)}, u32[]{:S(2)}, u32[]{:S(2)}) collective-permute-start(bf16[4,2,256,256]{3,2,0,1:T(8,128)(2,1)} %bitcast.139), channel_id=1, source_target_pairs={{0,1},{1,0},{2,3},{3,2},{4,5},{5,4},{6,7},{7,6},{8,9},{9,8},{10,11... | collective-permute-start | bytes 3145736 | tf_op jit(solution)/shard_map/ppermute | solution.py:1066
  331.6 8.9 %copy-start.9 = (f32[1,1024]{1,0:T(1,128)S(1)}, f32[1,1024]{1,0:T(1,128)}, u32[]{:S(2)}) copy-start(f32[1,1024]{1,0:T(1,128)} %get-tuple-element.60) | copy-start | bytes 12292
  331.6 8.9 %copy-start.10 = (f32[1,1024]{1,0:T(1,128)S(1)}, f32[1,1024]{1,0:T(1,128)}, u32[]{:S(2)}) copy-start(f32[1,1024]{1,0:T(1,128)} %get-tuple-element.59) | copy-start | bytes 12292
  332.6 52.9 %collective-permute-start.25 = (bf16[176,1024]{1,0:T(8,128)(2,1)}, bf16[176,1024]{1,0:T(8,128)(2,1)}, u32[]{:S(2)}, u32[]{:S(2)}) collective-permute-start(bf16[176,1024]{1,0:T(8,128)(2,1)} %get-tuple-element.77), channel_id=1, source_target_pairs={{0,12},{4,8},{8,4},{12,0},{1,13},{5,9},{9,5},{13,1},{2,14},{6,10},... | collective-permute-start | bytes 1081352 | tf_op jit(solution)/shard_map/ppermute | solution.py:949
  332.6 55.2 %collective-permute-start.24 = (bf16[176,1024]{1,0:T(8,128)(2,1)}, bf16[176,1024]{1,0:T(8,128)(2,1)}, u32[]{:S(2)}, u32[]{:S(2)}) collective-permute-start(bf16[176,1024]{1,0:T(8,128)(2,1)} %get-tuple-element.78), channel_id=1, source_target_pairs={{0,8},{4,12},{8,0},{12,4},{1,9},{5,13},{9,1},{13,5},{2,10},{6,14},... | collective-permute-start | bytes 1081352 | tf_op jit(solution)/shard_map/ppermute | solution.py:949
  332.6 55.2 %collective-permute-start.23 = (bf16[176,1024]{1,0:T(8,128)(2,1)}, bf16[176,1024]{1,0:T(8,128)(2,1)}, u32[]{:S(2)}, u32[]{:S(2)}) collective-permute-start(bf16[176,1024]{1,0:T(8,128)(2,1)} %get-tuple-element.76), channel_id=1, source_target_pairs={{0,4},{4,0},{8,12},{12,8},{1,5},{5,1},{9,13},{13,9},{2,6},{6,2},{1... | collective-permute-start | bytes 1081352 | tf_op jit(solution)/shard_map/ppermute | solution.py:949
  337.0 53.1 %all-to-all-start.3 = ((bf16[4,256,256]{2,1,0:T(8,128)(2,1)}), bf16[4,256,256]{2,1,0:T(8,128)(2,1)S(1)}, u32[]{:S(2)}, u32[]{:S(2)}) async-start(bf16[4,256,256]{2,1,0:T(8,128)(2,1)} %get-tuple-element.47), calls=%async_computation.3 | async-start | bytes 1048576 | tf_op jit(solution)/shard_map/all_to_all | solution.py:1028
  385.5 35.1 %collective-permute-start.18 = (bf16[2,704,512]{2,1,0:T(8,128)(2,1)}, bf16[2,704,512]{2,1,0:T(8,128)(2,1)}, u32[]{:S(2)}, u32[]{:S(2)}) collective-permute-start(bf16[2,704,512]{2,1,0:T(8,128)(2,1)} %get-tuple-element.64), channel_id=1, source_target_pairs={{0,16},{16,0},{1,17},{17,1},{2,18},{18,2},{3,19},{19,3},{4,20},{20... | collective-permute-start | bytes 4325384 | tf_op jit(solution)/shard_map/ppermute | solution.py:952
  390.1 36.4 %collective-permute-start.26 = (bf16[176,1024]{1,0:T(8,128)(2,1)}, bf16[176,1024]{1,0:T(8,128)(2,1)}, u32[]{:S(2)}, u32[]{:S(2)}) collective-permute-start(bf16[176,1024]{1,0:T(8,128)(2,1)} %fusion.11), channel_id=1, source_target_pairs={{0,16},{16,0},{1,17},{17,1},{2,18},{18,2},{3,19},{19,3},{4,20},{20... | collective-permute-start | bytes 1081352 | tf_op jit(solution)/shard_map/ppermute | solution.py:952
  390.1 44.7 %all-to-all-start.4 = ((f32[4,256,256]{2,1,0:T(8,128)}), f32[4,256,256]{2,1,0:T(8,128)}, u32[]{:S(2)}, u32[]{:S(2)}) async-start(f32[4,256,256]{2,1,0:T(8,128)} %get-tuple-element.58), calls=%async_computation.4 | async-start | bytes 2097152 | tf_op jit(solution)/shard_map/all_to_all | solution.py:1029
  396.1 22.3 %collective-permute-start.7 = (bf16[4,200,256]{2,1,0:T(8,128)(2,1)S(1)}, bf16[4,200,256]{2,1,0:T(8,128)(2,1)S(1)}, u32[]{:S(2)}, u32[]{:S(2)}) collective-permute-start(bf16[4,200,256]{2,1,0:T(8,128)(2,1)S(1)} %dynamic-slice_bitcast_fusion.1), channel_id=1, source_target_pairs={{0,2},{1,3},{2,0},{3,1},{4,6},{5,7},{6,4},{7,5},{8,10},{9,11},{10,... | collective-permute-start | bytes 1228808 | tf_op jit(solution)/shard_map/ppermute | solution.py:1068
  399.6 23.3 %copy-start.6 = (bf16[2,704,512]{2,1,0:T(8,128)(2,1)S(1)}, bf16[2,704,512]{2,1,0:T(8,128)(2,1)}, u32[]{:S(2)}) copy-start(bf16[2,704,512]{2,1,0:T(8,128)(2,1)} %get-tuple-element.63) | copy-start | bytes 4325380
  400.4 63.2 %collective-permute-start.13 = (bf16[4,256,256]{2,1,0:T(8,128)(2,1)}, bf16[4,256,256]{2,1,0:T(8,128)(2,1)}, u32[]{:S(2)}, u32[]{:S(2)}) collective-permute-start(bf16[4,256,256]{2,1,0:T(8,128)(2,1)} %dynamic-slice_bitcast_fusion), channel_id=1, source_target_pairs={{0,2},{1,3},{2,0},{3,1},{4,6},{5,7},{6,4},{7,5},{8,10},{9,11},{10,... | collective-permute-start | bytes 1572872 | tf_op jit(solution)/shard_map/ppermute | solution.py:1068
  418.5 9.6 %collective-permute-start.10 = (bf16[200,256]{1,0:T(8,128)(2,1)S(1)}, bf16[200,256]{1,0:T(8,128)(2,1)}, u32[]{:S(2)}, u32[]{:S(2)}) collective-permute-start(bf16[200,256]{1,0:T(8,128)(2,1)S(1)} %get-tuple-element.83), channel_id=1, source_target_pairs={{0,12},{4,8},{8,4},{12,0},{1,13},{5,9},{9,5},{13,1},{2,14},{6,10},... | collective-permute-start | bytes 307208 | tf_op jit(solution)/shard_map/ppermute | solution.py:949
  420.0 9.5 %collective-permute-start.9 = (bf16[200,256]{1,0:T(8,128)(2,1)S(1)}, bf16[200,256]{1,0:T(8,128)(2,1)}, u32[]{:S(2)}, u32[]{:S(2)}) collective-permute-start(bf16[200,256]{1,0:T(8,128)(2,1)S(1)} %get-tuple-element.84), channel_id=1, source_target_pairs={{0,8},{4,12},{8,0},{12,4},{1,9},{5,13},{9,1},{13,5},{2,10},{6,14},... | collective-permute-start | bytes 307208 | tf_op jit(solution)/shard_map/ppermute | solution.py:949
  420.6 14.3 %collective-permute-start.8 = (bf16[200,256]{1,0:T(8,128)(2,1)S(1)}, bf16[200,256]{1,0:T(8,128)(2,1)}, u32[]{:S(2)}, u32[]{:S(2)}) collective-permute-start(bf16[200,256]{1,0:T(8,128)(2,1)S(1)} %get-tuple-element.82), channel_id=1, source_target_pairs={{0,4},{4,0},{8,12},{12,8},{1,5},{5,1},{9,13},{13,9},{2,6},{6,2},{1... | collective-permute-start | bytes 307208 | tf_op jit(solution)/shard_map/ppermute | solution.py:949
  426.6 23.0 %collective-permute-start.21 = (bf16[2,176,512]{2,1,0:T(8,128)(2,1)}, bf16[2,176,512]{2,1,0:T(8,128)(2,1)}, u32[]{:S(2)}, u32[]{:S(2)}) collective-permute-start(bf16[2,176,512]{2,1,0:T(8,128)(2,1)} %get-tuple-element.75), channel_id=1, source_target_pairs={{0,12},{4,8},{8,4},{12,0},{1,13},{5,9},{9,5},{13,1},{2,14},{6,10},... | collective-permute-start | bytes 1081352 | tf_op jit(solution)/shard_map/ppermute | solution.py:949
  428.1 32.1 %collective-permute-start.20 = (bf16[2,176,512]{2,1,0:T(8,128)(2,1)}, bf16[2,176,512]{2,1,0:T(8,128)(2,1)}, u32[]{:S(2)}, u32[]{:S(2)}) collective-permute-start(bf16[2,176,512]{2,1,0:T(8,128)(2,1)} %get-tuple-element.74), channel_id=1, source_target_pairs={{0,8},{4,12},{8,0},{12,4},{1,9},{5,13},{9,1},{13,5},{2,10},{6,14},... | collective-permute-start | bytes 1081352 | tf_op jit(solution)/shard_map/ppermute | solution.py:949
  429.5 30.6 %collective-permute-start.19 = (bf16[2,176,512]{2,1,0:T(8,128)(2,1)}, bf16[2,176,512]{2,1,0:T(8,128)(2,1)}, u32[]{:S(2)}, u32[]{:S(2)}) collective-permute-start(bf16[2,176,512]{2,1,0:T(8,128)(2,1)} %get-tuple-element.73), channel_id=1, source_target_pairs={{0,4},{4,0},{8,12},{12,8},{1,5},{5,1},{9,13},{13,9},{2,6},{6,2},{1... | collective-permute-start | bytes 1081352 | tf_op jit(solution)/shard_map/ppermute | solution.py:949
  435.9 44.0 %collective-permute-start.11 = (bf16[200,256]{1,0:T(8,128)(2,1)S(1)}, bf16[200,256]{1,0:T(8,128)(2,1)}, u32[]{:S(2)}, u32[]{:S(2)}) collective-permute-start(bf16[200,256]{1,0:T(8,128)(2,1)S(1)} %fusion.20), channel_id=1, source_target_pairs={{0,16},{16,0},{1,17},{17,1},{2,18},{18,2},{3,19},{19,3},{4,20},{20... | collective-permute-start | bytes 307208 | tf_op jit(solution)/shard_map/ppermute | solution.py:952
  461.5 10.6 %collective-permute-start.22 = (bf16[2,176,512]{2,1,0:T(8,128)(2,1)S(1)}, bf16[2,176,512]{2,1,0:T(8,128)(2,1)}, u32[]{:S(2)}, u32[]{:S(2)}) collective-permute-start(bf16[2,176,512]{2,1,0:T(8,128)(2,1)S(1)} %fusion.14), channel_id=1, source_target_pairs={{0,16},{16,0},{1,17},{17,1},{2,18},{18,2},{3,19},{19,3},{4,20},{20... | collective-permute-start | bytes 1081352 | tf_op jit(solution)/shard_map/ppermute | solution.py:952
  465.6 16.6 %collective-permute-start.16 = (bf16[256,256]{1,0:T(8,128)(2,1)}, bf16[256,256]{1,0:T(8,128)(2,1)S(1)}, u32[]{:S(2)}, u32[]{:S(2)}) collective-permute-start(bf16[256,256]{1,0:T(8,128)(2,1)} %get-tuple-element.80), channel_id=1, source_target_pairs={{0,12},{4,8},{8,4},{12,0},{1,13},{5,9},{9,5},{13,1},{2,14},{6,10},... | collective-permute-start | bytes 393224 | tf_op jit(solution)/shard_map/ppermute | solution.py:949
  467.0 15.2 %collective-permute-start.15 = (bf16[256,256]{1,0:T(8,128)(2,1)}, bf16[256,256]{1,0:T(8,128)(2,1)}, u32[]{:S(2)}, u32[]{:S(2)}) collective-permute-start(bf16[256,256]{1,0:T(8,128)(2,1)} %get-tuple-element.81), channel_id=1, source_target_pairs={{0,8},{4,12},{8,0},{12,4},{1,9},{5,13},{9,1},{13,5},{2,10},{6,14},... | collective-permute-start | bytes 393224 | tf_op jit(solution)/shard_map/ppermute | solution.py:949
  467.0 7.5 %copy-start.8 = (bf16[1,176,4,256]{3,2,1,0:T(4,128)(2,1)S(1)}, bf16[1,176,4,256]{3,2,1,0:T(4,128)(2,1)}, u32[]{:S(2)}) copy-start(bf16[1,176,4,256]{3,2,1,0:T(4,128)(2,1)} %concatenate.54) | copy-start | bytes 1081348
  467.0 15.2 %collective-permute-start.14 = (bf16[256,256]{1,0:T(8,128)(2,1)S(1)}, bf16[256,256]{1,0:T(8,128)(2,1)}, u32[]{:S(2)}, u32[]{:S(2)}) collective-permute-start(bf16[256,256]{1,0:T(8,128)(2,1)S(1)} %get-tuple-element.79), channel_id=1, source_target_pairs={{0,4},{4,0},{8,12},{12,8},{1,5},{5,1},{9,13},{13,9},{2,6},{6,2},{1... | collective-permute-start | bytes 393224 | tf_op jit(solution)/shard_map/ppermute | solution.py:949
  476.5 18.3 %all-to-all-start.5 = ((bf16[4,3,176,256]{3,2,1,0:T(8,128)(2,1)}), bf16[4,3,176,256]{3,2,1,0:T(8,128)(2,1)S(1)}, u32[]{:S(2)}, u32[]{:S(2)}) async-start(bf16[4,3,176,256]{3,2,1,0:T(8,128)(2,1)} %copy.161), calls=%async_computation.5 | async-start | bytes 2162688 | tf_op jit(solution)/shard_map/all_to_all | solution.py:1051
  483.2 5.9 %collective-permute-start.17 = (bf16[256,256]{1,0:T(8,128)(2,1)S(1)}, bf16[256,256]{1,0:T(8,128)(2,1)S(1)}, u32[]{:S(2)}, u32[]{:S(2)}) collective-permute-start(bf16[256,256]{1,0:T(8,128)(2,1)S(1)} %fusion.17), channel_id=1, source_target_pairs={{0,16},{16,0},{1,17},{17,1},{2,18},{18,2},{3,19},{19,3},{4,20},{20... | collective-permute-start | bytes 393224 | tf_op jit(solution)/shard_map/ppermute | solution.py:952
  496.4 3.1 copy-start.1
Sparse Core Ops, SparseCore 0:
  11.1 71.2 all-gather.4

commit v3 on v1

v3 whole, which is shorter than its diff:
```python
import functools

import jax
import jax.numpy as jnp
from jax import lax
from jax.experimental import pallas as pl
from jax.experimental.pallas import tpu as pltpu
from jax.sharding import PartitionSpec as P

D = 1024
H = 16
HD = 64
RQ = 6
RK = 2
FAC = 10
MAX_DOC = 1024

EPS = 1e-06
ROPE = 10000.0
NEG = -1e30
BF = jnp.bfloat16
F32 = jnp.float32
LANES = 128
PAIRS = H // 2
FAC_ORDER = (6, 7, 8, 9, 0, 1, 2, 3, 4, 5)
FAC_BACK = (4, 5, 6, 7, 8, 9, 0, 1, 2, 3)
VMEM = pl.BlockSpec(memory_space=pltpu.VMEM)


def nn(a, b):
    return jnp.dot(a, b, preferred_element_type=F32)


def nt(a, b):
    return lax.dot_general(a, b, (((1,), (1,)), ((), ())), preferred_element_type=F32)


def tn(a, b):
    return lax.dot_general(a, b, (((0,), (0,)), ((), ())), preferred_element_type=F32)


def two_pass(a, b):
    high = a.astype(BF)
    low = (a - high.astype(F32)).astype(BF)
    return nn(high, b) + nn(low, b)


def lane_iota(shape):
    return lax.broadcasted_iota(jnp.int32, shape, len(shape) - 1)


def spread(rows, first, width):
    row = lax.broadcasted_iota(jnp.int32, (rows, width), 0)
    head = lax.broadcasted_iota(jnp.int32, (rows, width), 1) // HD
    return (row == head + first).astype(F32).astype(BF)


def collect(rows, width, first):
    head = lax.broadcasted_iota(jnp.int32, (rows, width), 0) // HD
    lane = lax.broadcasted_iota(jnp.int32, (rows, width), 1)
    return (lane == head + first).astype(F32).astype(BF)


GROUP = 4
GROUP_COLS = 48
RANK_COLS = FAC * HD
HEAD_COLS = H // GROUP * GROUP_COLS
ALL_COLS = RANK_COLS + HEAD_COLS


def factor_place(head, j):
    return head // GROUP * GROUP_COLS + j * GROUP + head % GROUP


def head_spread(j, first_head, width):
    row = lax.broadcasted_iota(jnp.int32, (HEAD_COLS, width), 0)
    head = lax.broadcasted_iota(jnp.int32, (HEAD_COLS, width), 1) // HD + first_head
    return (row == factor_place(head, j)).astype(F32).astype(BF)


def head_collect(j):
    head = lax.broadcasted_iota(jnp.int32, (D, HEAD_COLS), 0) // HD
    lane = lax.broadcasted_iota(jnp.int32, (D, HEAD_COLS), 1)
    return (lane == factor_place(head, j)).astype(F32).astype(BF)


def key_columns():
    row = lax.broadcasted_iota(jnp.int32, (HEAD_COLS, 2 * RK * H), 0)
    lane = lax.broadcasted_iota(jnp.int32, (HEAD_COLS, 2 * RK * H), 1)
    return (row == factor_place(lane % H, lane // H)).astype(F32).astype(BF)


def swap_halves(tile):
    lane = lane_iota(tile.shape)
    ahead = pltpu.roll(tile, LANES - HD // 2, 1)
    behind = pltpu.roll(tile, HD // 2, 1)
    return jnp.where(lane % HD < HD // 2, ahead, behind)


def double_left(tile):
    return jnp.where(lane_iota(tile.shape) < HD, tile, pltpu.roll(tile, HD, 1))


def double_right(tile):
    return jnp.where(lane_iota(tile.shape) < HD, pltpu.roll(tile, HD, 1), tile)


def params(**more):
    return pltpu.CompilerParams(vmem_limit_bytes=60 << 20, **more)


def call(body, outs, scratch=(), cost=None):
    return pl.pallas_call(
        body,
        out_shape=outs,
        scratch_shapes=scratch,
        compiler_params=params(),
        cost_estimate=cost,
    )


def cost_of(flops, moved):
    return pl.CostEstimate(flops=int(flops), bytes_accessed=int(moved), transcendentals=0)


MESH = pl.DeviceIdType.MESH
ANY = pl.BlockSpec(memory_space=pl.ANY)


class Mover:
    def __init__(self, send_sem, recv_sem):
        self.send_sem = send_sem
        self.recv_sem = recv_sem
        self.used = 0

    def copy(self, source, target, **place):
        index = self.used
        self.used += 1
        return pltpu.make_async_remote_copy(
            src_ref=source,
            dst_ref=target,
            send_sem=self.send_sem.at[index],
            recv_sem=self.recv_sem.at[index],
            device_id=place,
            device_id_type=MESH,
        )


def greet(partners):
    barrier = pltpu.get_barrier_semaphore()
    count = 0
    for present, place in partners:
        if present is None:
            pl.semaphore_signal(barrier, inc=1, device_id=place, device_id_type=MESH)
            count = count + 1
        else:

            @pl.when(present)
            def _():
                pl.semaphore_signal(barrier, inc=1, device_id=place, device_id_type=MESH)

            count = count + present.astype(jnp.int32)
    pl.semaphore_wait(barrier, count)


def neighbours():
    col = lax.axis_index("col")
    core = col + 1 - 2 * lax.rem(col, 2)
    across = lax.rem(col + 2, 4)
    return col, core, across


def square():
    dp = lax.axis_index("dp")
    x = lax.axis_index("col") // 2
    return dp, (dp * 2 + x, dp * 2 + 1 - x, (1 - dp) * 2 + x, (1 - dp) * 2 + 1 - x)


def comm_params(ident):
    return params(collective_id=ident, has_side_effects=True)


def start_body(tok_ref, w_ref, gain_ref, ffn_ref, x_ref, wall_ref, gains_ref, parts_ref, send_sem, recv_sem, local_sem):
    row = lax.axis_index("row")
    col, core, across = neighbours()
    cross = lax.rem(core + 2, 4)
    rows = [lax.rem(row + k, 4) for k in range(4)]
    back = [lax.rem(row + 4 - k, 4) for k in range(4)]
    greet([(None, {"col": c}) for c in (core, across, cross)] + [(None, {"row": r}) for r in rows[1:]])
    mover = Mover(send_sem, recv_sem)
    started = []

    def go(source, target, **place):
        c = mover.copy(source, target, **place)
        c.start()
        started.append(c)
        return c

    down = [None] + [go(w_ref, wall_ref.at[row, col], row=rows[k]) for k in range(1, 4)]
    sides = [go(w_ref, wall_ref.at[row, col], col=across)]
    cores = [go(w_ref, wall_ref.at[row, col], col=core)]
    rest = []
    for c in (across, cross, core):
        rest.append(go(gain_ref, gains_ref.at[col], col=c))
        rest.append(go(tok_ref.at[c], x_ref.at[col], col=c))
    for c in (across, cross, core):
        rest.append(go(ffn_ref.at[c], parts_ref.at[col], col=c))
    own = [
        pltpu.make_async_copy(w_ref, wall_ref.at[row, col], local_sem.at[0]),
        pltpu.make_async_copy(gain_ref, gains_ref.at[col], local_sem.at[1]),
        pltpu.make_async_copy(tok_ref.at[col], x_ref.at[col], local_sem.at[2]),
        pltpu.make_async_copy(ffn_ref.at[col], parts_ref.at[col], local_sem.at[3]),
    ]
    for c in own:
        c.start()
    for k in range(1, 4):
        down[k].wait_recv()
        block = wall_ref.at[back[k], col]
        sides.append(go(block, block, col=across))
        cores.append(go(block, block, col=core))
    passed = []
    for k in range(4):
        sides[k].wait_recv()
        block = wall_ref.at[back[k], across]
        passed.append(go(block, block, col=core))
    for c in cores + rest + passed:
        c.wait_recv()
    for c in started:
        c.wait_send()
    for c in own:
        c.wait()


def start(tok, w_own, gains, ffn_own):
    count = 24
    return pl.pallas_call(
        start_body,
        out_shape=(
            jax.ShapeDtypeStruct(tok.shape, tok.dtype),
            jax.ShapeDtypeStruct((4, 4) + w_own.shape, BF),
            jax.ShapeDtypeStruct((4,) + gains.shape, F32),
            jax.ShapeDtypeStruct(ffn_own.shape, BF),
        ),
        in_specs=[ANY] * 4,
        out_specs=(ANY,) * 4,
        scratch_shapes=[
            pltpu.SemaphoreType.DMA((count,)),
            pltpu.SemaphoreType.DMA((count,)),
            pltpu.SemaphoreType.DMA((4,)),
        ],
        compiler_params=comm_params(1),
        cost_estimate=cost_of(0, 8 << 20),
    )(tok, w_own, gains, ffn_own)


class AttendCopies:
    def __init__(self, w_ref, cot_ref, rows_ref, near_ref, send_sem, recv_sem, local_sem):
        row = lax.axis_index("row")
        col, core, across = neighbours()
        dp, spots = square()
        mover = Mover(send_sem, recv_sem)
        self.left = row >= 1
        self.right = row <= 2
        self.both = jnp.logical_and(self.left, self.right)
        self.from_left = row >= 2
        self.from_right = row <= 1
        self.partners = [
            (self.right, {"row": row + 1}),
            (self.left, {"row": row - 1}),
            (None, {"col": across}),
            (None, {"dp": 1 - dp}),
            (None, {"dp": 1 - dp, "col": across}),
        ]
        self.to_right = mover.copy(w_ref, rows_ref.at[row], row=row + 1)
        self.to_left = mover.copy(w_ref, rows_ref.at[row], row=row - 1)
        self.pass_right = mover.copy(rows_ref.at[row - 1], rows_ref.at[row - 1], row=row + 1)
        self.pass_left = mover.copy(rows_ref.at[row + 1], rows_ref.at[row + 1], row=row - 1)
        target = near_ref.at[spots[0]]
        self.cots = [
            mover.copy(cot_ref, target, col=across),
            mover.copy(cot_ref, target, dp=1 - dp),
            mover.copy(cot_ref, target, dp=1 - dp, col=across),
        ]
        self.own = [
            pltpu.make_async_copy(w_ref, rows_ref.at[row], local_sem.at[0]),
            pltpu.make_async_copy(cot_ref, target, local_sem.at[1]),
        ]

    def first(self):
        greet(self.partners)
        pl.when(self.right)(self.to_right.start)
        pl.when(self.left)(self.to_left.start)
        for c in self.cots + self.own:
            c.start()

    def second(self):
        pl.when(self.left)(self.to_right.wait_recv)
        pl.when(self.right)(self.to_left.wait_recv)
        pl.when(self.both)(self.pass_right.start)
        pl.when(self.both)(self.pass_left.start)

    def last(self):
        pl.when(self.right)(self.to_right.wait_send)
        pl.when(self.left)(self.to_left.wait_send)
        pl.when(self.both)(self.pass_right.wait_send)
        pl.when(self.both)(self.pass_left.wait_send)
        pl.when(self.from_left)(self.pass_right.wait_recv)
        pl.when(self.from_right)(self.pass_left.wait_recv)
        for c in self.cots + self.own:
            c.wait()


class BackCopies:
    def __init__(self, parts_ref, grads_ref, out_ref, got_ref, send_sem, recv_sem, local_sem):
        row = lax.axis_index("row")
        col, core, across = neighbours()
        cross = lax.rem(core + 2, 4)
        mover = Mover(send_sem, recv_sem)
        nxt, prv = lax.rem(row + 1, 4), lax.rem(row + 3, 4)
        self.partners = [(None, {"col": c}) for c in (core, across, cross)]
        self.partners += [(None, {"row": nxt}), (None, {"row": prv})]
        self.copies = [
            mover.copy(grads_ref.at[nxt], got_ref.at[0], row=nxt),
            mover.copy(grads_ref.at[prv], got_ref.at[1], row=prv),
        ]
        self.copies += [mover.copy(parts_ref.at[c], out_ref.at[col], col=c) for c in (across, cross, core)]
        self.own = pltpu.make_async_copy(parts_ref.at[col], out_ref.at[col], local_sem)

    def first(self):
        greet(self.partners)
        for c in self.copies:
            c.start()
        self.own.start()

    def last(self):
        for c in self.copies:
            c.wait()
        self.own.wait()


def gather_body(h_ref, cot_ref, rows_ref, near_ref, far_ref, cot_far_ref, last_ref, send_sem, recv_sem, local_sem):
    row = lax.axis_index("row")
    col, core, across = neighbours()
    dp, (me, on_x, on_y, on_both) = square()
    goes_right = row == 2
    goes_left = row == 1
    comes_left = row == 3
    comes_right = row == 0
    greet(
        [
            (None, {"col": core}),
            (None, {"col": across}),
            (None, {"dp": 1 - dp}),
            (row <= 2, {"row": row + 1}),
            (row >= 1, {"row": row - 1}),
        ]
    )
    mover = Mover(send_sem, recv_sem)
    half = h_ref.shape[0] // 2
    top, low = pl.ds(0, half), pl.ds(half, half)
    started = []

    def go(source, target, **place):
        c = mover.copy(source, target, **place)
        c.start()
        started.append(c)
        return c

    x_low = go(h_ref.at[low], near_ref.at[me, low], col=across)
    y_top = go(h_ref.at[top], near_ref.at[me, top], dp=1 - dp)
    x_top = go(h_ref.at[top], near_ref.at[me, top], col=across)
    y_low = go(h_ref.at[low], near_ref.at[me, low], dp=1 - dp)
    arriving = [go(h_ref, far_ref.at[me], col=core)]
    own = pltpu.make_async_copy(h_ref, near_ref.at[me], local_sem)
    own.start()
    right = mover.copy(rows_ref.at[row - 2], last_ref, row=row + 1)
    left = mover.copy(rows_ref.at[row + 2], last_ref, row=row - 1)
    pl.when(goes_right)(right.start)
    pl.when(goes_left)(left.start)
    for k in range(4):
        arriving.append(go(cot_ref.at[k], cot_far_ref.at[k], col=core))
    x_low.wait_recv()
    both_low = go(near_ref.at[on_x, low], near_ref.at[on_x, low], dp=1 - dp)
    y_top.wait_recv()
    both_top = go(near_ref.at[on_y, top], near_ref.at[on_y, top], col=across)
    x_top.wait_recv()
    arriving.append(go(near_ref.at[on_x], far_ref.at[on_x], col=core))
    y_low.wait_recv()
    arriving.append(go(near_ref.at[on_y], far_ref.at[on_y], col=core))
    both_low.wait_recv()
    both_top.wait_recv()
    arriving.append(go(near_ref.at[on_both], far_ref.at[on_both], col=core))
    for c in arriving:
        c.wait_recv()
    for c in started:
        c.wait_send()
    own.wait()
    pl.when(comes_left)(right.wait_recv)
    pl.when(comes_right)(left.wait_recv)
    pl.when(goes_right)(right.wait_send)
    pl.when(goes_left)(left.wait_send)


def gather(h, cot_near, w_rows):
    count = 16
    return pl.pallas_call(
        gather_body,
        out_shape=(
            jax.ShapeDtypeStruct((4,) + h.shape, BF),
            jax.ShapeDtypeStruct((4,) + h.shape, BF),
            jax.ShapeDtypeStruct(cot_near.shape, BF),
            jax.ShapeDtypeStruct(w_rows.shape[1:], BF),
        ),
        in_specs=[ANY] * 3,
        out_specs=(ANY,) * 4,
        scratch_shapes=[
            pltpu.SemaphoreType.DMA((count,)),
            pltpu.SemaphoreType.DMA((count,)),
            pltpu.SemaphoreType.DMA,
        ],
        compiler_params=comm_params(4),
        cost_estimate=cost_of(0, 12 << 20),
    )(h, cot_near, w_rows)


class SquareSum:
    def __init__(self, mover, part_ref, got_ref, pair_ref, diag_ref, far_ref):
        self.mover = mover
        self.part_ref = part_ref
        self.got_ref = got_ref
        self.pair_ref = pair_ref
        self.diag_ref = diag_ref
        self.far_ref = far_ref
        self.half = part_ref.shape[2] // 2
        self.started = []

    def go(self, source, target, **place):
        c = self.mover.copy(source, target, **place)
        c.start()
        self.started.append(c)
        return c

    def near(self, core, order):
        self.order = order
        self.cores = {}
        for name in (3, 1, 2, 0):
            spot = order[name]
            self.cores[name] = self.go(self.part_ref.at[1, spot], self.got_ref.at[spot], col=core)

    def add_pair(self, name):
        self.cores[name].wait_recv()
        spot = self.order[name]
        self.pair_ref[spot] = (self.part_ref[0, spot].astype(F32) + self.got_ref[spot].astype(F32)).astype(BF)

    def send(self, dp, across):
        me, on_x, on_y, on_both = self.order
        top, low = pl.ds(0, self.half), pl.ds(self.half, self.half)
        self.add_pair(3)
        d_top = self.go(self.pair_ref.at[on_both, top], self.diag_ref.at[0], col=across)
        d_low = self.go(self.pair_ref.at[on_both, low], self.diag_ref.at[1], dp=1 - dp)
        self.add_pair(1)
        self.far = [self.go(self.pair_ref.at[on_x, top], self.far_ref.at[0, top], col=across)]
        self.add_pair(2)
        self.far.append(self.go(self.pair_ref.at[on_y, low], self.far_ref.at[1, low], dp=1 - dp))
        self.add_pair(0)
        d_top.wait_recv()
        self.pair_ref[on_y, top] = (
            self.pair_ref[on_y, top].astype(F32) + self.diag_ref[0].astype(F32)
        ).astype(BF)
        self.far.append(self.go(self.pair_ref.at[on_y, top], self.far_ref.at[1, top], dp=1 - dp))
        d_low.wait_recv()
        self.pair_ref[on_x, low] = (
            self.pair_ref[on_x, low].astype(F32) + self.diag_ref[1].astype(F32)
        ).astype(BF)
        self.far.append(self.go(self.pair_ref.at[on_x, low], self.far_ref.at[0, low], col=across))

    def total(self):
        for c in self.far:
            c.wait_recv()
        return self.pair_ref[self.order[0]].astype(F32) + self.far_ref[0].astype(F32) + self.far_ref[1].astype(F32)

    def end(self):
        for c in self.started:
            c.wait_send()


def row_partners(row, n_row, core):
    return [
        (None, {"col": core}),
        (row + 1 < n_row, {"row": row + 1}),
        (row + 2 < n_row, {"row": row + 2}),
        (row >= 1, {"row": row - 1}),
        (row >= 2, {"row": row - 2}),
    ]


def window_body(n_row, x_ref, zero_ref, win_ref, send_sem, recv_sem, local_sem):
    row = lax.axis_index("row")
    col, core, _ = neighbours()
    side = lax.rem(col, 2)
    greet(row_partners(row, n_row, core))
    mover = Mover(send_sem, recv_sem)
    one = mover.copy(x_ref, win_ref.at[2], row=row + 1)
    two = mover.copy(x_ref, win_ref.at[0], row=row + 2)
    near = mover.copy(x_ref, win_ref.at[3], col=core)
    pass_one = mover.copy(win_ref.at[2], win_ref.at[1 + 2 * side], col=core)
    pass_two = mover.copy(win_ref.at[0], win_ref.at[1], col=core)
    has_one = row >= 1
    has_two = row >= 2

    @pl.when(row + 1 < n_row)
    def _():
        one.start()

    @pl.when(row + 2 < n_row)
    def _():
        two.start()

    @pl.when(side == 0)
    def _():
        near.start()

    own = pltpu.make_async_copy(x_ref, win_ref.at[4], local_sem.at[0])
    own.start()

    def fill(slot):
        return pltpu.make_async_copy(zero_ref, win_ref.at[slot], local_sem.at[slot + 1])

    for absent, slots in (
        (jnp.logical_not(has_two), (0,)),
        (jnp.logical_and(jnp.logical_not(has_two), side == 0), (1,)),
        (jnp.logical_and(jnp.logical_not(has_one), side == 1), (1,)),
        (jnp.logical_not(has_one), (2,)),
        (jnp.logical_and(jnp.logical_not(has_one), side == 0), (3,)),
    ):

        @pl.when(absent)
        def _():
            for slot in slots:
                c = fill(slot)
                c.start()
                c.wait()

    @pl.when(has_one)
    def _():
        one.wait_recv()
        pass_one.start()

    @pl.when(has_two)
    def _():
        two.wait_recv()

    sends_two = jnp.logical_and(has_two, side == 1)
    takes_two = jnp.logical_and(has_two, side == 0)

    @pl.when(sends_two)
    def _():
        pass_two.start()

    @pl.when(has_one)
    def _():
        pass_one.wait_recv()
        pass_one.wait_send()

    @pl.when(takes_two)
    def _():
        pass_two.wait_recv()

    @pl.when(sends_two)
    def _():
        pass_two.wait_send()

    @pl.when(side == 1)
    def _():
        near.wait_recv()

    @pl.when(side == 0)
    def _():
        near.wait_send()

    @pl.when(row + 1 < n_row)
    def _():
        one.wait_send()

    @pl.when(row + 2 < n_row)
    def _():
        two.wait_send()

    own.wait()


def window(x, n_row):
    zero = jnp.zeros(x.shape, x.dtype)
    return pl.pallas_call(
        functools.partial(window_body, n_row),
        out_shape=jax.ShapeDtypeStruct((5,) + x.shape, x.dtype),
        in_specs=[ANY, ANY],
        out_specs=ANY,
        scratch_shapes=[
            pltpu.SemaphoreType.DMA((5,)),
            pltpu.SemaphoreType.DMA((5,)),
            pltpu.SemaphoreType.DMA((6,)),
        ],
        compiler_params=comm_params(2),
        cost_estimate=cost_of(0, 1 << 20),
    )(x, zero)


def window_back_body(n_row, win_ref, sum_ref, near_ref, send_ref, far_ref, send_sem, recv_sem):
    row = lax.axis_index("row")
    col, core, _ = neighbours()
    side = lax.rem(col, 2)
    greet(row_partners(row, n_row, core))
    mover = Mover(send_sem, recv_sem)
    first = mover.copy(win_ref.at[1], near_ref.at[0], col=core)
    second = mover.copy(win_ref.at[3], near_ref.at[1], col=core)
    first.start()
    second.start()
    one = mover.copy(send_ref.at[0], far_ref.at[0], row=row - 1)
    two = mover.copy(send_ref.at[1], far_ref.at[1], row=row - 2)
    first.wait_recv()
    second.wait_recv()
    zero = jnp.zeros(near_ref.shape[1:], F32)
    low = near_ref[0].astype(F32)
    high = near_ref[1].astype(F32)
    left = side == 0
    send_ref[0] = (win_ref[2].astype(F32) + jnp.where(left, low, high)).astype(BF)
    send_ref[1] = (win_ref[0].astype(F32) + jnp.where(left, zero, low)).astype(BF)

    @pl.when(row >= 1)
    def _():
        one.start()

    @pl.when(row >= 2)
    def _():
        two.start()

    sum_ref[...] = win_ref[4].astype(F32) + jnp.where(left, high, zero)

    @pl.when(row + 1 < n_row)
    def _():
        one.wait_recv()
        sum_ref[...] += far_ref[0].astype(F32)

    @pl.when(row + 2 < n_row)
    def _():
        two.wait_recv()
        sum_ref[...] += far_ref[1].astype(F32)

    first.wait_send()
    second.wait_send()

    @pl.when(row >= 1)
    def _():
        one.wait_send()

    @pl.when(row >= 2)
    def _():
        two.wait_send()


def window_back(win, n_row):
    shape = win.shape[1:]
    return pl.pallas_call(
        functools.partial(window_back_body, n_row),
        out_shape=jax.ShapeDtypeStruct(shape, F32),
        in_specs=[VMEM],
        out_specs=VMEM,
        scratch_shapes=[
            pltpu.VMEM((2,) + shape, BF),
            pltpu.VMEM((2,) + shape, BF),
            pltpu.VMEM((2,) + shape, BF),
            pltpu.SemaphoreType.DMA((4,)),
            pltpu.SemaphoreType.DMA((4,)),
        ],
        compiler_params=comm_params(7),
        cost_estimate=cost_of(0, 1 << 20),
    )(win)


def front_body(x_ref, gain_ref, blocks_ref, turn_ref, h_ref, hf_ref, bq_ref, kf_ref, q_ref, w_ref):
    parts = x_ref.shape[0]
    feat = x_ref.shape[2]
    n_row = blocks_ref.shape[0]
    ranks_each = RANK_COLS // n_row
    xs = [x_ref[c].astype(F32) for c in range(parts)]
    total = sum(jnp.sum(v * v, axis=1, keepdims=True) for v in xs)
    scale = lax.rsqrt(total / D + EPS)
    for c in range(parts):
        lanes = slice(c * feat, (c + 1) * feat)
        h_ref[:, lanes] = (xs[c] * scale * gain_ref[c, :1]).astype(BF)
        for r in range(n_row):
            w_ref[r * ranks_each : (r + 1) * ranks_each, lanes] = blocks_ref[r, c, :ranks_each]
            w_ref[RANK_COLS + r * GROUP_COLS : RANK_COLS + (r + 1) * GROUP_COLS, lanes] = blocks_ref[
                r, c, ranks_each:
            ]
    both = nt(h_ref[...], w_ref[...])
    heads = both[:, RANK_COLS:]
    hf_ref[...] = heads
    cosine = turn_ref[:, :LANES]
    sine = turn_ref[:, LANES:]
    for tile in range(RANK_COLS // LANES):
        lanes = slice(tile * LANES, (tile + 1) * LANES)
        part = both[:, lanes]
        if tile < 4:
            part = part * cosine + swap_halves(part) * sine
        if tile < 3:
            bq_ref[:, lanes] = part
        else:
            kf_ref[:, (tile - 3) * LANES : (tile - 2) * LANES] = part.astype(BF)
    high = heads.astype(BF)
    low = (heads - high.astype(F32)).astype(BF)
    kf_ref[:, 2 * LANES :] = nn(high, key_columns()).astype(BF)
    ranks = []
    for r in range(RQ):
        tile = bq_ref[:, (r // 2) * LANES : (r // 2 + 1) * LANES]
        ranks.append(double_left(tile) if r % 2 == 0 else double_right(tile))
    width = 2 * LANES
    for p in range(D // width):
        lanes = slice(p * width, (p + 1) * width)
        acc = None
        for r in range(RQ):
            pick = head_spread(2 * RK + r, p * (width // HD), width)
            term = (nn(high, pick) + nn(low, pick)) * jnp.concatenate([ranks[r]] * 2, axis=1)
            acc = term if acc is None else acc + term
        q_ref[:, lanes] = (acc / RQ).astype(BF)


def front(x_parts, gains, blocks, turn):
    rows = x_parts.shape[1]
    return call(
        front_body,
        (
            jax.ShapeDtypeStruct((rows, D), BF),
            jax.ShapeDtypeStruct((rows, HEAD_COLS), F32),
            jax.ShapeDtypeStruct((rows, RQ * HD), F32),
            jax.ShapeDtypeStruct((rows, 2 * LANES + 2 * RK * H), BF),
            jax.ShapeDtypeStruct((rows, D), BF),
            jax.ShapeDtypeStruct((ALL_COLS, D), BF),
        ),
        cost=cost_of(2 * rows * D * 800 * 3, 6 << 20),
    )(x_parts, gains, blocks, turn)


def mask_bias(seg_ref, keys, rows):
    seg_row = seg_ref[...].astype(F32)
    wide = jnp.broadcast_to(seg_row, (LANES, keys))
    column = wide.T
    column = jnp.concatenate([column] * (rows // LANES), axis=1)
    key_idx = lax.broadcasted_iota(jnp.int32, (keys, rows), 0)
    query_idx = lax.broadcasted_iota(jnp.int32, (keys, rows), 1) + (keys - rows)
    same = column == seg_row[:, keys - rows :]
    return jnp.where(same & (key_idx <= query_idx), 0.0, NEG)


def attend_body(fast, q_ref, kf_ref, seg_ref, *refs):
    if fast:
        w_ref, cot_ref, o_ref, lse_ref, k_ref, v_ref, w_rows_ref, cot_near_ref = refs[:8]
        bias_ref, dup_ref, send_sem, recv_sem, local_sem = refs[8:]
        side_work = AttendCopies(w_ref, cot_ref, w_rows_ref, cot_near_ref, send_sem, recv_sem, local_sem)
        side_work.first()
    else:
        o_ref, lse_ref, k_ref, v_ref, bias_ref, dup_ref = refs
    rows = q_ref.shape[0]
    keys = kf_ref.shape[0]
    bias_ref[...] = mask_bias(seg_ref, keys, rows)
    for s in range(2 * RK):
        tile = kf_ref[:, (s // 2) * LANES : (s // 2 + 1) * LANES].astype(F32)
        dup_ref[s] = double_left(tile) if s % 2 == 0 else double_right(tile)

    def pair(p, carried):
        lanes = pl.ds(pl.multiple_of(p * LANES, LANES), LANES)
        weights = kf_ref[:, 2 * LANES :]
        made = []
        for kind in range(2):
            acc = None
            for s in range(RK):
                pick = spread(2 * RK * H, (kind * RK + s) * H + 2 * p, LANES)
                term = nn(weights, pick) * dup_ref[kind * RK + s]
                acc = term if acc is None else acc + term
            made.append((acc / RK).astype(BF))
        k_tile, v_tile = made
        k_ref[:, lanes] = k_tile
        v_ref[:, lanes] = v_tile
        v_turned = v_tile.astype(F32).T.astype(BF)
        q_turned = (q_ref[:, lanes].astype(F32) * HD**-0.5).T
        half = lax.broadcasted_iota(jnp.int32, q_turned.shape, 0) // HD
        outs = []
        for side in range(2):
            q_side = jnp.where(half == side, q_turned, 0.0).astype(BF)
            scores = nn(k_tile, q_side) + bias_ref[...]
            peak = jnp.max(scores, axis=0, keepdims=True)
            weight = jnp.exp(scores - peak)
            total = jnp.sum(weight, axis=0, keepdims=True)
            probs = (weight * (1.0 / total)).astype(BF)
            outs.append(nn(v_turned[side * HD : (side + 1) * HD], probs))
            lse_ref[2 * p + side] = jnp.broadcast_to(peak + jnp.log(total), (8, rows))
        o_ref[:, lanes] = jnp.concatenate(outs, axis=0).T.astype(BF)
        return carried

    if fast:
        lax.fori_loop(0, 5, pair, 0)
        side_work.second()
        lax.fori_loop(5, PAIRS, pair, 0)
        side_work.last()
    else:
        lax.fori_loop(0, PAIRS, pair, 0)


def attend(q, kf_window, seg_window, w_own=None, cot=None):
    rows = q.shape[0]
    keys = kf_window.shape[0]
    fast = w_own is not None
    outs = [
        jax.ShapeDtypeStruct((rows, D), BF),
        jax.ShapeDtypeStruct((H, 8, rows), F32),
        jax.ShapeDtypeStruct((keys, D), BF),
        jax.ShapeDtypeStruct((keys, D), BF),
    ]
    scratch = [pltpu.VMEM((keys, rows), F32), pltpu.VMEM((2 * RK, keys, LANES), F32)]
    in_specs, out_specs, more = [VMEM] * 3, [VMEM] * 4, []
    if fast:
        outs += [jax.ShapeDtypeStruct((4,) + w_own.shape, BF), jax.ShapeDtypeStruct((4,) + cot.shape, BF)]
        in_specs += [ANY] * 2
        out_specs += [ANY] * 2
        more = [w_own, cot]
        scratch += [
            pltpu.SemaphoreType.DMA((7,)),
            pltpu.SemaphoreType.DMA((7,)),
            pltpu.SemaphoreType.DMA((2,)),
        ]
    return pl.pallas_call(
        functools.partial(attend_body, fast),
        out_shape=tuple(outs),
        in_specs=in_specs,
        out_specs=tuple(out_specs),
        scratch_shapes=scratch,
        compiler_params=comm_params(3) if fast else params(),
        cost_estimate=cost_of(2 * rows * keys * D * 16, 16 << 20),
    )(q, kf_window, seg_window, *more)


def attend_back_body(fast, q_ref, k_ref, v_ref, do_ref, lse_ref, kf_ref, seg_ref, *refs):
    if fast:
        parts_ref, grads_ref, dq_ref, dkf_ref, out_ref, got_ref = refs[:6]
        bias_ref, dup_ref, sum_ref, fac_ref, send_sem, recv_sem, local_sem = refs[6:]
        side_work = BackCopies(parts_ref, grads_ref, out_ref, got_ref, send_sem, recv_sem, local_sem)
        side_work.first()
    else:
        dq_ref, dkf_ref, bias_ref, dup_ref, sum_ref, fac_ref = refs
    rows = q_ref.shape[0]
    keys = kf_ref.shape[0]
    bias_ref[...] = mask_bias(seg_ref, keys, rows)
    for s in range(2 * RK):
        tile = kf_ref[:, (s // 2) * LANES : (s // 2 + 1) * LANES].astype(F32)
        dup_ref[s] = double_left(tile) if s % 2 == 0 else double_right(tile)
    sum_ref[...] = jnp.zeros_like(sum_ref)
    fac_ref[...] = jnp.zeros_like(fac_ref)

    def pair(p, carried):
        lanes = pl.ds(pl.multiple_of(p * LANES, LANES), LANES)
        k_tile = k_ref[:, lanes]
        v_tile = v_ref[:, lanes]
        k_turned = k_tile.astype(F32).T.astype(BF)
        q_tile = q_ref[:, lanes].astype(F32) * HD**-0.5
        do_tile = do_ref[:, lanes].astype(F32)
        q_turned = q_tile.T
        do_turned = do_tile.T
        half = lax.broadcasted_iota(jnp.int32, q_turned.shape, 0) // HD
        lane_half = lax.broadcasted_iota(jnp.int32, q_tile.shape, 1) // HD
        d_k = None
        d_v = None
        d_q = []
        for side in range(2):
            q_side = jnp.where(half == side, q_turned, 0.0).astype(BF)
            do_side = jnp.where(half == side, do_turned, 0.0).astype(BF)
            scores = nn(k_tile, q_side) + bias_ref[...]
            probs = jnp.exp(scores - lse_ref[2 * p + side][:1])
            d_prob = nn(v_tile, do_side)
            delta = jnp.sum(probs * d_prob, axis=0, keepdims=True)
            d_score = (probs * (d_prob - delta)).astype(BF)
            d_q.append(nn(k_turned[side * HD : (side + 1) * HD], d_score))
            q_back = jnp.where(lane_half == side, q_tile, 0.0).astype(BF)
            do_back = jnp.where(lane_half == side, do_tile, 0.0).astype(BF)
            part_k = nn(d_score, q_back)
            part_v = nn(probs.astype(BF), do_back)
            d_k = part_k if d_k is None else d_k + part_k
            d_v = part_v if d_v is None else d_v + part_v
        dq_ref[:, lanes] = jnp.concatenate(d_q, axis=0).T * HD**-0.5
        weights = kf_ref[:, 2 * LANES :]
        for kind, grad in ((0, d_k), (1, d_v)):
            for s in range(RK):
                slot = kind * RK + s
                pick = spread(2 * RK * H, slot * H + 2 * p, LANES)
                sum_ref[slot] += nn(weights, pick) * grad
                fac_ref[...] += two_pass(grad * dup_ref[slot], collect(LANES, 2 * RK * H, slot * H + 2 * p))
        return carried

    lax.fori_loop(0, PAIRS, pair, 0)
    for tile in range(2):
        first = sum_ref[2 * tile]
        second = sum_ref[2 * tile + 1]
        first = first + pltpu.roll(first, HD, 1)
        second = second + pltpu.roll(second, HD, 1)
        merged = jnp.where(lane_iota(first.shape) < HD, first, second)
        dkf_ref[:, tile * LANES : (tile + 1) * LANES] = (merged / RK).astype(BF)
    dkf_ref[:, 2 * LANES :] = (fac_ref[...] / RK).astype(BF)
    if fast:
        side_work.last()


def attend_back(q, k, v, d_heads, lse, kf_window, seg_window, out_parts=None, grads=None):
    rows = q.shape[0]
    keys = kf_window.shape[0]
    fast = grads is not None
    outs = [jax.ShapeDtypeStruct((rows, D), F32), jax.ShapeDtypeStruct(kf_window.shape, BF)]
    scratch = [
        pltpu.VMEM((keys, rows), F32),
        pltpu.VMEM((2 * RK, keys, LANES), F32),
        pltpu.VMEM((2 * RK, keys, LANES), F32),
        pltpu.VMEM((keys, 2 * RK * H), F32),
    ]
    in_specs, out_specs, more = [VMEM] * 7, [VMEM] * 2, []
    if fast:
        outs += [
            jax.ShapeDtypeStruct(out_parts.shape, BF),
            jax.ShapeDtypeStruct((2,) + grads.shape[1:], BF),
        ]
        in_specs += [ANY] * 2
        out_specs += [ANY] * 2
        more = [out_parts, grads]
        scratch += [
            pltpu.SemaphoreType.DMA((5,)),
            pltpu.SemaphoreType.DMA((5,)),
            pltpu.SemaphoreType.DMA,
        ]
    return pl.pallas_call(
        functools.partial(attend_back_body, fast),
        out_shape=tuple(outs),
        in_specs=in_specs,
        out_specs=tuple(out_specs),
        scratch_shapes=scratch,
        compiler_params=comm_params(6) if fast else params(),
        cost_estimate=cost_of(2 * rows * keys * D * 40, 16 << 20),
    )(q, k, v, d_heads, lse, kf_window, seg_window, *more)


def mixing_body(x_ref, heads_ref, w_out_ref, gain_ref, mixed_ref, h_ref):
    parts, _, feat = x_ref.shape
    rows_of = w_out_ref.shape[0]
    head_rows = w_out_ref.shape[2]
    total = None
    for c in range(parts):
        lanes = slice(c * feat, (c + 1) * feat)
        acc = x_ref[c].astype(F32)
        for r in range(rows_of):
            acc = acc + nn(heads_ref[:, r * head_rows : (r + 1) * head_rows], w_out_ref[r, c])
        mixed_ref[:, lanes] = acc
        part = jnp.sum(acc * acc, axis=1, keepdims=True)
        total = part if total is None else total + part
    scale = lax.rsqrt(total / D + EPS)
    for c in range(parts):
        lanes = slice(c * feat, (c + 1) * feat)
        h_ref[:, lanes] = (mixed_ref[:, lanes] * scale * gain_ref[c, 1:2]).astype(BF)


def mixing(x_parts, heads, w_out, gains):
    rows = heads.shape[0]
    return call(
        mixing_body,
        (jax.ShapeDtypeStruct((rows, D), F32), jax.ShapeDtypeStruct((rows, D), BF)),
        cost=cost_of(2 * rows * D * D, 5 << 20),
    )(x_parts, heads, w_out, gains)


def ffn_steps(blocks, h_at, cot_at, w_ref, hid_ref, dg_ref, du_ref, out_at, back_at):
    def block(t, carried):
        h = h_at(t)[...]
        gate = nt(h, w_ref[0])
        up = nt(h, w_ref[1])
        d_hidden = nt(cot_at(t)[...], w_ref[2])
        sig = 1.0 / (1.0 + jnp.exp(-gate))
        silu = gate * sig
        hidden = (silu * up).astype(BF)
        d_gate = (d_hidden * up * sig * (1.0 + gate * (1.0 - sig))).astype(BF)
        d_up = (d_hidden * silu).astype(BF)
        rows = h.shape[0]
        place = pl.ds(pl.multiple_of(t * rows, rows), rows)
        hid_ref[place] = hidden
        dg_ref[place] = d_gate
        du_ref[place] = d_up
        out_at(t)[...] = nn(hidden, w_ref[2]).astype(BF)
        back_at(t)[...] = (nn(d_gate, w_ref[0]) + nn(d_up, w_ref[1])).astype(BF)
        return carried

    lax.fori_loop(0, blocks, block, 0)


def ffn_body(h_ref, cot_ref, w_ref, out_ref, back_ref, g_ref, hid_ref, dg_ref, du_ref):
    parts, rows, _ = h_ref.shape
    ffn_steps(
        parts, lambda t: h_ref.at[t], lambda t: cot_ref.at[t], w_ref, hid_ref, dg_ref, du_ref,
        lambda t: out_ref.at[t], lambda t: back_ref.at[t],
    )
    h_all = h_ref[...].reshape(parts * rows, D)
    cot_all = cot_ref[...].reshape(parts * rows, D)
    for place, (left, right) in enumerate(((dg_ref, h_all), (du_ref, h_all), (hid_ref, cot_all))):
        g_ref[place] = tn(left[...], right).astype(BF)


def ffn(h_all, cot_all, w):
    parts, rows, _ = h_all.shape
    units = w.shape[1]
    return call(
        ffn_body,
        (
            jax.ShapeDtypeStruct(h_all.shape, BF),
            jax.ShapeDtypeStruct(h_all.shape, BF),
            jax.ShapeDtypeStruct(w.shape, BF),
        ),
        scratch=[pltpu.VMEM((parts * rows, units), BF)] * 3,
        cost=cost_of(2 * parts * rows * 9 * D * units, 20 << 20),
    )(h_all, cot_all, w)


def ffn_square_body(
    near_ref, far_ref, cot_near_ref, cot_far_ref, rows_ref, last_ref,
    out_ref, back_ref, g_ref, cot_own_ref,
    w_ref, h_ref, cot_ref, hid_ref, dg_ref, du_ref, w_sem, h_sem, cot_sem,
):
    row = lax.axis_index("row")
    col = lax.axis_index("col")
    _, spots = square()
    core = lax.rem(col, 2)
    parts, _, units, feat = rows_ref.shape[1:]
    rows = near_ref.shape[1]
    waits = []
    for r in range(4):
        is_last = jnp.logical_or(jnp.logical_and(row == 3, r == 0), jnp.logical_and(row == 0, r == 3))
        for c in range(parts):
            target = w_ref.at[:, pl.ds(r * units, units), pl.ds(c * feat, feat)]
            kept = pltpu.make_async_copy(rows_ref.at[r, c], target, w_sem.at[r, c])
            late = pltpu.make_async_copy(last_ref.at[c], target, w_sem.at[r, c])
            pl.when(jnp.logical_not(is_last))(kept.start)
            pl.when(is_last)(late.start)
            waits.append(kept)
    for side, source in ((0, near_ref), (1, far_ref)):
        c = pltpu.make_async_copy(source, h_ref.at[side], h_sem.at[side])
        c.start()
        waits.append(c)
    for side, source in ((0, cot_near_ref), (1, cot_far_ref)):
        from_core = lax.rem(core + side, 2)
        for q in range(4):
            lanes = pl.ds(pl.multiple_of((q % 2 * 2 + from_core) * feat, feat), feat)
            for c in range(4):
                to = lax.rem(core + c, 2)
                copy = pltpu.make_async_copy(
                    source.at[q, pl.ds(c * rows, rows)],
                    cot_ref.at[to, q // 2 * 2 + c // 2, :, lanes],
                    cot_sem.at[side, q, c],
                )
                copy.start()
                waits.append(copy)
    for c in waits:
        c.wait()
    cot_own_ref[...] = cot_ref[0, spots[0]]
    ffn_steps(
        8, lambda t: h_ref.at[t // 4, lax.rem(t, 4)], lambda t: cot_ref.at[t // 4, lax.rem(t, 4)],
        w_ref, hid_ref, dg_ref, du_ref,
        lambda t: out_ref.at[t // 4, lax.rem(t, 4)], lambda t: back_ref.at[t // 4, lax.rem(t, 4)],
    )
    h_all = h_ref[...].reshape(8 * rows, D)
    cot_all = cot_ref[...].reshape(8 * rows, D)
    for place, (left, right) in enumerate(((dg_ref, h_all), (du_ref, h_all), (hid_ref, cot_all))):
        grad = tn(left[...], right)
        for r in range(4):
            g_ref[r, place] = grad[r * units : (r + 1) * units].astype(BF)


def ffn_square(near, far, cot_near, cot_far, w_rows, w_last):
    rows = near.shape[1]
    units = w_rows.shape[3]
    both = jax.ShapeDtypeStruct((2, 4, rows, D), BF)
    return pl.pallas_call(
        ffn_square_body,
        out_shape=(
            both,
            both,
            jax.ShapeDtypeStruct((4, 3, units, D), BF),
            jax.ShapeDtypeStruct((rows, D), BF),
        ),
        in_specs=[ANY] * 6,
        out_specs=(VMEM,) * 4,
        scratch_shapes=[
            pltpu.VMEM((3, 4 * units, D), BF),
            pltpu.VMEM((2, 4, rows, D), BF),
            pltpu.VMEM((2, 4, rows, D), BF),
        ]
        + [pltpu.VMEM((8 * rows, 4 * units), BF)] * 3
        + [
            pltpu.SemaphoreType.DMA((4, 4)),
            pltpu.SemaphoreType.DMA((2,)),
            pltpu.SemaphoreType.DMA((2, 4, 4)),
        ],
        compiler_params=params(),
        cost_estimate=cost_of(2 * 8 * rows * 9 * D * 4 * units, 24 << 20),
    )(near, far, cot_near, cot_far, w_rows, w_last)


def unmix_math(
    mixed_ref, cot_ref, d_h, heads_ref, w_out_ref, gain_ref, d_mixed_ref, d_heads_ref, g_out_ref, g_gain_ref
):
    rows_of, parts, head_rows, feat = w_out_ref.shape
    mixed = mixed_ref[...]
    scale = lax.rsqrt(jnp.sum(mixed * mixed, axis=1, keepdims=True) / D + EPS)
    normed = mixed * scale
    g_gain_ref[...] = jnp.sum(d_h * normed, axis=0, keepdims=True)
    gain = jnp.concatenate([gain_ref[c, 1:2] for c in range(parts)], axis=1)
    inner = d_h * gain
    dot = jnp.sum(inner * normed, axis=1, keepdims=True) / D
    d_mixed = cot_ref[...].astype(F32) + scale * (inner - normed * dot)
    d_mixed_ref[...] = d_mixed
    low = d_mixed.astype(BF)
    grad = tn(heads_ref[...], low)
    for r in range(rows_of):
        acc = None
        for c in range(parts):
            lanes = slice(c * feat, (c + 1) * feat)
            term = nt(low[:, lanes], w_out_ref[r, c])
            acc = term if acc is None else acc + term
            g_out_ref[r, c] = grad[r * head_rows : (r + 1) * head_rows, lanes].astype(BF)
        d_heads_ref[:, r * head_rows : (r + 1) * head_rows] = acc.astype(BF)


def write_output(mixed_ref, total, out_ref):
    parts, _, feat = out_ref.shape
    for c in range(parts):
        lanes = slice(c * feat, (c + 1) * feat)
        out_ref[c] = (mixed_ref[:, lanes] + total[:, lanes]).astype(BF)


def unmix_body(
    dh_ref, sum_ref, mixed_ref, cot_ref, heads_ref, w_out_ref, gain_ref,
    out_ref, d_mixed_ref, d_heads_ref, g_out_ref, g_gain_ref,
):
    unmix_math(
        mixed_ref, cot_ref, dh_ref[...], heads_ref, w_out_ref, gain_ref,
        d_mixed_ref, d_heads_ref, g_out_ref, g_gain_ref,
    )
    write_output(mixed_ref, sum_ref[...], out_ref)


def unmix_square_body(
    dh_ref, sum_ref, mixed_ref, cot_ref, heads_ref, w_out_ref, gain_ref, g_ref,
    out_ref, d_mixed_ref, d_heads_ref, g_out_ref, g_gain_ref, got_ref,
    near_ref, pair_ref, diag_ref, far_ref, send_sem, recv_sem,
):
    row = lax.axis_index("row")
    col, core, across = neighbours()
    dp, spots = square()
    third = lax.rem(row + 2, 4)
    greet(
        [(None, {"col": core}), (None, {"col": across}), (None, {"dp": 1 - dp}), (None, {"row": third})]
    )
    mover = Mover(send_sem, recv_sem)
    sums = [
        SquareSum(mover, part, near_ref.at[k], pair_ref.at[k], diag_ref.at[k], far_ref.at[k])
        for k, part in enumerate((dh_ref, sum_ref))
    ]
    for one in sums:
        one.near(core, spots)
    grads = mover.copy(g_ref.at[third], got_ref, row=third)
    grads.start()
    for one in sums:
        one.send(dp, across)
    unmix_math(
        mixed_ref, cot_ref, sums[0].total(), heads_ref, w_out_ref, gain_ref,
        d_mixed_ref, d_heads_ref, g_out_ref, g_gain_ref,
    )
    write_output(mixed_ref, sums[1].total(), out_ref)
    for one in sums:
        one.end()
    grads.wait()


def unmix(dh, out_sum, mixed, cot_own, heads, w_out, gains, grads=None):
    rows = heads.shape[0]
    parts, feat = w_out.shape[1], w_out.shape[3]
    outs = [
        jax.ShapeDtypeStruct((parts, rows, feat), BF),
        jax.ShapeDtypeStruct((rows, D), F32),
        jax.ShapeDtypeStruct((rows, D), BF),
        jax.ShapeDtypeStruct(w_out.shape, BF),
        jax.ShapeDtypeStruct((1, D), F32),
    ]
    cost = cost_of(4 * rows * D * D, 18 << 20)
    if grads is None:
        return call(unmix_body, tuple(outs), cost=cost)(dh, out_sum, mixed, cot_own, heads, w_out, gains)
    count = 2 * 10 + 1
    return pl.pallas_call(
        unmix_square_body,
        out_shape=tuple(outs) + (jax.ShapeDtypeStruct(grads.shape[1:], BF),),
        in_specs=[VMEM] * 7 + [ANY],
        out_specs=(VMEM,) * 5 + (ANY,),
        scratch_shapes=[
            pltpu.VMEM((2, 4, rows, D), BF),
            pltpu.VMEM((2, 4, rows, D), BF),
            pltpu.VMEM((2, 2, rows // 2, D), BF),
            pltpu.VMEM((2, 2, rows, D), BF),
            pltpu.SemaphoreType.DMA((count,)),
            pltpu.SemaphoreType.DMA((count,)),
        ],
        compiler_params=comm_params(5),
        cost_estimate=cost,
    )(dh, out_sum, mixed, cot_own, heads, w_out, gains, grads)


def back_body(
    fast, dq_ref, dkf_ref, hf_ref, bq_ref, turn_ref, w_ref, h_ref, x_ref, gain_ref, d_mixed_ref, g_two_ref, *refs
):
    if fast:
        g_own_ref, g_mid_ref, g_ends_ref, gi_ref, g_ref, cols_ref, d_ref, send_ref, send_sem, recv_sem = refs
        row = lax.axis_index("row")
        col, core, across = neighbours()
        cross = lax.rem(core + 2, 4)
        greet([(None, {"col": c}) for c in (core, across, cross)])
        mover = Mover(send_sem, recv_sem)
        width = x_ref.shape[2]
        for place in range(3):
            total = (
                g_own_ref[row, place].astype(F32)
                + g_mid_ref[place].astype(F32)
                + g_ends_ref[0, place].astype(F32)
                + g_ends_ref[1, place].astype(F32)
            ).astype(BF)
            for c in range(4):
                send_ref[c, place] = total[:, c * width : (c + 1) * width]
        copies = [mover.copy(send_ref.at[c], cols_ref.at[col], col=c) for c in (across, cross, core)]
        for c in copies:
            c.start()
        cols_ref[col] = send_ref[col]
    else:
        gi_ref, g_ref, d_ref = refs
    parts, rows, feat = x_ref.shape
    heads = hf_ref[...]
    high = heads.astype(BF)
    low = (heads - high.astype(F32)).astype(BF)
    dq = dq_ref[...] * (1.0 / RQ)
    cosine = turn_ref[:, :LANES]
    sine = turn_ref[:, LANES:]
    d_fac = jnp.zeros((rows, HEAD_COLS), F32)
    folded = []
    for r in range(RQ):
        tile = bq_ref[:, (r // 2) * LANES : (r // 2 + 1) * LANES]
        rank = double_left(tile) if r % 2 == 0 else double_right(tile)
        product = dq * jnp.concatenate([rank] * PAIRS, axis=1)
        d_fac = d_fac + two_pass(product, head_collect(2 * RK + r))
        pick = head_spread(2 * RK + r, 0, D)
        terms = (nn(high, pick) + nn(low, pick)) * dq
        acc = terms[:, :LANES]
        for p in range(1, PAIRS):
            acc = acc + terms[:, p * LANES : (p + 1) * LANES]
        folded.append(acc + pltpu.roll(acc, HD, 1))
    lane = lane_iota(folded[0].shape)

    def turn_back(part):
        return part * cosine - swap_halves(part) * sine

    for tile in range(3):
        merged = jnp.where(lane < HD, folded[2 * tile], folded[2 * tile + 1])
        d_ref[:, tile * LANES : (tile + 1) * LANES] = turn_back(merged).astype(BF)
    d_ref[:, 3 * LANES : 4 * LANES] = turn_back(dkf_ref[:, :LANES].astype(F32)).astype(BF)
    d_ref[:, 4 * LANES : 5 * LANES] = dkf_ref[:, LANES : 2 * LANES].astype(BF)
    key_low = dkf_ref[:, 2 * LANES :].astype(BF)
    d_fac = d_fac.astype(BF).astype(F32) + nt(key_low, key_columns())
    d_ref[:, RANK_COLS:] = d_fac.astype(BF)
    d_all = d_ref[...]
    d_h = nn(d_all, w_ref[...])
    xs = [x_ref[c].astype(F32) for c in range(parts)]
    total = sum(jnp.sum(v * v, axis=1, keepdims=True) for v in xs)
    scale = lax.rsqrt(total / D + EPS)
    dot = None
    gains = []
    for c in range(parts):
        lanes = slice(c * feat, (c + 1) * feat)
        normed = xs[c] * scale
        grad = d_h[:, lanes]
        gains.append(jnp.sum(grad * normed, axis=0, keepdims=True))
        part = jnp.sum(grad * gain_ref[c, :1] * normed, axis=1, keepdims=True)
        dot = part if dot is None else dot + part
    for c in range(parts):
        lanes = slice(c * feat, (c + 1) * feat)
        normed = xs[c] * scale
        gi_ref[c] = d_mixed_ref[:, lanes] + scale * (
            d_h[:, lanes] * gain_ref[c, :1] - normed * (dot / D)
        )
    grad = tn(d_all, h_ref[...])
    n_row = g_ref.shape[0]
    ranks_each = RANK_COLS // n_row
    used = FAC * GROUP
    for c in range(parts):
        lanes = slice(c * feat, (c + 1) * feat)
        tail = jnp.concatenate(
            [gains[c], g_two_ref[:, lanes], jnp.zeros((GROUP_COLS - used - 2, feat), F32)], axis=0
        )
        for r in range(n_row):
            first = RANK_COLS + r * GROUP_COLS
            g_ref[r, c, :ranks_each] = grad[r * ranks_each : (r + 1) * ranks_each, lanes].astype(BF)
            g_ref[r, c, ranks_each:] = jnp.concatenate([grad[first : first + used, lanes], tail], axis=0).astype(BF)
    if fast:
        for c in copies:
            c.wait()


def back(dq, dkf, hf, bq, turn, w_rh, h, x_parts, gains, d_mixed, g_two, n_row, grads=None):
    rows = dq.shape[0]
    parts, _, feat = x_parts.shape
    each = RANK_COLS // n_row + GROUP_COLS
    outs = [jax.ShapeDtypeStruct(x_parts.shape, F32), jax.ShapeDtypeStruct((n_row, parts, each, feat), BF)]
    scratch = [pltpu.VMEM((rows, ALL_COLS), BF)]
    more = []
    fast = grads is not None
    if fast:
        units = grads[0].shape[2]
        cols = (4, 3, units, feat)
        outs.append(jax.ShapeDtypeStruct(cols, BF))
        more = list(grads)
        scratch += [
            pltpu.VMEM(cols, BF),
            pltpu.SemaphoreType.DMA((3,)),
            pltpu.SemaphoreType.DMA((3,)),
        ]
    return pl.pallas_call(
        functools.partial(back_body, fast),
        out_shape=tuple(outs),
        in_specs=[VMEM] * (11 + len(more)),
        out_specs=(VMEM,) * len(outs),
        scratch_shapes=scratch,
        compiler_params=comm_params(8) if fast else params(),
        cost_estimate=cost_of(2 * rows * D * 800 * 6, 12 << 20),
    )(dq, dkf, hf, bq, turn, w_rh, h, x_parts, gains, d_mixed, g_two, *more)


def finish_body(
    g_ref, gi_ref, cols_ref, out_ref,
    grad_ref, gi_all_ref, cols_other_ref, out_other_ref,
    near_ref, pair_ref, far_ref, side_ref, down_ref, last_ref, end_ref, send_sem, recv_sem, local_sem,
):
    row = lax.axis_index("row")
    col, core, across = neighbours()
    cross = lax.rem(core + 2, 4)
    dp = lax.axis_index("dp")
    x, mine = col // 2, lax.rem(col, 2)
    rows = [lax.rem(row + k, 4) for k in range(4)]
    greet(
        [(None, {"col": c}) for c in (core, across, cross)]
        + [(None, {"row": r}) for r in rows[1:]]
        + [(None, {"dp": 1 - dp})]
    )
    mover = Mover(send_sem, recv_sem)
    started = []

    def go(source, target, **place):
        c = mover.copy(source, target, **place)
        c.start()
        started.append(c)
        return c

    first = [go(g_ref.at[r, (1 - x) * 2 + 1 - mine], near_ref.at[0, r], col=core) for r in range(4)]
    second = [go(g_ref.at[r, x * 2 + 1 - mine], near_ref.at[1, r], col=core) for r in range(4)]
    rest = [
        go(cols_ref, cols_other_ref, dp=1 - dp),
        go(out_ref, out_other_ref, dp=1 - dp),
    ]
    sides = []
    for r in range(4):
        first[r].wait_recv()
        pair_ref[r] = (g_ref[r, (1 - x) * 2 + mine].astype(F32) + near_ref[0, r].astype(F32)).astype(BF)
        sides.append(go(pair_ref.at[r], side_ref.at[r], col=across))
    for c in (across, cross, core):
        rest.append(go(gi_ref.at[c], gi_all_ref.at[col], col=c))
    own = pltpu.make_async_copy(gi_ref.at[col], gi_all_ref.at[col], local_sem)
    own.start()
    for r in range(4):
        second[r].wait_recv()
        sides[r].wait_recv()
        far_ref[r] = (
            g_ref[r, x * 2 + mine].astype(F32) + near_ref[1, r].astype(F32) + side_ref[r].astype(F32)
        ).astype(BF)
    downs = [go(far_ref.at[rows[k]], down_ref.at[k - 1], row=rows[k]) for k in range(1, 4)]
    total = far_ref[row].astype(F32)
    for k in range(3):
        downs[k].wait_recv()
        total = total + down_ref[k].astype(F32)
    last_ref[...] = total.astype(BF)
    end = go(last_ref, end_ref, dp=1 - dp)
    end.wait_recv()
    grad_ref[...] = last_ref[...].astype(F32) + end_ref[...].astype(F32)
    for c in rest:
        c.wait_recv()
    for c in started:
        c.wait_send()
    own.wait()


def finish(g, gi_parts, cols, g_out):
    block = g.shape[2:]
    count = 8 + 2 + 4 + 3 + 3 + 1
    return pl.pallas_call(
        finish_body,
        out_shape=(
            jax.ShapeDtypeStruct(block, F32),
            jax.ShapeDtypeStruct(gi_parts.shape, gi_parts.dtype),
            jax.ShapeDtypeStruct(cols.shape, BF),
            jax.ShapeDtypeStruct(g_out.shape, BF),
        ),
        in_specs=[VMEM, ANY, ANY, ANY],
        out_specs=(VMEM, ANY, ANY, ANY),
        scratch_shapes=[
            pltpu.VMEM((2, 4) + block, BF),
            pltpu.VMEM((4,) + block, BF),
            pltpu.VMEM((4,) + block, BF),
            pltpu.VMEM((4,) + block, BF),
            pltpu.VMEM((3,) + block, BF),
            pltpu.VMEM(block, BF),
            pltpu.VMEM(block, BF),
            pltpu.SemaphoreType.DMA((count,)),
            pltpu.SemaphoreType.DMA((count,)),
            pltpu.SemaphoreType.DMA,
        ],
        compiler_params=comm_params(9),
        cost_estimate=cost_of(0, 10 << 20),
    )(g, gi_parts, cols, g_out)


def local(
    tokens_in, segments, gain_attn, gain_ffn, w_heads, w_ranks, w_out, w_gate, w_up, w_down, cotangent
):
    n_row = lax.axis_size("row")
    n_col = lax.axis_size("col")
    row = lax.axis_index("row")
    col = lax.axis_index("col")
    micro, row_tokens, feat = tokens_in.shape
    subs = n_col // micro
    rows = row_tokens // subs
    length = row_tokens * n_row
    head_local = w_heads.shape[1] // FAC
    rank_local = w_ranks.shape[1]
    ffn_local = w_gate.shape[1]
    out_local = w_out.shape[0]
    block = row * subs + col % subs
    past = min(-(-(MAX_DOC - 1) // rows), n_row * subs - 1)
    keys = (past + 1) * rows

    dp_count = lax.axis_size("dp")
    fast = n_col == 4 and n_row == 4 and dp_count == 2 and micro == 2 and past == 4

    heads_t = jnp.transpose(w_heads.reshape(feat, head_local, FAC), (2, 1, 0))
    heads_t = heads_t[jnp.array(FAC_ORDER)].reshape(FAC * head_local, feat)
    pad = jnp.zeros((GROUP_COLS - FAC * head_local, feat), BF)
    w_own = jnp.concatenate([w_ranks.T, heads_t, pad], axis=0)
    gains_own = jnp.concatenate([gain_attn[None], gain_ffn[None], jnp.zeros((6, feat), F32)], axis=0)
    tokens = tokens_in.reshape(n_col, rows, feat)
    if fast:
        dp = lax.axis_index("dp")
        part = ffn_local // (2 * n_col)
        units = -(-part // 16) * 16
        ffn_own = jnp.stack([w_gate.T, w_up.T, w_down]).reshape(3, 2, n_col, part, feat)
        ffn_own = jnp.transpose(lax.dynamic_index_in_dim(ffn_own, dp, 1, False), (1, 0, 2, 3))
        ffn_own = jnp.pad(ffn_own, ((0, 0), (0, 0), (0, units - part), (0, 0)))
        x_parts, w_blocks, gains, ffn_parts = start(tokens, w_own, gains_own, ffn_own)
        w_out, x_parts = lax.optimization_barrier((w_out, x_parts))
    else:
        part = ffn_local // n_col
        units = part * n_row
        w_ffn = jnp.stack([w_gate.T, w_up.T, w_down]).reshape(3, n_col, part, feat)
        w_ffn = lax.all_to_all(jnp.transpose(w_ffn, (1, 0, 2, 3)), "col", 0, 0, tiled=True)
        w_ffn = jnp.transpose(w_ffn, (1, 2, 0, 3)).reshape(3, part, D)
        w_ffn = jnp.transpose(lax.all_gather(w_ffn, "row", axis=0), (1, 0, 2, 3)).reshape(3, units, D)
        w_blocks = lax.all_gather(w_own, ("row", "col"), axis=0).reshape((n_row, n_col) + w_own.shape)
        gains = lax.all_gather(gains_own, "col", axis=0)
        x_parts = lax.all_to_all(tokens, "col", 0, 0, tiled=True)
    w_out_all = lax.all_gather(w_out, ("row", "col"), axis=0).reshape((n_row, n_col) + w_out.shape)

    seg_row = lax.dynamic_index_in_dim(segments, col // subs, 0, keepdims=False)
    padded = jnp.concatenate([jnp.full((1, past * rows), -1, jnp.int32), seg_row], axis=1)
    seg_window = lax.dynamic_slice_in_dim(padded, block * rows, keys, 1)
    own_seg = seg_window[0, past * rows :]
    key_idx = jnp.arange(keys, dtype=jnp.int32)
    query_idx = jnp.arange(rows, dtype=jnp.int32) + past * rows
    before = (own_seg[:, None] == seg_window) & (key_idx[None, :] < query_idx[:, None])
    places = jnp.sum(before.astype(jnp.int32), axis=1)
    inverse = ROPE ** (-(jnp.arange(HD // 2, dtype=F32) * 2.0 / HD))
    angles = places.astype(F32)[:, None] * inverse[None, :]
    cosine = jnp.cos(angles)
    sine = jnp.sin(angles)
    turn = jnp.concatenate([cosine] * 4 + [-sine, sine, -sine, sine], axis=1)

    h_one, head_fac, bq_rot, key_fac, queries, w_rh = front(x_parts, gains, w_blocks, turn)

    groups = [[m * subs + s for s in range(subs)] for m in range(micro)]
    if fast:
        kf_window = window(key_fac, n_row).reshape(keys, -1)
        cot_rows = cotangent.reshape(micro * row_tokens, feat)
        heads_out, lse, key_all, value_all, w_rows, cot_near = attend(
            queries, kf_window, seg_window, ffn_parts, cot_rows
        )
        mixed, h_two = mixing(x_parts, heads_out, w_out_all, gains)
        h_near, h_far, cot_far, w_last = gather(h_two, cot_near, w_rows)
        out_part, dh_part, g_rows, cot_own = ffn_square(h_near, h_far, cot_near, cot_far, w_rows, w_last)
        out_parts, d_mixed, d_heads, g_out, g_gain_two, g_mid = unmix(
            dh_part, out_part, mixed, cot_own, heads_out, w_out_all, gains, g_rows
        )
        d_q, d_kf, output, g_ends = attend_back(
            queries, key_all, value_all, d_heads, lse, kf_window, seg_window, out_parts, g_rows
        )
        own_kf = window_back(d_kf.reshape(past + 1, rows, -1), n_row)
        g_out = lax.psum_scatter(
            g_out.reshape((n_row * n_col,) + w_out.shape), ("row", "col"), scatter_dimension=0, tiled=False
        )
        own_kf, g_out = lax.optimization_barrier((own_kf, g_out))
        gi_parts, g_rh, g_cols = back(
            d_q, own_kf, head_fac, bq_rot, turn, w_rh, h_one, x_parts, gains, d_mixed, g_gain_two, n_row,
            (g_rows, g_mid, g_ends),
        )
        g_rh, grad_input, cols_other, out_other = finish(g_rh, gi_parts, g_cols, g_out)
        g_out = g_out.astype(F32) + out_other.astype(F32)
        g_ffn = jnp.where(dp == 0, jnp.stack([g_cols, cols_other]), jnp.stack([cols_other, g_cols]))
        g_ffn = jnp.transpose(g_ffn[:, :, :, :part], (2, 0, 1, 3, 4)).reshape(3, ffn_local, feat).astype(F32)
    else:
        gathered = lax.all_gather(key_fac, "row", axis=0)
        gathered = lax.all_gather(gathered, "col", axis=1, axis_index_groups=groups)
        gathered = gathered.reshape(length, key_fac.shape[1])
        padded_kf = jnp.concatenate([jnp.zeros((past * rows, key_fac.shape[1]), BF), gathered], axis=0)
        kf_window = lax.dynamic_slice_in_dim(padded_kf, block * rows, keys, 0)
        heads_out, lse, key_all, value_all = attend(queries, kf_window, seg_window)
        mixed, h_two = mixing(x_parts, heads_out, w_out_all, gains)
        cot_own = lax.all_to_all(cotangent.reshape(n_col, rows, feat), "col", 0, 0, tiled=True)
        cot_own = jnp.transpose(cot_own, (1, 0, 2)).reshape(rows, D)
        cot_all = lax.all_gather(cot_own, "col", axis=0)
        h_all = lax.all_gather(h_two, "col", axis=0)
        out_part, dh_part, g_ffn = ffn(h_all, cot_all, w_ffn)
        dh_sum = lax.psum_scatter(dh_part, "col", scatter_dimension=0, tiled=False).astype(F32)
        out_sum = lax.psum_scatter(out_part, "col", scatter_dimension=0, tiled=False).astype(F32)
        out_parts, d_mixed, d_heads, g_out, g_gain_two = unmix(
            dh_sum, out_sum, mixed, cot_own, heads_out, w_out_all, gains
        )
        d_q, d_kf = attend_back(queries, key_all, value_all, d_heads, lse, kf_window, seg_window)
        spread_kf = jnp.zeros((past * rows + length, d_kf.shape[1]), BF)
        spread_kf = lax.dynamic_update_slice_in_dim(spread_kf, d_kf, block * rows, 0)[past * rows :]
        spread_kf = spread_kf.reshape(n_row, subs, rows, -1)
        own_kf = lax.psum_scatter(spread_kf, "row", scatter_dimension=0, tiled=False)
        own_kf = lax.psum_scatter(own_kf, "col", scatter_dimension=0, tiled=False, axis_index_groups=groups)
        gi_parts, g_rh = back(
            d_q, own_kf, head_fac, bq_rot, turn, w_rh, h_one, x_parts, gains, d_mixed, g_gain_two, n_row
        )
        output = lax.all_to_all(out_parts, "col", 0, 0, tiled=True)
        grad_input = lax.all_to_all(gi_parts, "col", 0, 0, tiled=True)
        g_ffn = lax.psum_scatter(g_ffn.reshape(3, n_row, part, D), "row", scatter_dimension=1, tiled=False)
        g_ffn = jnp.transpose(lax.psum(g_ffn, "dp").reshape(3, part, n_col, feat), (2, 0, 1, 3))
        g_ffn = lax.all_to_all(g_ffn, "col", 0, 0, tiled=True)
        g_ffn = jnp.transpose(g_ffn, (1, 0, 2, 3)).reshape(3, ffn_local, feat).astype(F32)

        def total(values):
            values = values.reshape((n_row * n_col,) + values.shape[2:])
            values = lax.psum_scatter(values, ("row", "col"), scatter_dimension=0, tiled=False)
            return lax.psum(values, "dp").astype(F32)

        g_out = total(g_out)
        g_rh = total(g_rh)

    used = rank_local + FAC * head_local
    own_heads = g_rh[rank_local:used].reshape(FAC, head_local, feat)
    own_heads = jnp.transpose(own_heads[jnp.array(FAC_BACK)], (2, 1, 0)).reshape(w_heads.shape)
    return (
        output.reshape(tokens_in.shape),
        grad_input.reshape(tokens_in.shape),
        g_rh[used],
        g_rh[used + 1],
        own_heads,
        g_rh[:rank_local].T,
        g_out,
        g_ffn[0].T,
        g_ffn[1].T,
        g_ffn[2],
    )


def solution(mesh):
    tokens = P(None, ("dp", "row"), "col")
    both = P("col", "row")
    turned = P("row", "col")
    gain = P("col")
    return jax.shard_map(
        local,
        mesh=mesh,
        in_specs=(tokens, P(None, "dp", None), gain, gain, both, both, turned, both, both, turned, tokens),
        out_specs=(tokens, tokens, gain, gain, both, both, turned, both, both, turned),
        check_vma=False,
    )
```

time: 661 us -> 354 us (0.54)
  waiting for transfers between devices: 397 us -> 1.27 us
  Pallas kernels: 100 us -> 318 us
  blocking collectives: 95.6 us -> 0 us
  local copies, waits for them, and re-layouts: 29.7 us -> 13.4 us
  starting transfers between devices: 11.5 us -> 0.08 us
    reduce_scatter x4 -> x1, waiting for transfers between devices: 301 us -> 1.22 us  [local(): lax.psum_scatter(g_out.reshape((n_row * n_col,) + w_out.shape), ('row', '...]
    pallas_call x4 -> x11, Pallas kernels: 95.2 us -> 312 us  [the longest x1 45.8 us: unmix(): pl.pallas_call(unmix_square_body, out_shape=tuple(outs) + (jax.ShapeDtype...]
    all_gather x3 -> x1, waiting for transfers between devices: 95.4 us -> 0.02 us  [local(): lax.all_gather(w_out, ('row', 'col'), axis=0)]
    psum x1 -> x0, blocking collectives: 46.8 us -> none  [local(): gains = lax.psum(gains, ('dp', 'row', 'col'))]
    all_gather x3 -> x0, blocking collectives: 37.5 us -> none  [the longest x1 19.3 us: local(): gathered = lax.all_gather(key_fac, 'row', axis=0)]
    all_to_all x1 -> x0, blocking collectives: 11.4 us -> none  [local(): lax.all_to_all(out_parts, 'col', 0, 0, tiled=True).reshape(tokens_in.shape)]
    all_to_all x3 -> x0, starting transfers between devices: 11.2 us -> none  [the longest x2 7.7 us: own_tokens(): lax.all_to_all(values.reshape(n_col, rows, feat), 'col', 0, 0, tiled=True)]
    slice x9 -> x3, local copies, waits for them, and re-layouts: 10.9 us -> 3.51 us  [the longest x1 1.38 us: local(): g_ffn[2]]
  transfers between devices with their start and end apart: 11 -> 2, of which waited for: 6 -> 1; matrix products, arithmetic and copies ran while one was open for 3% -> 1% of each run, Pallas kernels for 4% -> 41%
where the time goes in v3:
time: 354 us; the launch traced here: 353 us
  Pallas kernels  318 us (90%)
  between operations  14.4 us (4%)
  local copies, waits for them, and re-layouts  13.4 us (4%)
  other arithmetic  6.33 us (2%)
    pallas_call x1, Pallas kernels, unmix(): pl.pallas_call(unmix_square_body, out_shape=tuple(outs) + (jax.ShapeDtype...  45.8 us
    pallas_call x1, Pallas kernels, attend(): pl.pallas_call(functools.partial(attend_body, fast), out_shape=tuple(outs...  40.9 us
    pallas_call x1, Pallas kernels, attend_back(): pl.pallas_call(functools.partial(attend_back_body, fast), out_shape=tuple...  38 us
    pallas_call x1, Pallas kernels, window(): pl.pallas_call(functools.partial(window_body, n_row), out_shape=jax.Shape...  34.9 us
    pallas_call x1, Pallas kernels, finish(): pl.pallas_call(finish_body, out_shape=(jax.ShapeDtypeStruct(block, F32),...  30.6 us
    pallas_call x1, Pallas kernels, start(): pl.pallas_call(start_body, out_shape=(jax.ShapeDtypeStruct(tok.shape, tok...  30.6 us
    pallas_call x1, Pallas kernels, ffn_square(): pl.pallas_call(ffn_square_body, out_shape=(both, both, jax.ShapeDtypeStru...  26.2 us
    pallas_call x1, Pallas kernels, window_back(): pl.pallas_call(functools.partial(window_back_body, n_row), out_shape=jax....  24.3 us
  transfers between devices with their start and end apart: 2, of which 1 were waited for; matrix products, arithmetic and copies ran while one was open for 1% of the time, Pallas kernels for 41%

profile of v3, /device:TPU:0, one launch (start us, length us, event | category | flops | bytes accessed | tf_op | source)
XLA Modules:
  0.0 353.3 jit_solution(16423509571556632217)
XLA Ops:
  7.2 0.0 copy-start
  7.2 0.0 copy-start.6
  7.2 0.0 copy-start.8
  7.2 0.0 copy-start.7
  7.2 0.0 all-gather.3.cloned.1.call-start
  7.3 0.7 reshape.86
  8.0 0.7 pad_clamp_fusion.1
  8.7 0.6 gather_fusion
  9.3 1.2 fusion.4
  10.5 0.9 pad.5.ffn_ref
  11.3 0.1 pad.18.clone
  11.4 0.1 pad.15.clone
  11.5 0.7 maximum_maximum_fusion.w_ref
  12.3 0.7 maximum_maximum_fusion.1.gain_ref
  12.9 30.6 %shard_map.204 = (bf16[4,256,256]{2,1,0:T(8,128)(2,1)}, bf16[4,4,208,256]{3,2,1,0:T(8,128)(2,1)}, f32[4,8,256]{2,1,0:T(8,128)}, bf16[4,3,96,256]{3,2,1,0:T(8,128)(2,1)}) custom-call(bf16[4,256,256]{2,1,0:T(8,128)(2,1)} %bitcast.67, bf16[208,256]{1,0:T(8,128)(2,1)} %maximum_maximum_fusion.w_ref, f32[8,256]{1,0:T(8,128)} %maximum_maximum_fusion.1.gain_ref, ...), custom_call_target="tpu_custom_call" | custom-call | bytes 8388608 | tf_op jit(solution)/shard_map/pallas_call | solution.py:236
  43.5 0.0 all-gather.3.cloned.1.call-update
  43.5 0.0 reduce-scatter.2.cloned.1.call-start
  43.6 0.6 fusion.6
  44.3 0.4 convert_reduce_fusion
  44.7 0.5 multiply_sine_fusion
  45.2 1.0 concatenate.16.turn_ref
  46.2 5.4 %shard_map.205 = (bf16[256,1024]{1,0:T(8,128)(2,1)}, f32[256,192]{1,0:T(8,128)}, f32[256,384]{1,0:T(8,128)}, bf16[256,320]{1,0:T(8,128)(2,1)}, bf16[256,1024]{1,0:T(8,128)(2,1)}, /*index=5*/bf16[832,1024]{1,0:T(8,128)(2,1)}) custom-call(bf16[4,256,256]{2,1,0:T(8,128)(2,1)} %get-tuple-element.58.x_ref, f32[4,8,256]{2,1,0:T(8,128)} %get-tuple-element.59.gain_ref, ...), custom_call_target="tpu_custom_call" | custom-call | flops 1258291200 | bytes 6291456 | tf_op jit(solution)/shard_map/pallas_call | solution.py:731
  51.6 0.7 broadcast_in_dim.31.zero_ref
  52.3 34.9 %shard_map.206 = bf16[5,256,320]{2,1,0:T(8,128)(2,1)} custom-call(bf16[256,320]{1,0:T(8,128)(2,1)} %get-tuple-element.62.x_ref, bf16[256,320]{1,0:T(8,128)(2,1)} %broadcast_in_dim.31.zero_ref), custom_call_target="tpu_custom_call" | custom-call | bytes 1048576 | tf_op jit(solution)/shard_map/pallas_call | solution.py:594
  87.2 40.9 %shard_map.207 = (bf16[256,1024]{1,0:T(8,128)(2,1)}, f32[16,8,256]{2,1,0:T(8,128)}, bf16[1280,1024]{1,0:T(8,128)(2,1)}, bf16[1280,1024]{1,0:T(8,128)(2,1)}, bf16...) custom-call(bf16[256,1024]{1,0:T(8,128)(2,1)} %get-tuple-element.61.q_ref, bf16[1280,320]{1,0:T(8,128)(2,1)} %bitcast.60, ...), custom_call_target="tpu_custom_call" | custom-call | flops 10737418240 | bytes 16777216 | tf_op jit(solution)/shard_map/pallas_call | solution.py:832
  128.2 0.0 all-gather.3.cloned.1.call-done
  128.2 3.8 %shard_map.208 = (f32[256,1024]{1,0:T(8,128)}, bf16[256,1024]{1,0:T(8,128)(2,1)}) custom-call(bf16[4,256,256]{2,1,0:T(8,128)(2,1)} %get-tuple-element.58.x_ref, bf16[256,1024]{1,0:T(8,128)(2,1)} %get-tuple-element.66.heads_ref, bf16[4,4,256,256]{3,2,1,0:T(8,128)(2,1)} %bitcast.55, f32[4,8,256]{2,1,0:T(8,128)} %get-tuple-element.59.gain_ref), custom_call_target="tpu_custom_call" | custom-call | flops 536870912 | bytes 5242880 | tf_op jit(solution)/shard_map/pallas_call | solution.py:969
  132.0 21.7 %shard_map.209 = (bf16[4,256,1024]{2,1,0:T(8,128)(2,1)}, bf16[4,256,1024]{2,1,0:T(8,128)(2,1)}, bf16[4,1024,256]{2,1,0:T(8,128)(2,1)}, bf16[4,3,96,256]{3,2,1,0:T(8,128)(2,1)}) custom-call(bf16[256,1024]{1,0:T(8,128)(2,1)} %get-tuple-element.68.h_ref, bf16[4,1024,256]{2,1,0:T(8,128)(2,1)} %get-tuple-element.69.cot_ref.cot_near_ref, ...), custom_call_target="tpu_custom_call" | custom-call | bytes 12582912 | tf_op jit(solution)/shard_map/pallas_call | solution.py:406
  153.7 26.2 %shard_map.210 = (bf16[2,4,256,1024]{3,2,1,0:T(8,128)(2,1)}, bf16[2,4,256,1024]{3,2,1,0:T(8,128)(2,1)}, bf16[4,3,96,1024]{3,2,1,0:T(8,128)(2,1)}, bf16[256,1024]{1,0:T(8,128)(2,1)}) custom-call(bf16[4,256,1024]{2,1,0:T(8,128)(2,1)} %get-tuple-element.71.near_ref, bf16[4,256,1024]{2,1,0:T(8,128)(2,1)} %get-tuple-element.72.far_ref, ...), custom_call_target="tpu_custom_call" | custom-call | flops 14495514624 | bytes 25165824 | tf_op jit(solution)/shard_map/pallas_call | solution.py:1084
  180.0 45.8 %shard_map.211 = (bf16[4,256,256]{2,1,0:T(8,128)(2,1)}, f32[256,1024]{1,0:T(8,128)}, bf16[256,1024]{1,0:T(8,128)(2,1)}, bf16[4,4,256,256]{3,2,1,0:T(8,128)(2,1)}...) custom-call(bf16[2,4,256,1024]{3,2,1,0:T(8,128)(2,1)} %get-tuple-element.75.dh_ref, ...), custom_call_target="tpu_custom_call" | custom-call | flops 1073741824 | bytes 18874368 | tf_op jit(solution)/shard_map/pallas_call | solution.py:1200
  225.8 0.0 copy-start.9
  225.8 0.0 reduce-scatter.2.cloned.1.call-update
  225.8 0.6 copy-done.9
  226.4 38.0 %shard_map.212 = (f32[256,1024]{1,0:T(8,128)}, bf16[1280,320]{1,0:T(8,128)(2,1)}, bf16[4,256,256]{2,1,0:T(8,128)(2,1)}, bf16[2,3,96,1024]{3,2,1,0:T(8,128)(2,1)}) custom-call(bf16[256,1024]{1,0:T(8,128)(2,1)} %get-tuple-element.61.q_ref, bf16[1280,1024]{1,0:T(8,128)(2,1)} %get-tuple-element.64.k_ref, bf16[1280,1024]{1,0:T(8,128)(2,1)} %get-tuple-element.65.v_ref, ...), custom_call_target="tpu_custom_call" | custom-call | flops 26843545600 | bytes 16777216 | tf_op jit(solution)/shard_map/pallas_call | solution.py:937
  264.4 24.3 %shard_map.213.dkf_ref = f32[256,320]{1,0:T(8,128)} custom-call(bf16[5,256,320]{2,1,0:T(8,128)(2,1)} %bitcast.62), custom_call_target="tpu_custom_call" | custom-call | bytes 1048576 | tf_op jit(solution)/shard_map/pallas_call | solution.py:664
  288.8 1.2 reduce-scatter.2.cloned.1.call-done
  290.0 15.6 %shard_map.214 = (f32[4,256,256]{2,1,0:T(8,128)}, bf16[4,4,208,256]{3,2,1,0:T(8,128)(2,1)}, bf16[4,3,96,256]{3,2,1,0:T(8,128)(2,1)}) custom-call(f32[256,1024]{1,0:T(8,128)} %get-tuple-element.84.dq_ref, f32[256,320]{1,0:T(8,128)} %shard_map.213.dkf_ref, f32[256,192]{1,0:T(8,128)} %get-tuple-element.88.hf_ref, f32[256,384]{1,0:T(8,128)} %get-tuple-element.89.bq_ref, ...), custom_call_target="tpu_custom_call" | custom-call | flops 2516582400 | bytes 12582912 | tf_op jit(solution)/shard_map/pallas_call | solution.py:1333
  305.6 30.6 %shard_map.215 = (f32[208,256]{1,0:T(8,128)}, f32[4,256,256]{2,1,0:T(8,128)}, bf16[4,3,96,256]{3,2,1,0:T(8,128)(2,1)}, bf16[256,256]{1,0:T(8,128)(2,1)}) custom-call(bf16[4,4,208,256]{3,2,1,0:T(8,128)(2,1)} %get-tuple-element.96.g_ref, f32[4,256,256]{2,1,0:T(8,128)} %get-tuple-element.97.gi_ref, bf16[4,3,96,256]{3,2,1,0:T(8,128)(2,1)} %get-tuple-element.98.cols_ref, ...), custom_call_target="tpu_custom_call" | custom-call | bytes 10485760 | tf_op jit(solution)/shard_map/pallas_call | solution.py:1409
  336.2 0.8 slice.33
  337.0 1.6 slice_bitcast_fusion
  338.6 1.3 fusion.8
  339.9 1.4 convert_bitcast_fusion
  341.4 1.4 fusion.7
  342.8 0.7 convert_add_fusion
  343.5 0.6 gather_fusion.1
  344.1 0.6 reshape.96
  344.7 0.8 copy.51
  345.5 1.0 copy.52
  (26 shorter events, 0.1 us)
Async XLA Ops:
  7.2 36.4 %copy-start = (s32[2,1,2048]{2,1,0:T(1,128)S(1)}, s32[2,1,2048]{2,1,0:T(1,128)}, u32[]{:S(2)}) copy-start(s32[2,1,2048]{2,1,0:T(1,128)} %param.14) | copy-start | bytes 49156
  7.2 4.3 %copy-start.6 = (bf16[256,160]{0,1:T(8,128)(2,1)S(1)}, bf16[256,160]{0,1:T(8,128)(2,1)}, u32[]{:S(2)}) copy-start(bf16[256,160]{0,1:T(8,128)(2,1)} %param.18) | copy-start | bytes 245764
  7.2 5.0 %copy-start.8 = (f32[256]{0:T(256)S(1)}, f32[256]{0:T(256)}, u32[]{:S(2)}) copy-start(f32[256]{0:T(256)} %param.15) | copy-start | bytes 3076
  7.2 5.0 %copy-start.7 = (f32[256]{0:T(256)S(1)}, f32[256]{0:T(256)}, u32[]{:S(2)}) copy-start(f32[256]{0:T(256)} %param.16) | copy-start | bytes 3076
  7.2 121.0 %all-gather.3.cloned.1.call-start = ((), (), s32[]{:S(2)}) async-start(), calls=%async_computation.2 | async-start | bytes 2228224 | tf_op jit(solution)/shard_map/all_gather | solution.py:1483
  43.5 246.5 %reduce-scatter.2.cloned.1.call-start = ((), (), s32[]{:S(2)}) async-start(), calls=%async_computation.1 | async-start | bytes 2228224 | tf_op jit(solution)/shard_map/reduce_scatter | solution.py:1518
  225.8 0.7 copy-start.9
  305.6 34.3 %copy-start.1 = (bf16[4,3,96,256]{3,2,1,0:T(8,128)(2,1)S(1)}, bf16[4,3,96,256]{3,2,1,0:T(8,128)(2,1)}, u32[]{:S(2)}) copy-start(bf16[4,3,96,256]{3,2,1,0:T(8,128)(2,1)} %get-tuple-element.98.cols_ref) | copy-start | bytes 1769476
  341.3 1.4 copy-start.4
  341.3 1.4 copy-start.5
  341.3 3.4 copy-start.3
  341.4 4.2 %copy-start.2 = (f32[4,256,256]{2,1,0:T(8,128)S(1)}, f32[4,256,256]{2,1,0:T(8,128)}, u32[]{:S(2)}) copy-start(f32[4,256,256]{2,1,0:T(8,128)} %get-tuple-element.100) | copy-start | bytes 3145732
Sparse Core Ops, SparseCore 0:
  43.6 48.4 all-gather.2
  225.9 63.9 reduce-scatter.1
